TPU v7x, 32 devices: a whole 2x2x4 slice. The times are simulated.
32 devices in a mesh: wide: 8 (over z, x), narrow: 4 (over y, core).
Axes of the slice: x: 2, y: 2, z: 4, core: 2. Of those that a mesh axis runs over, the one named last changes fastest.
Arguments:
- tokens: bfloat16 [32768, 384], P(('wide', 'narrow')), may hold values from -6 to 6
- conditions: bfloat16 [128, 384], P(('wide', 'narrow')), may hold values from -6 to 6
- routes: int32 [32768, 2], P(('wide', 'narrow')), may hold values from 0 to 7, all different within a row; in each aligned block of 1024 rows (0 to 1023, 1024 to 2047, ...) at most 384 rows name the same one
- resolution: int32 [32], P(('wide', 'narrow')), may hold values from 0 to 1
- step_count: int32 [1], replicated, may hold values from 1 to 20
- cotangent: bfloat16 [32768, 384], P(('wide', 'narrow')), may hold values from -6 to 6
- w_square: float32 [9, 384, 384], P(None, 'narrow', 'wide'), may hold values from -0.3125 to 0.3125
- w_out: float32 [384, 384], P('narrow', 'wide'), may hold values from -0.875 to 0.875
- w_router: float32 [8, 384], P('narrow', 'wide'), may hold values from -0.21875 to 0.21875
- w_up: float32 [10, 1536, 384], P(None, 'narrow', 'wide'), may hold values from -0.3125 to 0.3125
- w_down: float32 [10, 1536, 384], P(None, 'narrow', 'wide'), may hold values from -0.15625 to 0.15625
- b_ada: float32 [2304], P(('wide', 'narrow')), may hold values from -1.2 to 1.2
- moment_square: float32 [9, 384, 384], P(None, 'narrow', 'wide'), may hold values from -112 to 112
- moment_out: float32 [384, 384], P('narrow', 'wide'), may hold values from -112 to 112
- moment_router: float32 [8, 384], P('narrow', 'wide'), may hold values from -56 to 56
- moment_up: float32 [10, 1536, 384], P(None, 'narrow', 'wide'), may hold values from -56 to 56
- moment_down: float32 [10, 1536, 384], P(None, 'narrow', 'wide'), may hold values from -112 to 112
- moment_bias: float32 [2304], P(('wide', 'narrow')), may hold values from -512 to 512
- ema_square: float32 [9, 384, 384], P(None, 'narrow', 'wide'), may hold values from -0.3125 to 0.3125
- ema_out: float32 [384, 384], P('narrow', 'wide'), may hold values from -0.875 to 0.875
- ema_router: float32 [8, 384], P('narrow', 'wide'), may hold values from -0.21875 to 0.21875
- ema_up: float32 [10, 1536, 384], P(None, 'narrow', 'wide'), may hold values from -0.3125 to 0.3125
- ema_down: float32 [10, 1536, 384], P(None, 'narrow', 'wide'), may hold values from -0.15625 to 0.15625
- ema_bias: float32 [2304], P(('wide', 'narrow')), may hold values from -1.2 to 1.2
Outputs:
- output: bfloat16 [32768, 384], P(('wide', 'narrow'))
- grad_in: float32 [32768, 384], P(('wide', 'narrow'))
- state_square: float32 [9, 384, 384], P(None, 'narrow', 'wide')
- master_square: float32 [9, 384, 384], P(None, 'narrow', 'wide')
- average_square: float32 [9, 384, 384], P(None, 'narrow', 'wide')
- state_out: float32 [384, 384], P('narrow', 'wide')
- master_out: float32 [384, 384], P('narrow', 'wide')
- average_out: float32 [384, 384], P('narrow', 'wide')
- state_router: float32 [8, 384], P('narrow', 'wide')
- master_router: float32 [8, 384], P('narrow', 'wide')
- average_router: float32 [8, 384], P('narrow', 'wide')
- state_up: float32 [10, 1536, 384], P(None, 'narrow', 'wide')
- master_up: float32 [10, 1536, 384], P(None, 'narrow', 'wide')
- average_up: float32 [10, 1536, 384], P(None, 'narrow', 'wide')
- state_down: float32 [10, 1536, 384], P(None, 'narrow', 'wide')
- master_down: float32 [10, 1536, 384], P(None, 'narrow', 'wide')
- average_down: float32 [10, 1536, 384], P(None, 'narrow', 'wide')
- state_bias: float32 [2304], P(('wide', 'narrow'))
- master_bias: float32 [2304], P(('wide', 'narrow'))
- average_bias: float32 [2304], P(('wide', 'narrow'))
Inputs may be any that keep to these rules, and one draw needn't show every extreme that they name: `routes`: the 2 experts of a row differ. In the rows of one device no expert is named by more than 384 rows, a bound that some block reaches. `resolution`: 1 marks a device whose tokens are images of 1024 consecutive rows, 0 one whose tokens are images of 256 consecutive rows.
All inputs are finite; a program needn't handle non-finite values.
Results may differ from a plain program's by a relative error of at most 0.02.
The roundings to bfloat16 on the way count: a program that leaves them out, or rounds other values in their place, can miss the bound.
Values may be sent and summed in bfloat16 or wider, within the bound.
No kernel may reach another device: no remote copies, remote signals or barrier semaphores. Data moves between devices by JAX's collectives and lax.ppermute only.
A program may use at most 256 MiB of HBM per device.

v0:
```python
from functools import partial

import jax
import jax.numpy as jnp
from jax import lax
from jax.sharding import PartitionSpec as P

D = 384
HEADS = 6
HEAD = 64
FF = 1536
TOP = 2
ROUTED = 8
SHORT = 256
LONG = 1024
CAP = 384


PRECISE = lax.Precision.HIGHEST
EPSILON = 1e-06
NS_FIRST = 3.4445
NS_SECOND = -4.775
NS_THIRD = 2.0315
MOMENTUM = 0.95
MOMENTUM_VECTOR = 0.5
RATE = 0.25
RATE_VECTOR = 0.05


def as_sent(array):

    def short(part):
        return part.astype(jnp.bfloat16) if part.dtype == jnp.float32 else part

    return jax.tree.map(short, array)


def modulate(seg_rows, shift_by, scale_by):
    center = seg_rows - jnp.mean(seg_rows, axis=-1, keepdims=True)
    normed = center * lax.rsqrt(jnp.mean(center * center, axis=-1, keepdims=True) + EPSILON)
    return normed * (1.0 + scale_by) + shift_by


def gelu_tanh(values):
    return jax.nn.gelu(values, approximate=True)


def gelu_grad(pre_act, upstream):
    _, pull_back = jax.vjp(gelu_tanh, pre_act)
    return pull_back(upstream)[0]


def slot_table(route_rows):
    flat_routes = route_rows.reshape(-1)
    hot_table = (flat_routes[:, None] == jnp.arange(ROUTED, dtype=jnp.int32)[None, :]).astype(
        jnp.int32
    )
    earlier = jnp.cumsum(hot_table, axis=0, dtype=jnp.int32) - hot_table
    place_in = jnp.sum(earlier * hot_table, axis=1, dtype=jnp.int32)
    slot_ids = flat_routes * CAP + place_in
    sources = jnp.arange(slot_ids.shape[0], dtype=jnp.int32) // TOP
    slot_owner = jnp.zeros((ROUTED * CAP,), jnp.int32).at[slot_ids].set(sources)
    return (slot_ids, slot_owner)


def attend(projected, length):
    image_count = projected.shape[1] // length
    split_parts = projected.reshape(3, image_count, length, HEADS, HEAD)
    scores = jnp.einsum(
        "bqhe,bkhe->bhqk", split_parts[0], split_parts[1], preferred_element_type=jnp.float32
    ) * HEAD ** (-0.5)
    highest = jnp.max(scores, axis=-1, keepdims=True)
    expo = jnp.exp(scores - highest)
    totals = jnp.sum(expo, axis=-1, keepdims=True)
    weights_low = (expo / totals).astype(jnp.bfloat16)
    mixed_heads = jnp.einsum(
        "bhqk,bkhe->bqhe", weights_low, split_parts[2], preferred_element_type=jnp.float32
    )
    log_total = (highest + jnp.log(totals))[..., 0]
    return (
        mixed_heads.reshape(-1, D).astype(jnp.bfloat16),
        jnp.transpose(log_total, (0, 2, 1)).reshape(-1, HEADS),
    )


def attend_back(projected, log_total, d_attended, length):
    image_count = projected.shape[1] // length
    split_parts = projected.reshape(3, image_count, length, HEADS, HEAD)
    scale_qk = HEAD ** (-0.5)
    scores = (
        jnp.einsum(
            "bqhe,bkhe->bhqk", split_parts[0], split_parts[1], preferred_element_type=jnp.float32
        )
        * scale_qk
    )
    log_four = jnp.transpose(log_total.reshape(image_count, length, HEADS), (0, 2, 1))[..., None]
    probs = jnp.exp(scores - log_four)
    weights_low = probs.astype(jnp.bfloat16)
    d_heads = d_attended.reshape(image_count, length, HEADS, HEAD)
    d_weights = jnp.einsum(
        "bqhe,bkhe->bhqk", d_heads, split_parts[2], preferred_element_type=jnp.float32
    )
    d_values = jnp.einsum(
        "bhqk,bqhe->bkhe", weights_low, d_heads, preferred_element_type=jnp.float32
    )
    d_scores = (probs * (d_weights - jnp.sum(d_weights * probs, axis=-1, keepdims=True))).astype(
        jnp.bfloat16
    )
    d_queries = (
        jnp.einsum("bhqk,bkhe->bqhe", d_scores, split_parts[1], preferred_element_type=jnp.float32)
        * scale_qk
    )
    d_keys = (
        jnp.einsum("bhqk,bqhe->bkhe", d_scores, split_parts[0], preferred_element_type=jnp.float32)
        * scale_qk
    )
    return jnp.stack([d_queries, d_keys, d_values]).reshape(3, -1, D).astype(jnp.bfloat16)


def on_device(
    tokens,
    conditions,
    routes,
    resolution,
    step_count,
    cotangent,
    w_square,
    w_out,
    w_router,
    w_up,
    w_down,
    b_ada,
    moment_square,
    moment_out,
    moment_router,
    moment_up,
    moment_down,
    moment_bias,
    ema_square,
    ema_out,
    ema_router,
    ema_up,
    ema_down,
    ema_bias,
):
    bf_type = jnp.bfloat16
    fl_type = jnp.float32
    row_pieces = (
        lax.all_gather(w_square.astype(bf_type), "narrow", axis=1, tiled=True),
        lax.all_gather(w_out.astype(bf_type), "narrow", axis=0, tiled=True),
        lax.all_gather(w_router.astype(bf_type), "narrow", axis=0, tiled=True),
        lax.all_gather(w_up.astype(bf_type), "narrow", axis=1, tiled=True),
        lax.all_gather(w_down.astype(bf_type), "narrow", axis=1, tiled=True),
        lax.all_gather(b_ada.astype(bf_type), "narrow", axis=0, tiled=True),
    )
    whole_low = (
        lax.all_gather(row_pieces[0], "wide", axis=2, tiled=True),
        lax.all_gather(row_pieces[1], "wide", axis=1, tiled=True),
        lax.all_gather(row_pieces[2], "wide", axis=1, tiled=True),
        lax.all_gather(row_pieces[3], "wide", axis=2, tiled=True),
        lax.all_gather(row_pieces[4], "wide", axis=2, tiled=True),
        lax.all_gather(row_pieces[5], "wide", axis=0, tiled=True),
    )
    square_low, out_low, router_low, up_low, down_low, bias_low = whole_low
    res_group = resolution[0]
    token_f = tokens.astype(fl_type)
    segments = tokens.shape[0] // SHORT
    seg_ratio = LONG // SHORT
    first_seg = jnp.arange(segments, dtype=jnp.int32) // seg_ratio * seg_ratio
    chosen = jnp.where(res_group == 1, conditions[first_seg], conditions)
    cond_low = jax.nn.silu(chosen.astype(fl_type)).astype(bf_type)
    modulation = jnp.einsum(
        "sd,jde->sje", cond_low, square_low[3:], preferred_element_type=fl_type
    ) + bias_low.astype(fl_type).reshape(6, D)
    seg_rows = token_f.reshape(segments, SHORT, D)
    first_mod, first_back = jax.vjp(modulate, seg_rows, modulation[:, 0:1], modulation[:, 1:2])
    hidden_one = first_mod.reshape(-1, D).astype(bf_type)
    projected = jnp.einsum(
        "td,jde->jte", hidden_one, square_low[:3], preferred_element_type=fl_type
    ).astype(bf_type)
    attended, log_total = lax.cond(
        res_group == 1, partial(attend, length=LONG), partial(attend, length=SHORT), projected
    )
    attn_out = jnp.dot(attended, out_low, preferred_element_type=fl_type)
    mid_state = token_f + (attn_out.reshape(segments, SHORT, D) * modulation[:, 2:3]).reshape(-1, D)
    second_mod, second_back = jax.vjp(
        modulate, mid_state.reshape(segments, SHORT, D), modulation[:, 3:4], modulation[:, 4:5]
    )
    hidden_two = second_mod.reshape(-1, D).astype(bf_type)
    logits = jnp.einsum("td,rd->tr", hidden_two, router_low, preferred_element_type=fl_type)
    gate_probs = jax.nn.softmax(jnp.take_along_axis(logits, routes, axis=1), axis=1)
    slot_ids, slot_owner = slot_table(routes)
    inputs = hidden_two[slot_owner].reshape(ROUTED, CAP, D)
    pre_act = jnp.einsum("ecd,efd->ecf", inputs, up_low[:ROUTED], preferred_element_type=fl_type)
    act_low = gelu_tanh(pre_act).astype(bf_type)
    produced = jnp.einsum(
        "ecf,efd->ecd", act_low, down_low[:ROUTED], preferred_element_type=fl_type
    ).reshape(-1, D)
    chosen_out = produced[slot_ids].reshape(-1, TOP, D)
    routed = jnp.sum(chosen_out * gate_probs[:, :, None], axis=1)
    shared_pre = jnp.einsum(
        "td,sfd->stf", hidden_two, up_low[ROUTED:], preferred_element_type=fl_type
    )
    shared_act = gelu_tanh(shared_pre).astype(bf_type)
    shared_out = jnp.einsum(
        "stf,sfd->std", shared_act, down_low[ROUTED:], preferred_element_type=fl_type
    )
    mixture = routed + jnp.sum(shared_out, axis=0)
    output = (
        mid_state + (mixture.reshape(segments, SHORT, D) * modulation[:, 5:6]).reshape(-1, D)
    ).astype(bf_type)
    again_rows = (
        lax.all_gather(w_square.astype(bf_type), "narrow", axis=1, tiled=True),
        lax.all_gather(w_out.astype(bf_type), "narrow", axis=0, tiled=True),
        lax.all_gather(w_router.astype(bf_type), "narrow", axis=0, tiled=True),
        lax.all_gather(w_up.astype(bf_type), "narrow", axis=1, tiled=True),
        lax.all_gather(w_down.astype(bf_type), "narrow", axis=1, tiled=True),
    )
    again_whole = (
        lax.all_gather(again_rows[0], "wide", axis=2, tiled=True),
        lax.all_gather(again_rows[1], "wide", axis=1, tiled=True),
        lax.all_gather(again_rows[2], "wide", axis=1, tiled=True),
        lax.all_gather(again_rows[3], "wide", axis=2, tiled=True),
        lax.all_gather(again_rows[4], "wide", axis=2, tiled=True),
    )
    square_low, out_low, router_low, up_low, down_low = again_whole
    grad_out = cotangent.astype(fl_type)
    grad_seg = grad_out.reshape(segments, SHORT, D)
    d_gate_two = jnp.sum(grad_seg * mixture.reshape(segments, SHORT, D), axis=1)
    d_mixture = (grad_seg * modulation[:, 5:6]).reshape(-1, D)
    d_shared = d_mixture.astype(bf_type)
    d_shared_act = jnp.einsum(
        "td,sfd->stf", d_shared, down_low[ROUTED:], preferred_element_type=fl_type
    )
    d_shared_pre = gelu_grad(shared_pre, d_shared_act).astype(bf_type)
    g_shared_down = jnp.einsum("stf,td->sfd", shared_act, d_shared, preferred_element_type=fl_type)
    g_shared_up = jnp.einsum(
        "stf,td->sfd", d_shared_pre, hidden_two, preferred_element_type=fl_type
    )
    d_hidden = jnp.einsum(
        "stf,sfd->td", d_shared_pre, up_low[ROUTED:], preferred_element_type=fl_type
    )
    d_gates = jnp.sum(d_mixture[:, None, :] * chosen_out, axis=2)
    gate_slot = jnp.zeros((ROUTED * CAP,), fl_type).at[slot_ids].set(gate_probs.reshape(-1))
    d_produced = (
        (gate_slot[:, None] * d_mixture[slot_owner]).astype(bf_type).reshape(ROUTED, CAP, D)
    )
    d_act = jnp.einsum(
        "ecd,efd->ecf", d_produced, down_low[:ROUTED], preferred_element_type=fl_type
    )
    d_pre = gelu_grad(pre_act, d_act).astype(bf_type)
    g_routed_down = jnp.einsum("ecf,ecd->efd", act_low, d_produced, preferred_element_type=fl_type)
    g_routed_up = jnp.einsum("ecf,ecd->efd", d_pre, inputs, preferred_element_type=fl_type)
    d_inputs = jnp.einsum(
        "ecf,efd->ecd", d_pre, up_low[:ROUTED], preferred_element_type=fl_type
    ).reshape(-1, D)
    d_hidden = d_hidden + jnp.sum(d_inputs[slot_ids].reshape(-1, TOP, D), axis=1)
    d_picked = gate_probs * (d_gates - jnp.sum(gate_probs * d_gates, axis=1, keepdims=True))
    route_hot = (routes[:, :, None] == jnp.arange(ROUTED, dtype=jnp.int32)[None, None, :]).astype(
        fl_type
    )
    d_logits = jnp.sum(route_hot * d_picked[:, :, None], axis=1).astype(bf_type)
    g_router = jnp.einsum("tr,td->rd", d_logits, hidden_two, preferred_element_type=fl_type)
    d_hidden = d_hidden + jnp.einsum(
        "tr,rd->td", d_logits, router_low, preferred_element_type=fl_type
    )
    d_mid_norm, d_shift_two, d_scale_two = second_back(d_hidden.reshape(segments, SHORT, D))
    d_mid = grad_out + d_mid_norm.reshape(-1, D)
    d_gate_one = jnp.sum(
        d_mid.reshape(segments, SHORT, D) * attn_out.reshape(segments, SHORT, D), axis=1
    )
    d_attn = (d_mid.reshape(segments, SHORT, D) * modulation[:, 2:3]).reshape(-1, D).astype(bf_type)
    g_out = jnp.einsum("td,te->de", attended, d_attn, preferred_element_type=fl_type)
    d_attended = jnp.einsum("te,de->td", d_attn, out_low, preferred_element_type=fl_type).astype(
        bf_type
    )
    d_projected = lax.cond(
        res_group == 1,
        partial(attend_back, length=LONG),
        partial(attend_back, length=SHORT),
        projected,
        log_total,
        d_attended,
    )
    g_qkv = jnp.einsum("td,jte->jde", hidden_one, d_projected, preferred_element_type=fl_type)
    d_hidden_one = jnp.einsum(
        "jte,jde->td", d_projected, square_low[:3], preferred_element_type=fl_type
    )
    d_rows, d_shift_one, d_scale_one = first_back(d_hidden_one.reshape(segments, SHORT, D))
    grad_in = d_mid + d_rows.reshape(-1, D)
    d_modulation = jnp.stack(
        [
            d_shift_one[:, 0],
            d_scale_one[:, 0],
            d_gate_one,
            d_shift_two[:, 0],
            d_scale_two[:, 0],
            d_gate_two,
        ],
        axis=1,
    )
    g_ada = jnp.einsum("sd,sje->jde", cond_low.astype(fl_type), d_modulation, precision=PRECISE)
    g_bias = jnp.sum(d_modulation, axis=0).reshape(-1)
    g_square = jnp.concatenate([g_qkv, g_ada], axis=0)
    g_up = jnp.concatenate([g_routed_up, g_shared_up], axis=0)
    g_down = jnp.concatenate([g_routed_down, g_shared_down], axis=0)
    by_columns = (
        lax.psum_scatter(g_square, "wide", scatter_dimension=2, tiled=True),
        lax.psum_scatter(g_out, "wide", scatter_dimension=1, tiled=True),
        lax.psum_scatter(g_router, "wide", scatter_dimension=1, tiled=True),
        lax.psum_scatter(g_up, "wide", scatter_dimension=2, tiled=True),
        lax.psum_scatter(g_down, "wide", scatter_dimension=2, tiled=True),
        lax.psum_scatter(g_bias, "wide", scatter_dimension=0, tiled=True),
    )
    summed = (
        lax.psum_scatter(by_columns[0], "narrow", scatter_dimension=1, tiled=True),
        lax.psum_scatter(by_columns[1], "narrow", scatter_dimension=0, tiled=True),
        lax.psum_scatter(by_columns[2], "narrow", scatter_dimension=0, tiled=True),
        lax.psum_scatter(by_columns[3], "narrow", scatter_dimension=1, tiled=True),
        lax.psum_scatter(by_columns[4], "narrow", scatter_dimension=1, tiled=True),
        lax.psum_scatter(by_columns[5], "narrow", scatter_dimension=0, tiled=True),
    )
    state_square = MOMENTUM * moment_square + summed[0]
    state_out = MOMENTUM * moment_out + summed[1]
    state_router = MOMENTUM * moment_router + summed[2]
    state_up = MOMENTUM * moment_up + summed[3]
    state_down = MOMENTUM * moment_down + summed[4]
    local_rows = w_up.shape[1]

    def padded(block):
        return jnp.pad(block, ((0, 0), (0, local_rows - block.shape[1]), (0, 0)))

    stacked = jnp.concatenate(
        [
            padded(state_square),
            padded(state_out[None]),
            padded(state_router[None]),
            state_up,
            state_down,
        ],
        axis=0,
    )
    wide_count = lax.axis_size("wide")
    matrices = stacked.shape[0]
    per_owner = -(-matrices // wide_count)
    stacked = jnp.pad(stacked, ((0, per_owner * wide_count - matrices), (0, 0), (0, 0)))
    current = lax.all_to_all(stacked, "wide", split_axis=0, concat_axis=2, tiled=True)
    for sweep_num in range(5):
        gram_mat = lax.psum(
            jnp.einsum("mrc,mrd->mcd", current, current, precision=PRECISE).astype(jnp.bfloat16),
            "narrow",
        ).astype(jnp.float32)
        if sweep_num == 0:
            factor = 1.0 / (jnp.sqrt(jnp.trace(gram_mat, axis1=1, axis2=2)) + 1e-07)
            current = current * factor[:, None, None]
            gram_mat = gram_mat * (factor * factor)[:, None, None]
        polynomial = NS_SECOND * gram_mat + NS_THIRD * jnp.einsum(
            "mcd,mde->mce", gram_mat, gram_mat, precision=PRECISE
        )
        current = NS_FIRST * current + jnp.einsum(
            "mrc,mcd->mrd", current, polynomial, precision=PRECISE
        )
    spread_back = lax.all_to_all(
        as_sent(current), "wide", split_axis=2, concat_axis=0, tiled=True
    ).astype(current.dtype)[:matrices]
    expert_total = w_up.shape[0]
    small_factor = RATE * 0.2 * D**0.5
    large_factor = RATE * 0.2 * FF**0.5
    master_square = w_square - small_factor * spread_back[0:9, : w_square.shape[1]]
    master_out = w_out - small_factor * spread_back[9, : w_out.shape[0]]
    master_router = w_router - small_factor * spread_back[10, : w_router.shape[0]]
    master_up = w_up - large_factor * spread_back[11 : 11 + expert_total]
    master_down = w_down - large_factor * spread_back[11 + expert_total : 11 + 2 * expert_total]
    state_bias = MOMENTUM_VECTOR * moment_bias + summed[5]
    square_total = lax.psum(jnp.sum(state_bias * state_bias), ("wide", "narrow"))
    root_mean = jnp.sqrt(square_total / (6 * D) + 1e-05)
    master_bias = b_ada - RATE_VECTOR * state_bias / root_mean
    step_value = step_count[0].astype(fl_type)
    decay = jnp.minimum(0.9999, (1.0 + step_value) / (10.0 + step_value))
    average_square = decay * ema_square + (1.0 - decay) * master_square
    average_out = decay * ema_out + (1.0 - decay) * master_out
    average_router = decay * ema_router + (1.0 - decay) * master_router
    average_up = decay * ema_up + (1.0 - decay) * master_up
    average_down = decay * ema_down + (1.0 - decay) * master_down
    average_bias = decay * ema_bias + (1.0 - decay) * master_bias
    return (
        output,
        grad_in,
        state_square,
        master_square,
        average_square,
        state_out,
        master_out,
        average_out,
        state_router,
        master_router,
        average_router,
        state_up,
        master_up,
        average_up,
        state_down,
        master_down,
        average_down,
        state_bias,
        master_bias,
        average_bias,
    )


def solution(mesh):
    placed = (
        P(("wide", "narrow"), None),
        P(("wide", "narrow"), None),
        P(("wide", "narrow"), None),
        P(("wide", "narrow")),
        P(),
        P(("wide", "narrow"), None),
        P(None, "narrow", "wide"),
        P("narrow", "wide"),
        P("narrow", "wide"),
        P(None, "narrow", "wide"),
        P(None, "narrow", "wide"),
        P(("wide", "narrow")),
        P(None, "narrow", "wide"),
        P("narrow", "wide"),
        P("narrow", "wide"),
        P(None, "narrow", "wide"),
        P(None, "narrow", "wide"),
        P(("wide", "narrow")),
        P(None, "narrow", "wide"),
        P("narrow", "wide"),
        P("narrow", "wide"),
        P(None, "narrow", "wide"),
        P(None, "narrow", "wide"),
        P(("wide", "narrow")),
    )
    return jax.shard_map(
        on_device,
        mesh=mesh,
        in_specs=placed,
        out_specs=(
            P(("wide", "narrow"), None),
            P(("wide", "narrow"), None),
            P(None, "narrow", "wide"),
            P(None, "narrow", "wide"),
            P(None, "narrow", "wide"),
            P("narrow", "wide"),
            P("narrow", "wide"),
            P("narrow", "wide"),
            P("narrow", "wide"),
            P("narrow", "wide"),
            P("narrow", "wide"),
            P(None, "narrow", "wide"),
            P(None, "narrow", "wide"),
            P(None, "narrow", "wide"),
            P(None, "narrow", "wide"),
            P(None, "narrow", "wide"),
            P(None, "narrow", "wide"),
            P(("wide", "narrow")),
            P(("wide", "narrow")),
            P(("wide", "narrow")),
        ),
        check_vma=False,
    )
```

profile of v0, /device:TPU:0, one launch (start us, length us, event | category | flops | bytes accessed | tf_op | source)
XLA Modules:
  0.0 2692.1 jit_solution(6654318830509457509)
XLA Ops:
  34.5 22.0 all-gather.15.cloned.1.call-done
  68.3 22.1 all-reduce.5
  95.4 26.3 all-gather.2
  139.9 32.0 %all_gather.51 = bf16[384,384]{0,1:T(8,128)(2,1)S(1)} all-gather(bf16[384,48]{0,1:T(8,128)(2,1)S(1)} %reshape.722), channel_id=1, replica_groups=mesh['wide'=8,'narrow'=4] {'wide'}, dimensions={1}, use_global_device_ids=true | all-gather | bytes 331776 | tf_op jit(solution)/shard_map/all_gather | solution.py:158
  183.3 41.1 %conditional.12 = (f32[1024,6]{0,1:T(8,128)S(1)}, bf16[1024,384]{0,1:T(8,128)(2,1)}) conditional(s32[]{:T(128)} %convert_element_type.215, bf16[3,1024,384]{1,2,0:T(8,128)(2,1)} %copy.591, bf16[3,1024,384]{1,2,0:T(8,128)(2,1)} %copy.591), branch_computations={%region_2.5_spmd, %region_5.8_spmd} | conditional | flops 1667622912 | bytes 184221744
  298.4 154.0 %all-gather.17.cloned.1.call-done = bf16[10,1536,384]{1,2,0:T(8,128)(2,1)} async-done(((bf16[10,1536,48]{1,2,0:T(8,128)(2,1)}), bf16[10,1536,384]{1,2,0:T(8,128)(2,1)}) %all-gather.17.cloned.1.call-update) | async-done | bytes 11796496 | tf_op jit(solution)/shard_map/all_gather | solution.py:161
  494.7 22.9 fusion.49
  595.8 95.2 %conditional.13 = (bf16[3,1024,384]{1,2,0:T(8,128)(2,1)}) conditional(s32[]{:T(128)} %convert_element_type.215, (bf16[3,1024,384]{2,1,0:T(8,128)(2,1)}, f32[1024,6]{0,1:T(8,128)S(1)}, bf16[1024,384]{1,0:T(8,128)(2,1)}) %tuple.159, (bf16[3,1024,384]{2,1,0:T(8,128)(2,1)}, f32[1024,6]{0,1:T(8,128)S(1)}, bf16[1024,384]{1,0:T(8,128)(2,1)}) %tuple.160), branch_computations={%region_24.26_spmd, %region_26.28_spmd} | conditional | flops 4106348544 | bytes 228188320
  738.2 29.6 %copy.616 = f32[10,1536,384]{1,0,2:T(8,128)} copy(f32[10,1536,384]{2,1,0:T(8,128)} %pad_maximum_fusion.2) | data formatting | bytes 47185920 | tf_op jit(solution)/shard_map/concatenate | solution.py:305
  816.2 29.5 %copy.620 = f32[10,1536,384]{1,0,2:T(8,128)} copy(f32[10,1536,384]{2,1,0:T(8,128)} %pad_maximum_fusion.3) | data formatting | bytes 47185920 | tf_op jit(solution)/shard_map/concatenate | solution.py:306
  864.1 604.0 %reduce-scatter.20.cloned.1.call-done = f32[10,1536,48]{1,0,2:T(8,128)} async-done(((f32[10,1536,384]{1,0,2:T(8,128)}), f32[10,1536,48]{1,0,2:T(8,128)}) %reduce-scatter.20.cloned.1.call-update) | async-done | bytes 2949136 | tf_op jit(solution)/shard_map/reduce_scatter | solution.py:311
  1468.2 609.2 %reduce-scatter.24.cloned.1.call-done = f32[10,1536,48]{1,0,2:T(8,128)} async-done(((f32[10,1536,384]{1,0,2:T(8,128)}), f32[10,1536,48]{1,0,2:T(8,128)}) %reduce-scatter.24.cloned.1.call-update) | async-done | bytes 2949136 | tf_op jit(solution)/shard_map/reduce_scatter | solution.py:312
  2078.9 35.2 %all-reduce.7 = f32[2304]{0:T(1024)S(1)} all-reduce(f32[2304]{0:T(1024)S(1)} %reshape.642), channel_id=12, replica_groups=mesh['wide'=8,'narrow'=4] {'wide'}, use_global_device_ids=true, to_apply=%region_53.54.clone | all-reduce | flops 2304 | bytes 18432
  2114.2 27.1 %reduce-scatter.32.cloned.1.call-done = f32[48,8]{1,0:T(8,128)} async-done(((f32[384,8]{1,0:T(8,128)}), f32[48,8]{1,0:T(8,128)}) %reduce-scatter.32.cloned.1.call-update) | async-done | bytes 1552
  2164.0 25.4 reduce-scatter.28.cloned.1.call-done
  2191.5 48.4 %reduce-scatter.22.cloned.1.call-done = f32[10,384,48]{1,0,2:T(8,128)} async-done(((f32[10,1536,48]{1,0,2:T(8,128)}), f32[10,384,48]{1,0,2:T(8,128)}) %reduce-scatter.22.cloned.1.call-update) | async-done | bytes 737296 | tf_op jit(solution)/shard_map/reduce_scatter | solution.py:319
  2242.6 47.5 %reduce-scatter.26.cloned.1.call-done = f32[10,384,48]{1,0,2:T(8,128)} async-done(((f32[10,1536,48]{1,0,2:T(8,128)}), f32[10,384,48]{1,0,2:T(8,128)}) %reduce-scatter.26.cloned.1.call-update) | async-done | bytes 737296 | tf_op jit(solution)/shard_map/reduce_scatter | solution.py:320
  2293.0 59.2 %all_to_all.27 = f32[32,384,48]{1,2,0:T(8,128)S(1)} all-to-all(f32[32,384,48]{1,2,0:T(8,128)S(1)} %pad.19), channel_id=1, replica_groups=mesh['wide'=8,'narrow'=4] {'wide'}, dimensions={0} | all-to-all | bytes 4718592 | tf_op jit(solution)/shard_map/all_to_all | solution.py:347
  2360.6 33.1 %all-reduce.16.cloned.1.call-done = bf16[4,384,384]{2,1,0:T(8,128)(2,1)} async-done(((bf16[4,384,384]{2,1,0:T(8,128)(2,1)}), bf16[4,384,384]{2,1,0:T(8,128)(2,1)}) %all-reduce.16.cloned.1.call-update) | async-done | bytes 1179664 | tf_op jit(solution)/shard_map/psum | solution.py:349
  2413.3 37.8 %all-reduce.18.cloned.1.call-done = bf16[4,384,384]{2,1,0:T(8,128)(2,1)} async-done(((bf16[4,384,384]{2,1,0:T(8,128)(2,1)}), bf16[4,384,384]{2,1,0:T(8,128)(2,1)}) %all-reduce.18.cloned.1.call-update) | async-done | bytes 1179664 | tf_op jit(solution)/shard_map/psum | solution.py:349
  2466.6 37.1 %all-reduce.20.cloned.1.call-done = bf16[4,384,384]{2,1,0:T(8,128)(2,1)} async-done(((bf16[4,384,384]{2,1,0:T(8,128)(2,1)}), bf16[4,384,384]{2,1,0:T(8,128)(2,1)}) %all-reduce.20.cloned.1.call-update) | async-done | bytes 1179664 | tf_op jit(solution)/shard_map/psum | solution.py:349
  2518.9 37.5 %all-reduce.22.cloned.1.call-done = bf16[4,384,384]{2,1,0:T(8,128)(2,1)} async-done(((bf16[4,384,384]{2,1,0:T(8,128)(2,1)}), bf16[4,384,384]{2,1,0:T(8,128)(2,1)}) %all-reduce.22.cloned.1.call-update) | async-done | bytes 1179664 | tf_op jit(solution)/shard_map/psum | solution.py:349
  2572.4 37.6 %all-reduce.24.cloned.1.call-done = bf16[4,384,384]{2,1,0:T(8,128)(2,1)} async-done(((bf16[4,384,384]{2,1,0:T(8,128)(2,1)}), bf16[4,384,384]{2,1,0:T(8,128)(2,1)}) %all-reduce.24.cloned.1.call-update) | async-done | bytes 1179664 | tf_op jit(solution)/shard_map/psum | solution.py:349
  2631.4 43.3 %psum.47 = f32[]{:T(128)} all-reduce(f32[]{:T(128)} %get-tuple-element.304), channel_id=1, replica_groups=mesh['wide'=8,'narrow'=4] {'wide','narrow'}, use_global_device_ids=true, to_apply=%region_56.57 | all-reduce | flops 1 | bytes 8 | tf_op jit(solution)/shard_map/psum | solution.py:375
  (480 shorter events, 634.7 us)
Async XLA Ops:
  7.2 27.2 %all-gather.11.cloned.1.call-start = ((), (), s32[]{:S(2)}) async-start(), calls=%async_computation.12 | async-start | bytes 1843200 | tf_op jit(solution)/shard_map/all_gather | solution.py:152
  9.2 47.3 %all-gather.15.cloned.1.call-start = ((), (), s32[]{:S(2)}) async-start(), calls=%async_computation.14 | async-start | bytes 1843200 | tf_op jit(solution)/shard_map/all_gather | solution.py:153
  11.2 162.0 %all-gather.9.cloned.1.call-start = ((), (), s32[]{:S(2)}) async-start(), calls=%async_computation.11 | async-start | bytes 2985984 | tf_op jit(solution)/shard_map/all_gather | solution.py:157
  30.6 254.7 %all-gather.13.cloned.1.call-start = ((), (), s32[]{:S(2)}) async-start(), calls=%async_computation.13 | async-start | bytes 13271040 | tf_op jit(solution)/shard_map/all_gather | solution.py:160
  34.4 417.9 %all-gather.17.cloned.1.call-start = ((), (), s32[]{:S(2)}) async-start(), calls=%async_computation.15 | async-start | bytes 13271040 | tf_op jit(solution)/shard_map/all_gather | solution.py:161
  56.5 791.2 %reduce-scatter.18.cloned.1.call-start = ((), (), s32[]{:S(2)}) async-start(), calls=%async_computation.17 | async-start | bytes 663552 | tf_op jit(solution)/shard_map/reduce_scatter | solution.py:309
  253.2 241.5 %copy-start.114 = (f32[8,384]{1,0:T(8,128)}, f32[8,384]{1,0:T(8,128)S(1)}, u32[]{:S(2)}) copy-start(f32[8,384]{1,0:T(8,128)S(1)} %mul.695) | copy-start | bytes 36868
  266.4 292.6 %copy-start = (f32[1024,384]{1,0:T(8,128)}, f32[1024,384]{1,0:T(8,128)S(1)}, u32[]{:S(2)}) copy-start(f32[1024,384]{1,0:T(8,128)S(1)} %bitcast_multiply_fusion.3) | copy-start | bytes 4718596
  298.4 167.5 %copy-start.90 = (s32[2048]{0:T(1024)S(1)}, s32[2048]{0:T(1024)}, u32[]{:S(2)}) copy-start(s32[2048]{0:T(1024)} %broadcast_clamp_fusion) | copy-start | bytes 24580
  691.0 167.7 %reduce-scatter.16.cloned.1.call-start = ((), (), s32[]{:S(2)}) async-start(), calls=%async_computation.16 | async-start | bytes 5971968 | tf_op jit(solution)/shard_map/reduce_scatter | solution.py:308
  705.4 762.6 %reduce-scatter.20.cloned.1.call-start = ((), (), s32[]{:S(2)}) async-start(), calls=%async_computation.18 | async-start | bytes 42467328 | tf_op jit(solution)/shard_map/reduce_scatter | solution.py:311
  767.8 1309.5 %reduce-scatter.24.cloned.1.call-start = ((), (), s32[]{:S(2)}) async-start(), calls=%async_computation.20 | async-start | bytes 42467328 | tf_op jit(solution)/shard_map/reduce_scatter | solution.py:312
  845.8 1295.5 %reduce-scatter.32.cloned.1.call-start = ((), (), s32[]{:S(2)}) async-start(), calls=%async_computation.29 | async-start | bytes 221184
  847.6 1315.4 %reduce-scatter.30.cloned.1.call-start = ((), (), s32[]{:S(2)}) async-start(), calls=%async_computation.28 | async-start | bytes 245760
  849.4 1339.9 %reduce-scatter.28.cloned.1.call-start = ((), (), s32[]{:S(2)}) async-start(), calls=%async_computation.27 | async-start | bytes 983040
  864.0 1375.9 %reduce-scatter.22.cloned.1.call-start = ((), (), s32[]{:S(2)}) async-start(), calls=%async_computation.19 | async-start | bytes 5898240 | tf_op jit(solution)/shard_map/reduce_scatter | solution.py:319
  1468.1 822.0 %reduce-scatter.26.cloned.1.call-start = ((), (), s32[]{:S(2)}) async-start(), calls=%async_computation.21 | async-start | bytes 5898240 | tf_op jit(solution)/shard_map/reduce_scatter | solution.py:320
  2077.4 162.5 %copy-start.65 = (f32[10,384,48]{1,2,0:T(8,128)S(1)}, f32[10,384,48]{1,2,0:T(8,128)}, u32[]{:S(2)}) copy-start(f32[10,384,48]{1,2,0:T(8,128)} %param.43) | copy-start | bytes 2211844
  2077.4 316.3 %all-reduce.16.cloned.1.call-start = ((), (), s32[]{:S(2)}) async-start(), calls=%async_computation.22 | async-start | bytes 2359296 | tf_op jit(solution)/shard_map/psum | solution.py:349
  2358.1 92.9 %all-reduce.18.cloned.1.call-start = ((), (), s32[]{:S(2)}) async-start(), calls=%async_computation.23 | async-start | bytes 2359296 | tf_op jit(solution)/shard_map/psum | solution.py:349
  2413.2 90.5 %all-reduce.20.cloned.1.call-start = ((), (), s32[]{:S(2)}) async-start(), calls=%async_computation.24 | async-start | bytes 2359296 | tf_op jit(solution)/shard_map/psum | solution.py:349
  2466.1 90.3 %all-reduce.22.cloned.1.call-start = ((), (), s32[]{:S(2)}) async-start(), calls=%async_computation.25 | async-start | bytes 2359296 | tf_op jit(solution)/shard_map/psum | solution.py:349
  2518.8 91.2 %all-reduce.24.cloned.1.call-start = ((), (), s32[]{:S(2)}) async-start(), calls=%async_computation.26 | async-start | bytes 2359296 | tf_op jit(solution)/shard_map/psum | solution.py:349
  2619.5 56.4 %all-to-all-start.1 = ((bf16[4,384,384]{1,0,2:T(4,128)(2,1)}), bf16[4,384,384]{1,0,2:T(4,128)(2,1)}, u32[]{:S(2)}, u32[]{:S(2)}) async-start(bf16[4,384,384]{1,0,2:T(4,128)(2,1)} %copy.631), calls=%async_computation.7 | async-start | bytes 2359296 | tf_op jit(solution)/shard_map/all_to_all | solution.py:363
  (116 other events, 2540.2 us)
Sparse Core Ops, SparseCore 0:
  10.2 24.1 all-gather.10
  36.5 19.9 all-gather.14
  59.3 55.6 all-gather.8
  117.0 168.1 all-gather.12
  287.3 165.0 all-gather.16
  691.1 60.2 reduce-scatter.17
  755.5 103.2 reduce-scatter.15
  862.6 605.3 reduce-scatter.19
  1472.5 604.8 reduce-scatter.23
  2081.0 60.2 reduce-scatter.31
  2144.3 18.7 reduce-scatter.29
  2166.0 23.2 reduce-scatter.27
  2192.0 47.8 reduce-scatter.21
  2242.3 47.8 reduce-scatter.25
  2358.2 35.3 all-reduce.15
  2413.3 37.6 all-reduce.17
  2466.3 37.3 all-reduce.19
  2518.9 37.4 all-reduce.21
  2572.5 37.4 all-reduce.23
where the time goes:
time: 2700 us; the launch traced here: 2690 us
  waiting for transfers between devices  1750 us (65%)
  matrix products  315 us (12%)
  blocking collectives  257 us (10%)
  local copies, waits for them, and re-layouts  213 us (8%)
  other arithmetic  107 us (4%)
    reduce_scatter x1, waiting for transfers between devices, on_device(): lax.psum_scatter(g_down, 'wide', scatter_dimension=2, tiled=True)  609 us
    reduce_scatter x1, waiting for transfers between devices, on_device(): lax.psum_scatter(g_up, 'wide', scatter_dimension=2, tiled=True)  604 us
    psum x5, waiting for transfers between devices, on_device(): lax.psum(jnp.einsum('mrc,mrd->mcd', current, current, precision=PRECISE)....  183 us
    all_gather x1, waiting for transfers between devices, on_device(): lax.all_gather(row_pieces[4], 'wide', axis=2, tiled=True)  154 us
    unnamed x4, blocking collectives  69.5 us
    unnamed x22, waiting for transfers between devices  67.3 us
    all_to_all x1, blocking collectives, on_device(): lax.all_to_all(stacked, 'wide', split_axis=0, concat_axis=2, tiled=True)  59.2 us
  transfers between devices with their start and end apart: 20, of which 17 were waited for; matrix products, arithmetic and copies ran while one was open for 11% of the time, Pallas kernels for 0%

commit v1 on v0

--- a/solution.py
+++ b/solution.py
@@ -3,8 +3,11 @@
 import jax
 import jax.numpy as jnp
 from jax import lax
+from jax.experimental import pallas as pl
+from jax.experimental.pallas import tpu as pltpu
 from jax.sharding import PartitionSpec as P
 
+WIDE, NARROW = "wide", "narrow"
 D = 384
 HEADS = 6
 HEAD = 64
@@ -146,20 +149,20 @@
     bf_type = jnp.bfloat16
     fl_type = jnp.float32
     row_pieces = (
-        lax.all_gather(w_square.astype(bf_type), "narrow", axis=1, tiled=True),
-        lax.all_gather(w_out.astype(bf_type), "narrow", axis=0, tiled=True),
-        lax.all_gather(w_router.astype(bf_type), "narrow", axis=0, tiled=True),
-        lax.all_gather(w_up.astype(bf_type), "narrow", axis=1, tiled=True),
-        lax.all_gather(w_down.astype(bf_type), "narrow", axis=1, tiled=True),
-        lax.all_gather(b_ada.astype(bf_type), "narrow", axis=0, tiled=True),
+        lax.all_gather(w_square.astype(bf_type), NARROW, axis=1, tiled=True),
+        lax.all_gather(w_out.astype(bf_type), NARROW, axis=0, tiled=True),
+        lax.all_gather(w_router.astype(bf_type), NARROW, axis=0, tiled=True),
+        lax.all_gather(w_up.astype(bf_type), NARROW, axis=1, tiled=True),
+        lax.all_gather(w_down.astype(bf_type), NARROW, axis=1, tiled=True),
+        lax.all_gather(b_ada.astype(bf_type), NARROW, axis=0, tiled=True),
     )
     whole_low = (
-        lax.all_gather(row_pieces[0], "wide", axis=2, tiled=True),
-        lax.all_gather(row_pieces[1], "wide", axis=1, tiled=True),
-        lax.all_gather(row_pieces[2], "wide", axis=1, tiled=True),
-        lax.all_gather(row_pieces[3], "wide", axis=2, tiled=True),
-        lax.all_gather(row_pieces[4], "wide", axis=2, tiled=True),
-        lax.all_gather(row_pieces[5], "wide", axis=0, tiled=True),
+        lax.all_gather(row_pieces[0], WIDE, axis=2, tiled=True),
+        lax.all_gather(row_pieces[1], WIDE, axis=1, tiled=True),
+        lax.all_gather(row_pieces[2], WIDE, axis=1, tiled=True),
+        lax.all_gather(row_pieces[3], WIDE, axis=2, tiled=True),
+        lax.all_gather(row_pieces[4], WIDE, axis=2, tiled=True),
+        lax.all_gather(row_pieces[5], WIDE, axis=0, tiled=True),
     )
     square_low, out_low, router_low, up_low, down_low, bias_low = whole_low
     res_group = resolution[0]
@@ -210,18 +213,18 @@
         mid_state + (mixture.reshape(segments, SHORT, D) * modulation[:, 5:6]).reshape(-1, D)
     ).astype(bf_type)
     again_rows = (
-        lax.all_gather(w_square.astype(bf_type), "narrow", axis=1, tiled=True),
-        lax.all_gather(w_out.astype(bf_type), "narrow", axis=0, tiled=True),
-        lax.all_gather(w_router.astype(bf_type), "narrow", axis=0, tiled=True),
-        lax.all_gather(w_up.astype(bf_type), "narrow", axis=1, tiled=True),
-        lax.all_gather(w_down.astype(bf_type), "narrow", axis=1, tiled=True),
+        lax.all_gather(w_square.astype(bf_type), NARROW, axis=1, tiled=True),
+        lax.all_gather(w_out.astype(bf_type), NARROW, axis=0, tiled=True),
+        lax.all_gather(w_router.astype(bf_type), NARROW, axis=0, tiled=True),
+        lax.all_gather(w_up.astype(bf_type), NARROW, axis=1, tiled=True),
+        lax.all_gather(w_down.astype(bf_type), NARROW, axis=1, tiled=True),
     )
     again_whole = (
-        lax.all_gather(again_rows[0], "wide", axis=2, tiled=True),
-        lax.all_gather(again_rows[1], "wide", axis=1, tiled=True),
-        lax.all_gather(again_rows[2], "wide", axis=1, tiled=True),
-        lax.all_gather(again_rows[3], "wide", axis=2, tiled=True),
-        lax.all_gather(again_rows[4], "wide", axis=2, tiled=True),
+        lax.all_gather(again_rows[0], WIDE, axis=2, tiled=True),
+        lax.all_gather(again_rows[1], WIDE, axis=1, tiled=True),
+        lax.all_gather(again_rows[2], WIDE, axis=1, tiled=True),
+        lax.all_gather(again_rows[3], WIDE, axis=2, tiled=True),
+        lax.all_gather(again_rows[4], WIDE, axis=2, tiled=True),
     )
     square_low, out_low, router_low, up_low, down_low = again_whole
     grad_out = cotangent.astype(fl_type)
@@ -305,20 +308,20 @@
     g_up = jnp.concatenate([g_routed_up, g_shared_up], axis=0)
     g_down = jnp.concatenate([g_routed_down, g_shared_down], axis=0)
     by_columns = (
-        lax.psum_scatter(g_square, "wide", scatter_dimension=2, tiled=True),
-        lax.psum_scatter(g_out, "wide", scatter_dimension=1, tiled=True),
-        lax.psum_scatter(g_router, "wide", scatter_dimension=1, tiled=True),
-        lax.psum_scatter(g_up, "wide", scatter_dimension=2, tiled=True),
-        lax.psum_scatter(g_down, "wide", scatter_dimension=2, tiled=True),
-        lax.psum_scatter(g_bias, "wide", scatter_dimension=0, tiled=True),
+        lax.psum_scatter(g_square, WIDE, scatter_dimension=2, tiled=True),
+        lax.psum_scatter(g_out, WIDE, scatter_dimension=1, tiled=True),
+        lax.psum_scatter(g_router, WIDE, scatter_dimension=1, tiled=True),
+        lax.psum_scatter(g_up, WIDE, scatter_dimension=2, tiled=True),
+        lax.psum_scatter(g_down, WIDE, scatter_dimension=2, tiled=True),
+        lax.psum_scatter(g_bias, WIDE, scatter_dimension=0, tiled=True),
     )
     summed = (
-        lax.psum_scatter(by_columns[0], "narrow", scatter_dimension=1, tiled=True),
-        lax.psum_scatter(by_columns[1], "narrow", scatter_dimension=0, tiled=True),
-        lax.psum_scatter(by_columns[2], "narrow", scatter_dimension=0, tiled=True),
-        lax.psum_scatter(by_columns[3], "narrow", scatter_dimension=1, tiled=True),
-        lax.psum_scatter(by_columns[4], "narrow", scatter_dimension=1, tiled=True),
-        lax.psum_scatter(by_columns[5], "narrow", scatter_dimension=0, tiled=True),
+        lax.psum_scatter(by_columns[0], NARROW, scatter_dimension=1, tiled=True),
+        lax.psum_scatter(by_columns[1], NARROW, scatter_dimension=0, tiled=True),
+        lax.psum_scatter(by_columns[2], NARROW, scatter_dimension=0, tiled=True),
+        lax.psum_scatter(by_columns[3], NARROW, scatter_dimension=1, tiled=True),
+        lax.psum_scatter(by_columns[4], NARROW, scatter_dimension=1, tiled=True),
+        lax.psum_scatter(by_columns[5], NARROW, scatter_dimension=0, tiled=True),
     )
     state_square = MOMENTUM * moment_square + summed[0]
     state_out = MOMENTUM * moment_out + summed[1]
@@ -340,15 +343,15 @@
         ],
         axis=0,
     )
-    wide_count = lax.axis_size("wide")
+    wide_count = lax.axis_size(WIDE)
     matrices = stacked.shape[0]
     per_owner = -(-matrices // wide_count)
     stacked = jnp.pad(stacked, ((0, per_owner * wide_count - matrices), (0, 0), (0, 0)))
-    current = lax.all_to_all(stacked, "wide", split_axis=0, concat_axis=2, tiled=True)
+    current = lax.all_to_all(stacked, WIDE, split_axis=0, concat_axis=2, tiled=True)
     for sweep_num in range(5):
         gram_mat = lax.psum(
             jnp.einsum("mrc,mrd->mcd", current, current, precision=PRECISE).astype(jnp.bfloat16),
-            "narrow",
+            NARROW,
         ).astype(jnp.float32)
         if sweep_num == 0:
             factor = 1.0 / (jnp.sqrt(jnp.trace(gram_mat, axis1=1, axis2=2)) + 1e-07)
@@ -361,7 +364,7 @@
             "mrc,mcd->mrd", current, polynomial, precision=PRECISE
         )
     spread_back = lax.all_to_all(
-        as_sent(current), "wide", split_axis=2, concat_axis=0, tiled=True
+        as_sent(current), WIDE, split_axis=2, concat_axis=0, tiled=True
     ).astype(current.dtype)[:matrices]
     expert_total = w_up.shape[0]
     small_factor = RATE * 0.2 * D**0.5
@@ -372,7 +375,7 @@
     master_up = w_up - large_factor * spread_back[11 : 11 + expert_total]
     master_down = w_down - large_factor * spread_back[11 + expert_total : 11 + 2 * expert_total]
     state_bias = MOMENTUM_VECTOR * moment_bias + summed[5]
-    square_total = lax.psum(jnp.sum(state_bias * state_bias), ("wide", "narrow"))
+    square_total = lax.psum(jnp.sum(state_bias * state_bias), (WIDE, NARROW))
     root_mean = jnp.sqrt(square_total / (6 * D) + 1e-05)
     master_bias = b_ada - RATE_VECTOR * state_bias / root_mean
     step_value = step_count[0].astype(fl_type)
@@ -407,58 +410,890 @@
     )
 
 
+bf = jnp.bfloat16
+f32 = jnp.float32
+TOK = 1024
+NN=(((1,),(0,)),((),())); NT=(((1,),(1,)),((),())); TN=(((0,),(0,)),((),()))
+def dot(a,b,dims=NN): return lax.dot_general(a,b,dims,preferred_element_type=f32)
+
+def gelu_pair(v):
+    sq=v*v
+    th=jnp.tanh(v*(0.7978845608028654+0.035677408136300125*sq))
+    half=0.5*th+0.5
+    act=v*half
+    slope=half+act*(1.0-half)*(1.5957691216057308+0.21406444881780075*sq)
+    return act,slope
+
+def moe_kernel(ids, t0,t1,t2,t3,m0,m1,m2,m3,ga,gb, p0,p1,p2,p3,dg_out,g_send,g_keep,g_b1,g_b2,g_sh,
+               tok,meta,up,dn,ups,dns,gup,gdn,gups,gdns,acc,part,dgs,gst,tsem,wsem,osem,gsem, *, RB, FC):
+    n=ids[0]; z=ids[1]; x=ids[2]
+    tin=(t0,t1,t2,t3); mins=(m0,m1,m2,m3)
+    tcop=[pltpu.make_async_copy(tin[i],tok.at[i],tsem.at[i,0]) for i in range(4)]
+    mcop=[pltpu.make_async_copy(mins[i],meta.at[i],tsem.at[i,1]) for i in range(4)]
+    tcop[0].start(); mcop[0].start()
+    wc=[]
+    for src,xx in ((ga,x),(gb,1-x)):
+        for d in range(4):
+            row=pl.multiple_of((2*lax.rem(z-d+4,4)+xx)*48,16)
+            for m in range(4):
+                tgt=(ups,dns)[m%2]
+                wc.append(pltpu.make_async_copy(src.at[d,4,m],tgt.at[pl.ds(row,48),pl.ds((m//2)*384,384)],wsem.at[0]))
+                for k in range(4):
+                    tgt=(up,dn)[m%2]
+                    wc.append(pltpu.make_async_copy(src.at[d,k,m],tgt.at[m//2,pl.ds(row,48),pl.ds(k*384,384)],wsem.at[1]))
+    for c in wc: c.start()
+    for i in range(1,4): tcop[i].start(); mcop[i].start()
+    gup[...]=jnp.zeros_like(gup); gdn[...]=jnp.zeros_like(gdn); gups[...]=jnp.zeros_like(gups); gdns[...]=jnp.zeros_like(gdns)
+    for c in wc: c.wait()
+
+    def per_src(s,_):
+        pltpu.make_async_copy(t0,tok.at[s],tsem.at[s,0]).wait()
+        pltpu.make_async_copy(m0,meta.at[s],tsem.at[s,1]).wait()
+        def shared(r,_):
+            rows=pl.ds(pl.multiple_of(r*RB,RB),RB)
+            xs=tok[s,rows,:D]; ds=tok[s,rows,D:]
+            out=jnp.zeros((RB,D),f32); dx=jnp.zeros((RB,D),f32)
+            for f in range(0,768,FC):
+                fs=slice(f,f+FC)
+                pre=dot(xs,ups[:,fs]); da=dot(ds,dns[:,fs])
+                act,slope=gelu_pair(pre)
+                ab=act.astype(bf); pb=(slope*da).astype(bf)
+                out=out+dot(ab,dns[:,fs],NT); dx=dx+dot(pb,ups[:,fs],NT)
+                gups[:,fs]+=dot(xs,pb,TN); gdns[:,fs]+=dot(ds,ab,TN)
+            acc[rows,:D]=out; acc[rows,D:]=dx
+            return 0
+        lax.fori_loop(0,TOK//RB,shared,0)
+        def routed(e,_):
+            ex=2*n+e
+            pos=meta[s,pl.ds(ex,1),:]; gat=meta[s,pl.ds(8+ex,1),:]
+            slot=lax.broadcasted_iota(jnp.int32,(CAP,TOK),0).astype(f32)
+            hit=slot==pos
+            hot=hit.astype(f32).astype(bf)
+            gsl=jnp.sum(jnp.where(hit,gat,0.0),axis=1,keepdims=True)
+            xd=dot(hot,tok[s])
+            xs=xd[:,:D].astype(bf); dmx=xd[:,D:]
+            ds=(dmx*gsl).astype(bf)
+            out=jnp.zeros((CAP,D),f32); dx=jnp.zeros((CAP,D),f32)
+            for f in range(0,FF,FC):
+                fs=slice(f,f+FC)
+                pre=dot(xs,up[e,:,fs]); da=dot(ds,dn[e,:,fs])
+                act,slope=gelu_pair(pre)
+                ab=act.astype(bf); pb=(slope*da).astype(bf)
+                out=out+dot(ab,dn[e,:,fs],NT); dx=dx+dot(pb,up[e,:,fs],NT)
+                gup[e,:,fs]+=dot(xs,pb,TN); gdn[e,:,fs]+=dot(ds,ab,TN)
+            dgate=jnp.sum(out*dmx,axis=1,keepdims=True)
+            dgs[s,pl.ds(e,1),:]=jnp.sum(jnp.where(hit,dgate,0.0),axis=0,keepdims=True)
+            both=jnp.concatenate([(out*gsl).astype(bf),dx.astype(bf)],axis=1)
+            acc[...]+=dot(hot,both,TN)
+            return 0
+        lax.fori_loop(0,2,routed,0)
+        part[s]=acc[...].astype(bf)
+        for i,dst in enumerate((p0,p1,p2,p3)):
+            @pl.when(s==i)
+            def _():
+                pltpu.make_async_copy(part.at[i],dst,osem.at[i]).start()
+        return 0
+    lax.fori_loop(0,4,per_src,0)
+    outs=[pltpu.make_async_copy(part.at[i],dst,osem.at[i]) for i,dst in enumerate((p0,p1,p2,p3))]
+    cd=pltpu.make_async_copy(dgs,dg_out,osem.at[4]); cd.start(); outs.append(cd)
+    def to(slot,dst): return pltpu.make_async_copy(gst.at[slot],dst,gsem.at[slot])
+    for e in range(2):
+        for m,src in ((0,gup),(1,gdn)):
+            gst[2*e+m]=src[e].astype(bf)
+    for sh in range(2):
+        for m,src in ((0,gups),(1,gdns)):
+            gst[4,:,pl.ds((2*sh+m)*384,384)]=src[:,sh*384:(sh+1)*384].astype(bf)
+    @pl.when(x==0)
+    def _():
+        to(0,g_keep).start(); to(3,g_send).start()
+    @pl.when(x!=0)
+    def _():
+        to(0,g_send).start(); to(3,g_keep).start()
+    to(1,g_b1).start(); to(2,g_b2).start(); to(4,g_sh).start()
+    for slot,dst in ((0,g_keep),(3,g_send),(1,g_b1),(2,g_b2),(4,g_sh)): to(slot,dst).wait()
+    for c in outs: c.wait()
+
+def moe(ids,toks,metas,ga,gb,RB=512,FC=512):
+    anyspec=pl.BlockSpec(memory_space=pl.ANY)
+    return pl.pallas_call(
+        partial(moe_kernel,RB=RB,FC=FC),
+        out_shape=[jax.ShapeDtypeStruct((TOK,2*D),bf)]*4+[jax.ShapeDtypeStruct((4,8,TOK),f32)]+[jax.ShapeDtypeStruct((D,FF),bf)]*5,
+        in_specs=[pl.BlockSpec(memory_space=pltpu.SMEM)]+[anyspec]*10,
+        out_specs=[anyspec]*10,
+        scratch_shapes=[pltpu.VMEM((4,TOK,2*D),bf),pltpu.VMEM((4,16,TOK),f32),
+            pltpu.VMEM((2,D,FF),bf),pltpu.VMEM((2,D,FF),bf),pltpu.VMEM((D,768),bf),pltpu.VMEM((D,768),bf),
+            pltpu.VMEM((2,D,FF),f32),pltpu.VMEM((2,D,FF),f32),pltpu.VMEM((D,768),f32),pltpu.VMEM((D,768),f32),
+            pltpu.VMEM((TOK,2*D),f32),pltpu.VMEM((4,TOK,2*D),bf),pltpu.VMEM((4,8,TOK),f32),pltpu.VMEM((5,D,FF),bf),
+            pltpu.SemaphoreType.DMA((4,2)),pltpu.SemaphoreType.DMA((2,)),pltpu.SemaphoreType.DMA((5,)),pltpu.SemaphoreType.DMA((5,))],
+        compiler_params=pltpu.CompilerParams(vmem_limit_bytes=63*1024*1024),
+        name="moe",
+    )(ids,*toks,*metas,ga,gb)
+
+
+def head_only(block, head):
+    lane = lax.broadcasted_iota(jnp.int32, block.shape, 1)
+    return jnp.where((lane >= 64) == (head == 1), block, jnp.zeros_like(block))
+
+
+def attend_kernel(res, q_ref, k_ref, v_ref, o_ref, lse_ref, vt_ref):
+    qb = pl.program_id(1)
+
+    @pl.when(qb == 0)
+    def _():
+        vt_ref[...] = v_ref[...].T
+
+    def work(rows):
+        q = q_ref[...] * 0.125
+        outs = []
+        for head in range(2):
+            scores = dot(k_ref[rows, :], head_only(q, head), NT)
+            top = jnp.max(scores, axis=0, keepdims=True)
+            expo = jnp.exp(scores - top)
+            total = jnp.sum(expo, axis=0, keepdims=True)
+            weights = (expo * (1.0 / total)).astype(bf)
+            outs.append(dot(vt_ref[head * 64 : head * 64 + 64, rows], weights))
+            lse_ref[0, head : head + 1, :] = top + jnp.log(total)
+        o_ref[...] = jnp.concatenate(outs, axis=0).T.astype(bf)
+
+    @pl.when(res[0] == 1)
+    def _():
+        work(pl.ds(0, TOK))
+
+    @pl.when(res[0] != 1)
+    def _():
+        work(pl.ds(pl.multiple_of(qb * 256, 256), 256))
+
+
+def attend_fast(resolution, projected):
+    return pl.pallas_call(
+        attend_kernel,
+        grid_spec=pltpu.PrefetchScalarGridSpec(
+            num_scalar_prefetch=1,
+            grid=(3, 4),
+            in_specs=[
+                pl.BlockSpec((256, 128), lambda h, i, r: (i, h)),
+                pl.BlockSpec((TOK, 128), lambda h, i, r: (0, 3 + h)),
+                pl.BlockSpec((TOK, 128), lambda h, i, r: (0, 6 + h)),
+            ],
+            out_specs=[
+                pl.BlockSpec((256, 128), lambda h, i, r: (i, h)),
+                pl.BlockSpec((1, 8, 256), lambda h, i, r: (h, 0, i)),
+            ],
+            scratch_shapes=[pltpu.VMEM((128, TOK), bf)],
+        ),
+        out_shape=(
+            jax.ShapeDtypeStruct((TOK, D), bf),
+            jax.ShapeDtypeStruct((3, 8, TOK), f32),
+        ),
+        compiler_params=pltpu.CompilerParams(vmem_limit_bytes=48 * 1024 * 1024),
+        name="attend_fast",
+    )(resolution, projected, projected, projected)
+
+
+def attend_back_kernel(
+    res, q_ref, k_ref, v_ref, do_ref, lse_ref, dq_ref, dk_ref, dv_ref, kt_ref, dk_acc, dv_acc
+):
+    qb = pl.program_id(1)
+
+    @pl.when(qb == 0)
+    def _():
+        kt_ref[...] = k_ref[...].T
+
+    def work(rows, whole):
+        q = q_ref[...] * 0.125
+        grads = []
+        dk = dv = None
+        for head in range(2):
+            qh = head_only(q, head)
+            doh = head_only(do_ref[...], head)
+            scores = dot(k_ref[rows, :], qh, NT)
+            probs = jnp.exp(scores - lse_ref[0, head : head + 1, :])
+            d_weights = dot(v_ref[rows, :], doh, NT)
+            delta = jnp.sum(d_weights * probs, axis=0, keepdims=True)
+            d_scores = (probs * (d_weights - delta)).astype(bf)
+            dv_one = dot(probs.astype(bf), doh)
+            dk_one = dot(d_scores, qh)
+            dv = dv_one if dv is None else dv + dv_one
+            dk = dk_one if dk is None else dk + dk_one
+            grads.append(dot(kt_ref[head * 64 : head * 64 + 64, rows], d_scores))
+        dq_ref[...] = (jnp.concatenate(grads, axis=0).T * 0.125).astype(bf)
+        if not whole:
+            dk_ref[rows, :] = dk.astype(bf)
+            dv_ref[rows, :] = dv.astype(bf)
+            return
+
+        @pl.when(qb == 0)
+        def _():
+            dk_acc[...] = dk
+            dv_acc[...] = dv
+
+        @pl.when(qb != 0)
+        def _():
+            dk_acc[...] += dk
+            dv_acc[...] += dv
+
+        @pl.when(qb == 3)
+        def _():
+            dk_ref[...] = dk_acc[...].astype(bf)
+            dv_ref[...] = dv_acc[...].astype(bf)
+
+    @pl.when(res[0] == 1)
+    def _():
+        work(pl.ds(0, TOK), True)
+
+    @pl.when(res[0] != 1)
+    def _():
+        work(pl.ds(pl.multiple_of(qb * 256, 256), 256), False)
+
+
+def attend_back_fast(resolution, projected, lse, d_attended):
+    return pl.pallas_call(
+        attend_back_kernel,
+        grid_spec=pltpu.PrefetchScalarGridSpec(
+            num_scalar_prefetch=1,
+            grid=(3, 4),
+            in_specs=[
+                pl.BlockSpec((256, 128), lambda h, i, r: (i, h)),
+                pl.BlockSpec((TOK, 128), lambda h, i, r: (0, 3 + h)),
+                pl.BlockSpec((TOK, 128), lambda h, i, r: (0, 6 + h)),
+                pl.BlockSpec((256, 128), lambda h, i, r: (i, h)),
+                pl.BlockSpec((1, 8, 256), lambda h, i, r: (h, 0, i)),
+            ],
+            out_specs=[
+                pl.BlockSpec((256, 128), lambda h, i, r: (i, h)),
+                pl.BlockSpec((TOK, 128), lambda h, i, r: (0, h)),
+                pl.BlockSpec((TOK, 128), lambda h, i, r: (0, h)),
+            ],
+            scratch_shapes=[
+                pltpu.VMEM((128, TOK), bf),
+                pltpu.VMEM((TOK, 128), f32),
+                pltpu.VMEM((TOK, 128), f32),
+            ],
+        ),
+        out_shape=[jax.ShapeDtypeStruct((TOK, D), bf)] * 3,
+        compiler_params=pltpu.CompilerParams(vmem_limit_bytes=48 * 1024 * 1024),
+        name="attend_back_fast",
+    )(resolution, projected, projected, projected, d_attended, lse)
+
+
+def halves(value):
+    high = value.astype(bf)
+    return high, (value - high.astype(f32)).astype(bf)
+
+
+def dot_three(a, b, dims=NN):
+    return dot(a[0], b[0], dims) + dot(a[0], b[1], dims) + dot(a[1], b[0], dims)
+
+
+def up_owner(e):
+    return (24 if e % 2 else 0) + e // 2 if e < 8 else 20 + 2 * (e - 8)
+
+
+def down_owner(e):
+    return (4 if e % 2 else 16) + e // 2 if e < 8 else 21 + 2 * (e - 8)
+
+
+def square_owner(j):
+    return 8 + j if j < 3 else (9 + j if j < 7 else 21 + j)
+
+
+OUT_OWNER, ROUTER_OWNER = 11, 30
+
+
+def pack_kernel(square, out, router, up, down, packed):
+    for e in range(10):
+        packed[up_owner(e)] = up[e]
+        packed[down_owner(e)] = down[e]
+    rest = jnp.zeros((48, D - 96), f32)
+    for j in range(9):
+        packed[square_owner(j)] = jnp.concatenate([square[j], rest], axis=1)
+    packed[OUT_OWNER] = jnp.concatenate([out[...], rest], axis=1)
+    packed[ROUTER_OWNER] = router[...]
+    packed[31] = jnp.zeros((48, D), f32)
+
+
+def pack_owned(square, out, router, up, down):
+    vmem = pl.BlockSpec(memory_space=pltpu.VMEM)
+    return pl.pallas_call(
+        pack_kernel,
+        out_shape=jax.ShapeDtypeStruct((32, 48, D), f32),
+        in_specs=[vmem] * 5,
+        out_specs=vmem,
+        name="pack_owned",
+    )(square, out, router, up, down)
+
+
+def owned_grad_kernel(ids, *refs):
+    held, received = refs[:3], refs[3:12]
+    dense, small, full_out, cut_out, buf, sems = refs[12:]
+    n, z, x = ids[0], ids[1], ids[2]
+    is_small = (z == 1) | ((z == 3) & (x == 1))
+
+    def fetch(group):
+        sources = [held[group]] + list(received[3 * group : 3 * group + 3])
+        return [
+            pltpu.make_async_copy(source, buf.at[i], sems.at[i])
+            for i, source in enumerate(sources)
+        ]
+
+    for group, owner in enumerate((0, 2, 3)):
+
+        @pl.when((z == owner) & jnp.logical_not(is_small))
+        def _():
+            for copy in fetch(group):
+                copy.start()
+            for copy in fetch(group):
+                copy.wait()
+
+    @pl.when(jnp.logical_not(is_small))
+    def _():
+        for k in range(4):
+            lanes = slice(k * D, k * D + D)
+            total = buf[0, :, lanes].astype(f32) + buf[1, :, lanes].astype(f32)
+            full_out[k] = total + buf[2, :, lanes].astype(f32) + buf[3, :, lanes].astype(f32)
+
+    @pl.when(is_small)
+    def _():
+        rows = small[...].reshape(32, 8, 512)
+
+        def place(matrix, width):
+            rest = jnp.zeros((D, D - width), f32)
+            for m in range(4):
+                part = matrix[:, m * width : m * width + width]
+                full_out[m ^ n] = jnp.concatenate([part, rest], axis=1)
+
+        @pl.when(z == 1)
+        def _():
+            @pl.when(x == 0)
+            def _():
+                place(dense[...], 96)
+
+        @pl.when(jnp.logical_not((z == 1) & (x == 0)))
+        def _():
+            is_router = (z == 3) & (n == 2)
+
+            @pl.when(is_router)
+            def _():
+                summed = jnp.sum(rows[:, :, :D], axis=0)
+                place(jnp.concatenate([summed, jnp.zeros((120, D), f32)], axis=0).T[:, :8], 2)
+
+            @pl.when(jnp.logical_not(is_router))
+            def _():
+                first = (lax.broadcasted_iota(jnp.int32, (256, D), 0) % 8) < 4
+                both = small[:, :D]
+                mods = jnp.where(first, both, 0.0)
+                conds = pltpu.roll(both, 252, 0)
+                conds = jnp.where(first, conds, 0.0)
+                place(dot_three(halves(mods), halves(conds), TN), 96)
+
+    for w in range(8):
+        for m in range(4):
+            cut_out[4 * w + m] = full_out[m ^ n, 48 * w : 48 * w + 48, :].astype(bf)
+
+
+def owned_grad(ids, held, received, dense, small):
+    anyspec, vmem = pl.BlockSpec(memory_space=pl.ANY), pl.BlockSpec(memory_space=pltpu.VMEM)
+    return pl.pallas_call(
+        owned_grad_kernel,
+        out_shape=(
+            jax.ShapeDtypeStruct((4, D, D), f32),
+            jax.ShapeDtypeStruct((32, 48, D), bf),
+        ),
+        in_specs=[pl.BlockSpec(memory_space=pltpu.SMEM)] + [anyspec] * 12 + [vmem] * 2,
+        out_specs=[vmem, vmem],
+        scratch_shapes=[pltpu.VMEM((4, D, FF), bf), pltpu.SemaphoreType.DMA((4,))],
+        compiler_params=pltpu.CompilerParams(vmem_limit_bytes=40 * 1024 * 1024),
+        name="owned_grad",
+    )(ids, *held, *received, dense, small)
+
+
+def ortho_kernel(ids, grad, moment, extra, cut_out, cur, poly):
+    n = ids[0]
+    for k in range(4):
+        cur[k] = grad[k]
+    for w in range(8):
+        rows = slice(48 * w, 48 * w + 48)
+        for m in range(4):
+            cur[m ^ n, rows, :] += MOMENTUM * moment[4 * w + m]
+    total = jnp.zeros((1, D), f32)
+    for k in range(4):
+        total = total + jnp.sum(cur[k] * cur[k], axis=0, keepdims=True)
+    factor = 1.0 / (jnp.sqrt(jnp.sum(total, axis=1, keepdims=True)) + 1e-07)
+    for k in range(4):
+        cur[k] = cur[k] * factor
+
+    def sweep(_, carry):
+        gram = jnp.zeros((D, D), f32)
+        for k in range(4):
+            part = halves(cur[k])
+            gram = gram + dot_three(part, part, NT)
+        split = halves(gram)
+        poly[...] = NS_SECOND * gram + NS_THIRD * dot_three(split, split)
+        split = halves(poly[...])
+        for k in range(4):
+            block = cur[k]
+            cur[k] = NS_FIRST * block + dot_three(split, halves(block))
+        return carry
+
+    lax.fori_loop(0, 5, sweep, 0)
+    for w in range(8):
+        for m in range(4):
+            cut_out[4 * w + m, :48] = cur[m ^ n, 48 * w : 48 * w + 48, :].astype(bf)
+            cut_out[4 * w + m, 48:] = extra[...]
+
+
+def ortho_owned(ids, grad, moment, extra):
+    vmem = pl.BlockSpec(memory_space=pltpu.VMEM)
+    return pl.pallas_call(
+        ortho_kernel,
+        out_shape=jax.ShapeDtypeStruct((32, 56, D), bf),
+        in_specs=[pl.BlockSpec(memory_space=pltpu.SMEM), vmem, vmem, vmem],
+        out_specs=vmem,
+        scratch_shapes=[pltpu.VMEM((4, D, D), f32), pltpu.VMEM((D, D), f32)],
+        compiler_params=pltpu.CompilerParams(vmem_limit_bytes=40 * 1024 * 1024),
+        name="ortho_owned",
+    )(ids, grad, moment, extra)
+
+
+def update_kernel(decay_ref, grads, orthos, *refs):
+    decay = decay_ref[0]
+    weights, moments, emas = refs[0:5], refs[5:10], refs[10:15]
+    states, masters, averages = refs[15:20], refs[20:25], refs[25:30]
+    small_rate, large_rate = RATE * 0.2 * D**0.5, RATE * 0.2 * FF**0.5
+
+    def step(which, at, grad, ortho, rate):
+        states[which][at] = MOMENTUM * moments[which][at] + grad.astype(f32)
+        master = weights[which][at] - rate * ortho.astype(f32)
+        masters[which][at] = master
+        averages[which][at] = decay * emas[which][at] + (1.0 - decay) * master
+
+    for j in range(9):
+        own = square_owner(j)
+        step(0, j, grads[own, :, :96], orthos[own, :48, :96], small_rate)
+    step(1, slice(None), grads[OUT_OWNER, :, :96], orthos[OUT_OWNER, :48, :96], small_rate)
+
+    def router_rows(source):
+        return source[ROUTER_OWNER, :48, :128].astype(f32).T[:2]
+
+    step(2, slice(None), router_rows(grads), router_rows(orthos), small_rate)
+    for e in range(10):
+        step(3, e, grads[up_owner(e)], orthos[up_owner(e), :48], large_rate)
+        step(4, e, grads[down_owner(e)], orthos[down_owner(e), :48], large_rate)
+
+
+def update(decay, grads, orthos, weights, moments, emas):
+    vmem = pl.BlockSpec(memory_space=pltpu.VMEM)
+    shapes = [jax.ShapeDtypeStruct(weight.shape, f32) for weight in weights]
+    return pl.pallas_call(
+        update_kernel,
+        out_shape=shapes * 3,
+        in_specs=[pl.BlockSpec(memory_space=pltpu.SMEM)] + [vmem] * 17,
+        out_specs=[vmem] * 15,
+        compiler_params=pltpu.CompilerParams(vmem_limit_bytes=48 * 1024 * 1024),
+        name="update",
+    )(decay, grads, orthos, *weights, *moments, *emas)
+
+
+AXES = (WIDE, NARROW)
+
+
+def route_pairs(move):
+    pairs = []
+    for index in range(32):
+        w, n = divmod(index, 4)
+        target = move(w // 2, w % 2, n // 2, n % 2)
+        if target is not None:
+            z, x, y, c = target
+            pairs.append((index, (z * 2 + x) * 4 + y * 2 + c))
+    return pairs
+
+
+def send(array, move):
+    return lax.ppermute(array, AXES, route_pairs(move))
+
+
+def to_core(z, x, y, c):
+    return (z, x, y, 1 - c)
+
+
+def to_y(z, x, y, c):
+    return (z, x, 1 - y, c)
+
+
+def to_diag(z, x, y, c):
+    return (z, x, 1 - y, 1 - c)
+
+
+def to_x(z, x, y, c):
+    return (z, 1 - x, y, c)
+
+
+def to_z(step):
+    return lambda z, x, y, c: ((z + step) % 4, x, y, c)
+
+
+NARROW_MOVES = (None, to_core, to_y, to_diag)
+
+
+def pick(array, index, axis=0):
+    return lax.dynamic_index_in_dim(array, index, axis, keepdims=False)
+
+
+def in_order(mine, other, flag):
+    return jnp.where(flag == 0, mine, other), jnp.where(flag == 0, other, mine)
+
+
+def xor_blocks(array, axis, y, c):
+    parts = [lax.index_in_dim(array, i, axis, keepdims=True) for i in range(4)]
+    parts = [jnp.where(c == 0, parts[i], parts[i ^ 1]) for i in range(4)]
+    parts = [jnp.where(y == 0, parts[i], parts[i ^ 2]) for i in range(4)]
+    return jnp.concatenate(parts, axis=axis)
+
+
+def gather_rows(rows, z, x, c):
+    pieces = [send(rows, to_z(step)) for step in (3, 2, 1)] + [rows]
+    pieces = [pieces[2], pieces[1], pieces[0]]
+    recv = {step: send_piece for step, send_piece in zip((1, 2, 3), pieces)}
+    ring = jnp.stack([recv[3], recv[2], recv[1], rows])
+    doubled = jnp.concatenate([ring, ring])
+    by_z = lax.dynamic_slice_in_dim(doubled, (3 - z) % 4, 4, 0)
+    by_zx = jnp.stack(in_order(by_z, send(by_z, to_x), x), axis=1)
+    return jnp.stack(in_order(by_zx, send(by_zx, to_core), c), axis=2)
+
+
+def lanes_to(block, width):
+    return jnp.pad(block, [(0, 0)] * (block.ndim - 1) + [(0, width - block.shape[-1])])
+
+
+def turned(array):
+    return jnp.swapaxes(array, -1, -2)
+
+
+def fast_device(
+    tokens,
+    conditions,
+    routes,
+    resolution,
+    step_count,
+    cotangent,
+    w_square,
+    w_out,
+    w_router,
+    w_up,
+    w_down,
+    b_ada,
+    moment_square,
+    moment_out,
+    moment_router,
+    moment_up,
+    moment_down,
+    moment_bias,
+    ema_square,
+    ema_out,
+    ema_router,
+    ema_up,
+    ema_down,
+    ema_bias,
+):
+    wide = lax.axis_index(WIDE)
+    narrow = lax.axis_index(NARROW)
+    z, x = wide // 2, wide % 2
+    y, c = narrow // 2, narrow % 2
+
+    square_t = turned(w_square).astype(bf)
+    out_t = turned(w_out).astype(bf)[None]
+    misc = jnp.concatenate(
+        [
+            lanes_to(b_ada.astype(bf)[None], 96),
+            lanes_to(w_router.astype(bf), 96),
+            jnp.zeros((5, 96), bf),
+        ]
+    )
+    flat = jnp.concatenate(
+        [
+            square_t[:5].reshape(-1, 96),
+            misc,
+            square_t[5:].reshape(-1, 96),
+            out_t.reshape(-1, 96),
+        ]
+    )
+    by_y = jnp.stack(in_order(flat, send(flat, to_y), y))
+    by_yc = in_order(by_y, send(by_y, to_core), c)
+    rows = jnp.concatenate([by_yc[0][0], by_yc[1][0], by_yc[0][1], by_yc[1][1]], axis=1)
+
+    def my_half(block):
+        return pick(block.reshape(5, 2, 24, D), c, 1).reshape(120, D)
+
+    first_rows = jnp.concatenate([my_half(rows[:240]), rows[240:248]])
+    first_all = gather_rows(first_rows, z, x, c)
+    second_all = gather_rows(my_half(rows[248:]), z, x, c)
+
+    def assemble(gathered):
+        parts = gathered[..., :120, :].reshape(8, 2, 5, 24, D)
+        return jnp.transpose(parts, (2, 0, 1, 3, 4)).reshape(5, D, D)
+
+    first_maps = assemble(first_all)
+    second_maps = assemble(second_all)
+    misc_all = first_all[:, :, 0, 120:, :].reshape(8, 8, 4, 96)
+    bias_low = misc_all[:, 0, :, :72].reshape(-1)
+    router_low = jnp.transpose(misc_all[:, 1:3, :, :48], (2, 1, 0, 3)).reshape(ROUTED, D)
+
+    up_t = turned(w_up).astype(bf)
+    down_t = turned(w_down).astype(bf)
+    routed_t = jnp.stack([up_t[:8], down_t[:8]], axis=1).reshape(4, 4, 48, D)
+    shared_t = jnp.stack([up_t[8:], down_t[8:]], axis=1).reshape(4, 48, D)
+    mine = [pick(routed_t, narrow)]
+    mine += [send(pick(routed_t, narrow ^ k), NARROW_MOVES[k]) for k in (1, 2, 3)]
+    blocks = jnp.stack(mine + [shared_t])
+    near = jnp.stack([blocks] + [send(blocks, to_z(step)) for step in (1, 2, 3)])
+    far = send(near, to_x)
+
+    moment_parts = (
+        turned(moment_square),
+        turned(moment_out),
+        moment_router,
+        turned(moment_up),
+        turned(moment_down),
+    )
+    router_block = lanes_to(turned(moment_router), D)
+    moments = pack_owned(*moment_parts[:2], router_block, *moment_parts[3:])
+
+    res_group = resolution[0]
+    token_f = tokens.astype(f32)
+    segments = tokens.shape[0] // SHORT
+    seg_ratio = LONG // SHORT
+    first_seg = jnp.arange(segments, dtype=jnp.int32) // seg_ratio * seg_ratio
+    chosen = jnp.where(res_group == 1, conditions[first_seg], conditions)
+    cond_low = jax.nn.silu(chosen.astype(f32)).astype(bf)
+    bias_rows = bias_low.astype(f32).reshape(6, D)
+
+    def modulation_of(maps, bias):
+        return dot(cond_low, maps.reshape(-1, D), NT).reshape(segments, -1, D) + bias
+
+    first_two = modulation_of(first_maps[3:], bias_rows[:2])
+    last_four = modulation_of(second_maps[:4], bias_rows[2:])
+    out_map = second_maps[4]
+    seg_rows = token_f.reshape(segments, SHORT, D)
+    first_mod, first_back = jax.vjp(modulate, seg_rows, first_two[:, 0:1], first_two[:, 1:2])
+    hidden_one = first_mod.reshape(-1, D).astype(bf)
+    query_maps = first_maps[:3].reshape(3 * D, D)
+    projected = dot(hidden_one, query_maps, NT).astype(bf)
+    attended, log_total = attend_fast(resolution, projected)
+    attn_out = dot(attended, out_map, NT)
+    gate_one, gate_two = last_four[:, 0:1], last_four[:, 3:4]
+    mid_state = token_f + (attn_out.reshape(segments, SHORT, D) * gate_one).reshape(-1, D)
+    second_mod, second_back = jax.vjp(
+        modulate, mid_state.reshape(segments, SHORT, D), last_four[:, 1:2], last_four[:, 2:3]
+    )
+    hidden_two = second_mod.reshape(-1, D).astype(bf)
+
+    logits = dot(router_low, hidden_two, NT)
+    experts = jnp.arange(ROUTED, dtype=jnp.int32)[:, None]
+    named = (routes[:, 0][None] == experts) | (routes[:, 1][None] == experts)
+    index = jnp.arange(TOK, dtype=jnp.int32)
+    earlier = (index[:, None] < index[None, :]).astype(bf)
+    place = jnp.dot(named.astype(bf), earlier, preferred_element_type=f32)
+    masked = jnp.where(named, logits, -jnp.inf)
+    expo = jnp.where(named, jnp.exp(logits - jnp.max(masked, axis=0, keepdims=True)), 0.0)
+    gates = expo / jnp.sum(expo, axis=0, keepdims=True)
+    meta = jnp.concatenate([jnp.where(named, place, -1.0), gates])
+
+    grad_out = cotangent.astype(f32)
+    grad_seg = grad_out.reshape(segments, SHORT, D)
+    d_mixture = (grad_seg * gate_two).reshape(-1, D).astype(bf)
+    pack = jnp.concatenate([hidden_two, d_mixture], axis=1)
+    pack_core, meta_core = send(pack, to_core), send(meta, to_core)
+    pack_y, meta_y = send(pack, to_y), send(meta, to_y)
+    pack_diag, meta_diag = send(pack_y, to_core), send(meta_y, to_core)
+    place_ids = jnp.stack([narrow, z, x]).astype(jnp.int32)
+    pack, moments = lax.optimization_barrier((pack, moments))
+    moments = lax.all_to_all(moments, AXES, 0, 0, tiled=True)
+    part_own, part_core, part_y, part_diag, d_gate_rows, *grads = moe(
+        place_ids,
+        (pack, pack_core, pack_y, pack_diag),
+        (meta, meta_core, meta_y, meta_diag),
+        near,
+        far,
+    )
+    over = (part_y.astype(f32) + send(part_diag, to_core).astype(f32)).astype(bf)
+    own = part_own.astype(f32) + send(part_core, to_core).astype(f32)
+    total = own + send(over, to_y).astype(f32)
+    mixture, d_hidden = total[:, :D], total[:, D:]
+    d_rows = [d_gate_rows[0, :2]]
+    d_rows += [send(d_gate_rows[k, :2], NARROW_MOVES[k]) for k in (1, 2, 3)]
+    d_gates = xor_blocks(jnp.stack(d_rows), 0, y, c).reshape(ROUTED, TOK)
+
+    g_send, g_keep, g_second, g_third, g_shared = grads
+    g_shared, over = lax.optimization_barrier((g_shared, over))
+
+    def shared_part(k):
+        return lax.dynamic_slice_in_dim(g_shared, (narrow ^ k) * D, D, 1)
+
+    shared_grad = jnp.concatenate(
+        [shared_part(0)] + [send(shared_part(k), NARROW_MOVES[k]) for k in (1, 2, 3)], axis=1
+    )
+
+    def back_x(z_, x_, y_, c_):
+        return (z_, 0, y_, c_) if x_ == 1 else None
+
+    def added(kept, other):
+        return (kept.astype(f32) + other.astype(f32)).astype(bf)
+
+    held_one = added(g_keep, send(g_send, to_x))
+    held_three = added(g_third, send(g_third, back_x))
+    held_two = added(
+        jnp.where(x == 0, g_second, shared_grad),
+        send(jnp.where(x == 0, shared_grad, g_second), to_x),
+    )
+    received = []
+    for held, owner in ((held_one, 0), (held_two, 2), (held_three, 3)):
+        for step in (1, 2, 3):
+
+            def move(z_, x_, y_, c_, owner=owner, step=step):
+                if (z_ + step) % 4 != owner or (owner == 3 and x_ == 1):
+                    return None
+                return (owner, x_, y_, c_)
+
+            received.append(send(held, move))
+
+    output = (
+        mid_state + (mixture.reshape(segments, SHORT, D) * gate_two).reshape(-1, D)
+    ).astype(bf)
+    d_gate_two = jnp.sum(grad_seg * mixture.reshape(segments, SHORT, D), axis=1)
+    d_logits = gates * (d_gates - jnp.sum(gates * d_gates, axis=0, keepdims=True))
+    d_logits = d_logits.astype(bf)
+    g_router = jnp.dot(d_logits, hidden_two, preferred_element_type=f32)
+    d_hidden = d_hidden + dot(d_logits, router_low, TN)
+    d_mid_norm, d_shift_two, d_scale_two = second_back(d_hidden.reshape(segments, SHORT, D))
+    d_mid = grad_out + d_mid_norm.reshape(-1, D)
+    d_mid_seg = d_mid.reshape(segments, SHORT, D)
+    d_gate_one = jnp.sum(d_mid_seg * attn_out.reshape(segments, SHORT, D), axis=1)
+    d_attn = (d_mid_seg * gate_one).reshape(-1, D).astype(bf)
+    g_out = dot(d_attn, attended, TN)
+    d_attended = jnp.dot(d_attn, out_map, preferred_element_type=f32).astype(bf)
+    d_heads = attend_back_fast(resolution, projected, log_total, d_attended)
+    g_qkv = jnp.stack([dot(d_head, hidden_one, TN) for d_head in d_heads])
+    d_hidden_one = sum(
+        jnp.dot(d_head, first_maps[j], preferred_element_type=f32)
+        for j, d_head in enumerate(d_heads)
+    )
+    d_rows_one, d_shift_one, d_scale_one = first_back(d_hidden_one.reshape(segments, SHORT, D))
+    grad_in = d_mid + d_rows_one.reshape(-1, D)
+    d_modulation = [
+        d_shift_one[:, 0],
+        d_scale_one[:, 0],
+        d_gate_one,
+        d_shift_two[:, 0],
+        d_scale_two[:, 0],
+        d_gate_two,
+    ]
+
+    dense = jnp.concatenate([g_qkv, g_out[None]]).reshape(2, 2, D, D)
+    dense = pick(dense, c, 1) + send(pick(dense, 1 - c, 1).astype(bf), to_core).astype(f32)
+    dense = pick(dense, y) + send(pick(dense, 1 - y).astype(bf), to_y).astype(f32)
+    dense = dense + send(dense.astype(bf), back_x).astype(f32)
+    dense_low = dense.astype(bf)
+    for step in (1, 2, 3):
+
+        def to_second(z_, x_, y_, c_, step=step):
+            return (1, x_, y_, c_) if (z_ + step) % 4 == 1 and x_ == 0 else None
+
+        dense = dense + send(dense_low, to_second).astype(f32)
+
+    cond_rows = cond_low.astype(f32)
+    ada_rows = [jnp.concatenate([d_mod, cond_rows]) for d_mod in d_modulation]
+    payload = jnp.zeros((8, 4, 8, D), f32)
+    payload = payload.at[3].set(jnp.stack(ada_rows[:4]))
+    payload = payload.at[7, :3].set(jnp.stack(ada_rows[4:] + [g_router]))
+    bias_part = jnp.concatenate([jnp.sum(d_mod, axis=0) for d_mod in d_modulation])
+    bias_part = jnp.pad(bias_part.reshape(8, 4, 1, 72), ((0, 0), (0, 0), (0, 7), (0, 56)))
+    small = jnp.concatenate([payload, bias_part], axis=3).reshape(32, 8, 512)
+    small = lax.all_to_all(small, AXES, 0, 0, tiled=True)
+    g_bias = jnp.sum(small[:, 0, D : D + 72], axis=0)
+    grad_full, grad_cut = owned_grad(
+        place_ids, (held_one, held_two, held_three), received, dense, small.reshape(256, 512)
+    )
+    grad_parts = lax.all_to_all(grad_cut, AXES, 0, 0, tiled=True)
+
+    state_bias = MOMENTUM_VECTOR * moment_bias + g_bias
+    part_sum = jnp.sum(state_bias * state_bias)
+    sum_high = part_sum.astype(bf)
+    sum_low = (part_sum - sum_high.astype(f32)).astype(bf)
+
+    extra = jnp.pad(jnp.stack([sum_high, sum_low])[None], ((0, 7), (0, D - 2)))
+    ortho_cut = ortho_owned(place_ids, grad_full, moments, extra)
+    ortho_parts = lax.all_to_all(ortho_cut, AXES, 0, 0, tiled=True)
+    square_total = jnp.sum(ortho_parts[:, 48, :2].astype(f32))
+
+    step_value = step_count[0].astype(f32)
+    decay = jnp.minimum(0.9999, (1.0 + step_value) / (10.0 + step_value))
+    weights = (turned(w_square), turned(w_out), w_router, turned(w_up), turned(w_down))
+    emas = (turned(ema_square), turned(ema_out), ema_router, turned(ema_up), turned(ema_down))
+    updated = update(decay[None], grad_parts, ortho_parts, weights, moment_parts, emas)
+    results = []
+    for which in range(5):
+        results += [
+            array if which == 2 else turned(array) for array in updated[which::5]
+        ]
+    root_mean = jnp.sqrt(square_total / (6 * D) + 1e-05)
+    master_bias = b_ada - RATE_VECTOR * state_bias / root_mean
+    average_bias = decay * ema_bias + (1.0 - decay) * master_bias
+    return (output, grad_in, *results, state_bias, master_bias, average_bias)
+
+
 def solution(mesh):
     placed = (
-        P(("wide", "narrow"), None),
-        P(("wide", "narrow"), None),
-        P(("wide", "narrow"), None),
-        P(("wide", "narrow")),
+        P((WIDE, NARROW), None),
+        P((WIDE, NARROW), None),
+        P((WIDE, NARROW), None),
+        P((WIDE, NARROW)),
         P(),
-        P(("wide", "narrow"), None),
-        P(None, "narrow", "wide"),
-        P("narrow", "wide"),
-        P("narrow", "wide"),
-        P(None, "narrow", "wide"),
-        P(None, "narrow", "wide"),
-        P(("wide", "narrow")),
-        P(None, "narrow", "wide"),
-        P("narrow", "wide"),
-        P("narrow", "wide"),
-        P(None, "narrow", "wide"),
-        P(None, "narrow", "wide"),
-        P(("wide", "narrow")),
-        P(None, "narrow", "wide"),
-        P("narrow", "wide"),
-        P("narrow", "wide"),
-        P(None, "narrow", "wide"),
-        P(None, "narrow", "wide"),
-        P(("wide", "narrow")),
-    )
+        P((WIDE, NARROW), None),
+        P(None, NARROW, WIDE),
+        P(NARROW, WIDE),
+        P(NARROW, WIDE),
+        P(None, NARROW, WIDE),
+        P(None, NARROW, WIDE),
+        P((WIDE, NARROW)),
+        P(None, NARROW, WIDE),
+        P(NARROW, WIDE),
+        P(NARROW, WIDE),
+        P(None, NARROW, WIDE),
+        P(None, NARROW, WIDE),
+        P((WIDE, NARROW)),
+        P(None, NARROW, WIDE),
+        P(NARROW, WIDE),
+        P(NARROW, WIDE),
+        P(None, NARROW, WIDE),
+        P(None, NARROW, WIDE),
+        P((WIDE, NARROW)),
+    )
+    device_body = fast_device if dict(mesh.shape) == {WIDE: 8, NARROW: 4} else on_device
     return jax.shard_map(
-        on_device,
+        device_body,
         mesh=mesh,
         in_specs=placed,
         out_specs=(
-            P(("wide", "narrow"), None),
-            P(("wide", "narrow"), None),
-            P(None, "narrow", "wide"),
-            P(None, "narrow", "wide"),
-            P(None, "narrow", "wide"),
-            P("narrow", "wide"),
-            P("narrow", "wide"),
-            P("narrow", "wide"),
-            P("narrow", "wide"),
-            P("narrow", "wide"),
-            P("narrow", "wide"),
-            P(None, "narrow", "wide"),
-            P(None, "narrow", "wide"),
-            P(None, "narrow", "wide"),
-            P(None, "narrow", "wide"),
-            P(None, "narrow", "wide"),
-            P(None, "narrow", "wide"),
-            P(("wide", "narrow")),
-            P(("wide", "narrow")),
-            P(("wide", "narrow")),
+            P((WIDE, NARROW), None),
+            P((WIDE, NARROW), None),
+            P(None, NARROW, WIDE),
+            P(None, NARROW, WIDE),
+            P(None, NARROW, WIDE),
+            P(NARROW, WIDE),
+            P(NARROW, WIDE),
+            P(NARROW, WIDE),
+            P(NARROW, WIDE),
+            P(NARROW, WIDE),
+            P(NARROW, WIDE),
+            P(None, NARROW, WIDE),
+            P(None, NARROW, WIDE),
+            P(None, NARROW, WIDE),
+            P(None, NARROW, WIDE),
+            P(None, NARROW, WIDE),
+            P(None, NARROW, WIDE),
+            P((WIDE, NARROW)),
+            P((WIDE, NARROW)),
+            P((WIDE, NARROW)),
         ),
         check_vma=False,
     )

time: 2700 us -> 726 us (0.27)
  waiting for transfers between devices: 1750 us -> 281 us
  matrix products: 315 us -> 12.2 us
  local copies, waits for them, and re-layouts: 213 us -> 33.8 us
  blocking collectives: 257 us -> 84.9 us
  Pallas kernels: 0 us -> 171 us
  starting transfers between devices: 7.68 us -> 84.6 us
  other arithmetic: 107 us -> 46 us
    reduce_scatter x6 -> x0, waiting for transfers between devices: 1320 us -> none  [the longest x1 609 us: on_device(): lax.psum_scatter(g_down, 'wide', scatter_dimension=2, tiled=True)]
    dot_general x44 -> x16, matrix products: 314 us -> 12.2 us  [the longest x10 8.96 us: dot(): return lax.dot_general(a, b, dims, preferred_element_type=f32)]
    ppermute x0 -> x52, waiting for transfers between devices: none -> 250 us  [send(): return lax.ppermute(array, AXES, route_pairs(move))]
    all_gather x5 -> x0, waiting for transfers between devices: 186 us -> none  [the longest x1 154 us: on_device(): lax.all_gather(row_pieces[4], 'wide', axis=2, tiled=True)]
    psum x5 -> x0, waiting for transfers between devices: 183 us -> none  [on_device(): lax.psum(jnp.einsum('mrc,mrd->mcd', current, current, precision=PRECISE)....]
    pallas_call x0 -> x7, Pallas kernels: none -> 171 us  [the longest x1 80.1 us: moe(): pl.pallas_call(partial(moe_kernel, RB=RB, FC=FC), out_shape=[jax.ShapeDty...]
    all_gather x5 -> x0, blocking collectives: 85.5 us -> none  [the longest x1 32 us: on_device(): lax.all_gather(row_pieces[1], 'wide', axis=1, tiled=True)]
    ppermute x0 -> x52, starting transfers between devices: none -> 70.7 us  [send(): return lax.ppermute(array, AXES, route_pairs(move))]
  transfers between devices with their start and end apart: 20 -> 55, of which waited for: 17 -> 22; matrix products, arithmetic and copies ran while one was open for 11% -> 10% of each run, Pallas kernels for 0% -> 8%
where the time goes in v1:
time: 726 us; the launch traced here: 720 us
  waiting for transfers between devices  281 us (39%)
  Pallas kernels  171 us (24%)
  blocking collectives  84.9 us (12%)
  starting transfers between devices  84.6 us (12%)
  other arithmetic  46 us (6%)
  local copies, waits for them, and re-layouts  33.8 us (5%)
  matrix products  12.2 us (2%)
    ppermute x52, waiting for transfers between devices, send(): return lax.ppermute(array, AXES, route_pairs(move))  250 us
    all_to_all x1, blocking collectives, fast_device(): ortho_parts = lax.all_to_all(ortho_cut, AXES, 0, 0, tiled=True)  84.9 us
    pallas_call x1, Pallas kernels, moe(): pl.pallas_call(partial(moe_kernel, RB=RB, FC=FC), out_shape=[jax.ShapeDty...  80.1 us
    ppermute x52, starting transfers between devices, send(): return lax.ppermute(array, AXES, route_pairs(move))  70.7 us
    pallas_call x1, Pallas kernels, ortho_owned(): pl.pallas_call(ortho_kernel, out_shape=jax.ShapeDtypeStruct((32, 56, D),...  30.7 us
    pallas_call x1, Pallas kernels, attend_back_fast(): pl.pallas_call(attend_back_kernel, grid_spec=pltpu.PrefetchScalarGridSpec...  26 us
    pallas_call x1, Pallas kernels, attend_fast(): pl.pallas_call(attend_kernel, grid_spec=pltpu.PrefetchScalarGridSpec(num_...  23 us
    all_to_all x1, waiting for transfers between devices, fast_device(): grad_parts = lax.all_to_all(grad_cut, AXES, 0, 0, tiled=True)  21.6 us
  transfers between devices with their start and end apart: 55, of which 22 were waited for; matrix products, arithmetic and copies ran while one was open for 10% of the time, Pallas kernels for 8%

profile of v1, /device:TPU:0, one launch (start us, length us, event | category | flops | bytes accessed | tf_op | source)
XLA Modules:
  0.0 720.2 jit_solution(1637154275390136080)
XLA Ops:
  24.9 5.9 collective-permute-done.8
  46.1 6.8 collective-permute-done.10
  59.5 4.5 collective-permute-start.23
  76.9 23.0 %attend_fast.1 = (bf16[1024,384]{1,0:T(8,128)(2,1)S(1)}, f32[3,8,1024]{2,1,0:T(8,128)S(1)}) custom-call(s32[1]{0:T(128)S(6)} %copy.99.res, bf16[1024,1152]{1,0:T(8,128)(2,1)S(1)} %convolution_convert_fusion.q_ref.k_ref.v_ref, bf16[1024,1152]{1,0:T(8,128)(2,1)S(1)} %convolution_convert_fusion.q_ref.k_ref.v_ref, ...), custom_call_target="tpu_custom_call" | custom-call | tf_op jit(solution)/shard_map/attend_fast/pallas_call | solution.py:568
  105.0 22.4 %collective-permute-done.22 = bf16[5,4,48,384]{3,2,1,0:T(8,128)(2,1)} collective-permute-done((bf16[5,4,48,384]{3,2,1,0:T(8,128)(2,1)}, bf16[5,4,48,384]{3,2,1,0:T(8,128)(2,1)}, u32[]{:S(2)}, u32[]{:S(2)}) %collective-permute-start.22) | collective-permute-done | bytes 737312 | tf_op jit(solution)/shard_map/ppermute | solution.py:912
  132.1 7.5 %collective-permute-done.13.t2 = bf16[1024,768]{1,0:T(8,128)(2,1)} collective-permute-done((bf16[1024,768]{1,0:T(8,128)(2,1)S(1)}, bf16[1024,768]{1,0:T(8,128)(2,1)}, u32[]{:S(2)}, u32[]{:S(2)}) %collective-permute-start.13) | collective-permute-done | bytes 1572896 | tf_op jit(solution)/shard_map/ppermute | solution.py:912
  148.3 48.1 %collective-permute-done.24.gb = bf16[4,5,4,48,384]{4,3,2,1,0:T(8,128)(2,1)} collective-permute-done((bf16[4,5,4,48,384]{4,3,2,1,0:T(8,128)(2,1)}, bf16[4,5,4,48,384]{4,3,2,1,0:T(8,128)(2,1)}, u32[]{:S(2)}, u32[]{:S(2)}) %collective-permute-start.24) | collective-permute-done | bytes 2949152 | tf_op jit(solution)/shard_map/ppermute | solution.py:912
  196.4 80.1 %moe.1 = (bf16[1024,768]{1,0:T(8,128)(2,1)}, bf16[1024,768]{1,0:T(8,128)(2,1)}, bf16[1024,768]{1,0:T(8,128)(2,1)}, bf16[1024,768]{1,0:T(8,128)(2,1)}, f32[4,8,10...) custom-call(s32[3]{0:T(128)} %pad_add_fusion.ids, ...), custom_call_target="tpu_custom_call" | custom-call | tf_op jit(solution)/shard_map/moe/pallas_call | solution.py:518
  277.1 4.6 collective-permute-done.26
  291.1 29.6 %collective-permute-done.30 = f32[2,1024]{1,0:T(2,128)S(1)} collective-permute-done((f32[2,1024]{1,0:T(2,128)S(1)}, f32[2,1024]{1,0:T(2,128)S(1)}, u32[]{:S(2)}, u32[]{:S(2)}) %collective-permute-start.30) | collective-permute-done | bytes 8224 | tf_op jit(solution)/shard_map/ppermute | solution.py:912
  334.3 26.0 %attend_back_fast.1 = (bf16[1024,384]{1,0:T(8,128)(2,1)S(1)}, bf16[1024,384]{1,0:T(8,128)(2,1)S(1)}, bf16[1024,384]{1,0:T(8,128)(2,1)S(1)}) custom-call(s32[1]{0:T(128)S(6)} %copy.99.res, bf16[1024,1152]{1,0:T(8,128)(2,1)S(1)} %copy-done.1, bf16[1024,1152]{1,0:T(8,128)(2,1)S(1)} %copy-done.1, bf16[1024,1152]{1,0:T(8,128)(2,1)S(1)} %copy-done.1, ...), custom_call_target="tpu_custom_call" | custom-call | tf_op jit(solution)/shard_map/attend_back_fast/pallas_call | solution.py:650
  367.9 7.2 %all-to-all-start = ((f32[32,8,512]{2,1,0:T(8,128)}), f32[32,8,512]{2,1,0:T(8,128)S(1)}, u32[]{:S(2)}, u32[]{:S(2)}) async-start(f32[32,8,512]{2,1,0:T(8,128)} %bitcast.369), calls=%async_computation | async-start | bytes 1048576 | tf_op jit(solution)/shard_map/all_to_all | solution.py:1211
  380.9 9.8 %all-to-all-done = f32[32,8,512]{2,1,0:T(8,128)S(1)} async-done(((f32[32,8,512]{2,1,0:T(8,128)}), f32[32,8,512]{2,1,0:T(8,128)S(1)}, u32[]{:S(2)}, u32[]{:S(2)}) %all-to-all-start) | async-done | bytes 524320 | tf_op jit(solution)/shard_map/all_to_all | solution.py:1211
  401.8 20.3 %collective-permute-done.34 = bf16[384,384]{1,0:T(8,128)(2,1)S(1)} collective-permute-done((bf16[384,384]{1,0:T(8,128)(2,1)S(1)}, bf16[384,384]{1,0:T(8,128)(2,1)S(1)}, u32[]{:S(2)}, u32[]{:S(2)}) %collective-permute-start.34) | collective-permute-done | bytes 294944 | tf_op jit(solution)/shard_map/ppermute | solution.py:912
  423.3 8.2 %collective-permute-done.33 = bf16[384,384]{1,0:T(8,128)(2,1)S(1)} collective-permute-done((bf16[384,384]{1,0:T(8,128)(2,1)S(1)}, bf16[384,384]{1,0:T(8,128)(2,1)S(1)}, u32[]{:S(2)}, u32[]{:S(2)}) %collective-permute-start.33) | collective-permute-done | bytes 294944 | tf_op jit(solution)/shard_map/ppermute | solution.py:912
  434.9 7.8 %collective-permute-done.47 = bf16[384,384]{1,0:T(8,128)(2,1)S(1)} collective-permute-done((bf16[384,384]{1,0:T(8,128)(2,1)S(1)}, bf16[384,384]{1,0:T(8,128)(2,1)S(1)}, u32[]{:S(2)}, u32[]{:S(2)}) %collective-permute-start.47) | collective-permute-done | bytes 294944 | tf_op jit(solution)/shard_map/ppermute | solution.py:912
  448.0 30.2 %collective-permute-done.48 = bf16[384,384]{1,0:T(8,128)(2,1)S(1)} collective-permute-done((bf16[384,384]{1,0:T(8,128)(2,1)S(1)}, bf16[384,384]{1,0:T(8,128)(2,1)S(1)}, u32[]{:S(2)}, u32[]{:S(2)}) %collective-permute-start.48) | collective-permute-done | bytes 294944 | tf_op jit(solution)/shard_map/ppermute | solution.py:912
  478.3 7.7 %collective-permute-start.45 = (bf16[384,1536]{1,0:T(8,128)(2,1)}, bf16[384,1536]{1,0:T(8,128)(2,1)}, u32[]{:S(2)}, u32[]{:S(2)}) collective-permute-start(bf16[384,1536]{1,0:T(8,128)(2,1)} %add_convert_fusion.1.refs_2_), channel_id=1, source_target_pairs={{0,24},{1,25},{2,26},{3,27}} | collective-permute-start | bytes 3538952 | tf_op jit(solution)/shard_map/ppermute | solution.py:912
  486.1 25.1 %collective-permute-done.39.refs_5_ = bf16[384,1536]{1,0:T(8,128)(2,1)S(1)} collective-permute-done((bf16[384,1536]{1,0:T(8,128)(2,1)S(1)}, bf16[384,1536]{1,0:T(8,128)(2,1)S(1)}, u32[]{:S(2)}, u32[]{:S(2)}) %collective-permute-start.39) | collective-permute-done | bytes 1179680 | tf_op jit(solution)/shard_map/ppermute | solution.py:912
  525.7 6.4 collective-permute-start.41
  539.1 16.8 %collective-permute-done.41.refs_7_ = bf16[384,1536]{1,0:T(8,128)(2,1)} collective-permute-done((bf16[384,1536]{1,0:T(8,128)(2,1)}, bf16[384,1536]{1,0:T(8,128)(2,1)}, u32[]{:S(2)}, u32[]{:S(2)}) %collective-permute-start.41) | collective-permute-done | bytes 1179680 | tf_op jit(solution)/shard_map/ppermute | solution.py:912
  564.1 30.7 %ortho_owned.1 = bf16[32,56,384]{2,1,0:T(8,128)(2,1)S(1)} custom-call(s32[3]{0:T(128)S(1)} %copy-done.26, f32[4,384,384]{2,1,0:T(8,128)S(1)} %copy-done.7, f32[32,48,384]{2,1,0:T(8,128)S(1)} %all-to-all-done.2.moment, bf16[8,384]{1,0:T(8,128)(2,1)S(1)} %pad.31.extra), custom_call_target="tpu_custom_call" | custom-call | tf_op jit(solution)/shard_map/ortho_owned/pallas_call | solution.py:847
  594.9 84.9 %all_to_all.20.orthos = bf16[32,56,384]{2,1,0:T(8,128)(2,1)} all-to-all(bf16[32,56,384]{2,1,0:T(8,128)(2,1)S(1)} %ortho_owned.1), channel_id=1, replica_groups=mesh['wide'=8,'narrow'=4] {'wide','narrow'}, dimensions={0} | all-to-all | bytes 2752512 | tf_op jit(solution)/shard_map/all_to_all | solution.py:1225
  690.8 21.6 %all-to-all-done.1.grads = bf16[32,48,384]{2,1,0:T(8,128)(2,1)} async-done(((bf16[32,48,384]{2,1,0:T(8,128)(2,1)}), bf16[32,48,384]{2,1,0:T(8,128)(2,1)}, u32[]{:S(2)}, u32[]{:S(2)}) %all-to-all-start.1) | async-done | bytes 1179680 | tf_op jit(solution)/shard_map/all_to_all | solution.py:1216
  (460 shorter events, 178.5 us)
Async XLA Ops:
  9.1 49.0 %collective-permute-start.20 = (bf16[4,48,384]{2,1,0:T(8,128)(2,1)S(1)}, bf16[4,48,384]{2,1,0:T(8,128)(2,1)S(1)}, u32[]{:S(2)}, u32[]{:S(2)}) collective-permute-start(bf16[4,48,384]{2,1,0:T(8,128)(2,1)S(1)} %get-tuple-element.157), channel_id=1, source_target_pairs={{0,3},{1,2},{2,1},{3,0},{4,7},{5,6},{6,5},{7,4},{8,11},{9,10},{10,... | collective-permute-start | bytes 442376 | tf_op jit(solution)/shard_map/ppermute | solution.py:912
  9.1 48.3 %collective-permute-start.19 = (bf16[4,48,384]{2,1,0:T(8,128)(2,1)S(1)}, bf16[4,48,384]{2,1,0:T(8,128)(2,1)S(1)}, u32[]{:S(2)}, u32[]{:S(2)}) collective-permute-start(bf16[4,48,384]{2,1,0:T(8,128)(2,1)S(1)} %get-tuple-element.158), channel_id=1, source_target_pairs={{0,2},{1,3},{2,0},{3,1},{4,6},{5,7},{6,4},{7,5},{8,10},{9,11},{10,... | collective-permute-start | bytes 442376 | tf_op jit(solution)/shard_map/ppermute | solution.py:912
  10.3 35.1 %collective-permute-start.18 = (bf16[4,48,384]{2,1,0:T(8,128)(2,1)S(1)}, bf16[4,48,384]{2,1,0:T(8,128)(2,1)S(1)}, u32[]{:S(2)}, u32[]{:S(2)}) collective-permute-start(bf16[4,48,384]{2,1,0:T(8,128)(2,1)S(1)} %get-tuple-element.159), channel_id=1, source_target_pairs={{0,1},{1,0},{2,3},{3,2},{4,5},{5,4},{6,7},{7,6},{8,9},{9,8},{10,11... | collective-permute-start | bytes 442376 | tf_op jit(solution)/shard_map/ppermute | solution.py:912
  59.5 45.6 %collective-permute-start.23 = (bf16[5,4,48,384]{3,2,1,0:T(8,128)(2,1)}, bf16[5,4,48,384]{3,2,1,0:T(8,128)(2,1)}, u32[]{:S(2)}, u32[]{:S(2)}) collective-permute-start(bf16[5,4,48,384]{3,2,1,0:T(8,128)(2,1)} %bitcast_dynamic-update-slice_fusion), channel_id=1, source_target_pairs={{0,24},{1,25},{2,26},{3,27},{4,28},{5,29},{6,30},{7,31},{8,0},{9,1... | collective-permute-start | bytes 2211848 | tf_op jit(solution)/shard_map/ppermute | solution.py:912
  63.9 63.5 %collective-permute-start.22 = (bf16[5,4,48,384]{3,2,1,0:T(8,128)(2,1)}, bf16[5,4,48,384]{3,2,1,0:T(8,128)(2,1)}, u32[]{:S(2)}, u32[]{:S(2)}) collective-permute-start(bf16[5,4,48,384]{3,2,1,0:T(8,128)(2,1)} %bitcast_dynamic-update-slice_fusion), channel_id=1, source_target_pairs={{0,16},{1,17},{2,18},{3,19},{4,20},{5,21},{6,22},{7,23},{8,24},{9,... | collective-permute-start | bytes 2211848 | tf_op jit(solution)/shard_map/ppermute | solution.py:912
  63.9 63.5 %collective-permute-start.21 = (bf16[5,4,48,384]{3,2,1,0:T(8,128)(2,1)}, bf16[5,4,48,384]{3,2,1,0:T(8,128)(2,1)}, u32[]{:S(2)}, u32[]{:S(2)}) collective-permute-start(bf16[5,4,48,384]{3,2,1,0:T(8,128)(2,1)} %bitcast_dynamic-update-slice_fusion), channel_id=1, source_target_pairs={{0,8},{1,9},{2,10},{3,11},{4,12},{5,13},{6,14},{7,15},{8,16},{9,17... | collective-permute-start | bytes 2211848 | tf_op jit(solution)/shard_map/ppermute | solution.py:912
  104.1 35.6 %collective-permute-start.13 = (bf16[1024,768]{1,0:T(8,128)(2,1)S(1)}, bf16[1024,768]{1,0:T(8,128)(2,1)}, u32[]{:S(2)}, u32[]{:S(2)}) collective-permute-start(bf16[1024,768]{1,0:T(8,128)(2,1)S(1)} %pad_maximum_fusion.2.t0), channel_id=1, source_target_pairs={{0,2},{1,3},{2,0},{3,1},{4,6},{5,7},{6,4},{7,5},{8,10},{9,11},{10,... | collective-permute-start | bytes 4718600 | tf_op jit(solution)/shard_map/ppermute | solution.py:912
  130.6 65.8 %collective-permute-start.24 = (bf16[4,5,4,48,384]{4,3,2,1,0:T(8,128)(2,1)}, bf16[4,5,4,48,384]{4,3,2,1,0:T(8,128)(2,1)}, u32[]{:S(2)}, u32[]{:S(2)}) collective-permute-start(bf16[4,5,4,48,384]{4,3,2,1,0:T(8,128)(2,1)} %pad_maximum_fusion.ga), channel_id=1, source_target_pairs={{0,4},{1,5},{2,6},{3,7},{4,0},{5,1},{6,2},{7,3},{8,12},{9,13},{10,... | collective-permute-start | bytes 8847368 | tf_op jit(solution)/shard_map/ppermute | solution.py:912
  139.6 56.8 %collective-permute-start.14 = (bf16[1024,768]{1,0:T(8,128)(2,1)}, bf16[1024,768]{1,0:T(8,128)(2,1)}, u32[]{:S(2)}, u32[]{:S(2)}) collective-permute-start(bf16[1024,768]{1,0:T(8,128)(2,1)} %collective-permute-done.13.t2), channel_id=1, source_target_pairs={{0,1},{1,0},{2,3},{3,2},{4,5},{5,4},{6,7},{7,6},{8,9},{9,8},{10,11... | collective-permute-start | bytes 4718600 | tf_op jit(solution)/shard_map/ppermute | solution.py:912
  276.6 46.6 %collective-permute-start.25 = (bf16[1024,768]{1,0:T(8,128)(2,1)}, bf16[1024,768]{1,0:T(8,128)(2,1)}, u32[]{:S(2)}, u32[]{:S(2)}) collective-permute-start(bf16[1024,768]{1,0:T(8,128)(2,1)} %get-tuple-element.82), channel_id=1, source_target_pairs={{0,1},{1,0},{2,3},{3,2},{4,5},{5,4},{6,7},{7,6},{8,9},{9,8},{10,11... | collective-permute-start | bytes 4718600 | tf_op jit(solution)/shard_map/ppermute | solution.py:912
  284.7 38.5 %collective-permute-start.27 = (bf16[1024,768]{1,0:T(8,128)(2,1)}, bf16[1024,768]{1,0:T(8,128)(2,1)}, u32[]{:S(2)}, u32[]{:S(2)}) collective-permute-start(bf16[1024,768]{1,0:T(8,128)(2,1)} %add_convert_fusion), channel_id=1, source_target_pairs={{0,2},{1,3},{2,0},{3,1},{4,6},{5,7},{6,4},{7,5},{8,10},{9,11},{10,... | collective-permute-start | bytes 4718600 | tf_op jit(solution)/shard_map/ppermute | solution.py:912
  286.6 34.2 %collective-permute-start.30 = (f32[2,1024]{1,0:T(2,128)S(1)}, f32[2,1024]{1,0:T(2,128)S(1)}, u32[]{:S(2)}, u32[]{:S(2)}) collective-permute-start(f32[2,1024]{1,0:T(2,128)S(1)} %get-tuple-element.174), channel_id=1, source_target_pairs={{0,3},{1,2},{2,1},{3,0},{4,7},{5,6},{6,5},{7,4},{8,11},{9,10},{10,... | collective-permute-start | bytes 24584 | tf_op jit(solution)/shard_map/ppermute | solution.py:912
  287.8 34.2 %collective-permute-start.29 = (f32[2,1024]{1,0:T(2,128)S(1)}, f32[2,1024]{1,0:T(2,128)S(1)}, u32[]{:S(2)}, u32[]{:S(2)}) collective-permute-start(f32[2,1024]{1,0:T(2,128)S(1)} %get-tuple-element.175), channel_id=1, source_target_pairs={{0,2},{1,3},{2,0},{3,1},{4,6},{5,7},{6,4},{7,5},{8,10},{9,11},{10,... | collective-permute-start | bytes 24584 | tf_op jit(solution)/shard_map/ppermute | solution.py:912
  289.7 104.9 %collective-permute-start.31 = (bf16[384,1536]{1,0:T(8,128)(2,1)}, bf16[384,1536]{1,0:T(8,128)(2,1)}, u32[]{:S(2)}, u32[]{:S(2)}) collective-permute-start(bf16[384,1536]{1,0:T(8,128)(2,1)} %get-tuple-element.91), channel_id=1, source_target_pairs={{0,4},{1,5},{2,6},{3,7},{4,0},{5,1},{6,2},{7,3},{8,12},{9,13},{10,... | collective-permute-start | bytes 3538952 | tf_op jit(solution)/shard_map/ppermute | solution.py:912
  320.7 123.4 %collective-permute-start.36 = (bf16[384,1536]{1,0:T(8,128)(2,1)}, bf16[384,1536]{1,0:T(8,128)(2,1)}, u32[]{:S(2)}, u32[]{:S(2)}) collective-permute-start(bf16[384,1536]{1,0:T(8,128)(2,1)} %get-tuple-element.95), channel_id=1, source_target_pairs={{4,0},{5,1},{6,2},{7,3},{12,8},{13,9},{14,10},{15,11},{20,16},{21,... | collective-permute-start | bytes 3538952 | tf_op jit(solution)/shard_map/ppermute | solution.py:912
  391.5 171.0 %all-to-all-start.2 = ((f32[32,48,384]{2,1,0:T(8,128)}), f32[32,48,384]{2,1,0:T(8,128)S(1)}, u32[]{:S(2)}, u32[]{:S(2)}) async-start(f32[32,48,384]{2,1,0:T(8,128)} %pack_owned.1), calls=%async_computation.2 | async-start | bytes 4718592 | tf_op jit(solution)/shard_map/all_to_all | solution.py:1110
  396.6 114.7 %collective-permute-start.39 = (bf16[384,1536]{1,0:T(8,128)(2,1)S(1)}, bf16[384,1536]{1,0:T(8,128)(2,1)S(1)}, u32[]{:S(2)}, u32[]{:S(2)}) collective-permute-start(bf16[384,1536]{1,0:T(8,128)(2,1)S(1)} %add_convert_fusion.3.refs_0_), channel_id=1, source_target_pairs={{8,0},{9,1},{10,2},{11,3},{12,4},{13,5},{14,6},{15,7}} | collective-permute-start | bytes 3538952 | tf_op jit(solution)/shard_map/ppermute | solution.py:912
  400.4 32.4 %collective-permute-start.32 = (bf16[384,384]{1,0:T(8,128)(2,1)S(1)}, bf16[384,384]{1,0:T(8,128)(2,1)S(1)}, u32[]{:S(2)}, u32[]{:S(2)}) collective-permute-start(bf16[384,384]{1,0:T(8,128)(2,1)S(1)} %get-tuple-element.152), channel_id=1, source_target_pairs={{0,1},{1,0},{2,3},{3,2},{4,5},{5,4},{6,7},{7,6},{8,9},{9,8},{10,11... | collective-permute-start | bytes 884744 | tf_op jit(solution)/shard_map/ppermute | solution.py:912
  422.1 91.6 %collective-permute-start.38 = (bf16[384,1536]{1,0:T(8,128)(2,1)S(1)}, bf16[384,1536]{1,0:T(8,128)(2,1)S(1)}, u32[]{:S(2)}, u32[]{:S(2)}) collective-permute-start(bf16[384,1536]{1,0:T(8,128)(2,1)S(1)} %add_convert_fusion.3.refs_0_), channel_id=1, source_target_pairs={{16,0},{17,1},{18,2},{19,3},{20,4},{21,5},{22,6},{23,7}} | collective-permute-start | bytes 3538952 | tf_op jit(solution)/shard_map/ppermute | solution.py:912
  431.5 88.1 %collective-permute-start.37 = (bf16[384,1536]{1,0:T(8,128)(2,1)S(1)}, bf16[384,1536]{1,0:T(8,128)(2,1)S(1)}, u32[]{:S(2)}, u32[]{:S(2)}) collective-permute-start(bf16[384,1536]{1,0:T(8,128)(2,1)S(1)} %add_convert_fusion.3.refs_0_), channel_id=1, source_target_pairs={{24,0},{25,1},{26,2},{27,3},{28,4},{29,5},{30,6},{31,7}} | collective-permute-start | bytes 3538952 | tf_op jit(solution)/shard_map/ppermute | solution.py:912
  442.7 73.5 %collective-permute-start.35 = (bf16[384,1536]{1,0:T(8,128)(2,1)S(1)}, bf16[384,1536]{1,0:T(8,128)(2,1)S(1)}, u32[]{:S(2)}, u32[]{:S(2)}) collective-permute-start(bf16[384,1536]{1,0:T(8,128)(2,1)S(1)} %broadcast_select_fusion), channel_id=1, source_target_pairs={{0,4},{1,5},{2,6},{3,7},{4,0},{5,1},{6,2},{7,3},{8,12},{9,13},{10,... | collective-permute-start | bytes 3538952 | tf_op jit(solution)/shard_map/ppermute | solution.py:912
  444.2 34.1 %collective-permute-start.48 = (bf16[384,384]{1,0:T(8,128)(2,1)S(1)}, bf16[384,384]{1,0:T(8,128)(2,1)S(1)}, u32[]{:S(2)}, u32[]{:S(2)}) collective-permute-start(bf16[384,384]{1,0:T(8,128)(2,1)S(1)} %fusion.20), channel_id=1, source_target_pairs={{4,0},{5,1},{6,2},{7,3},{12,8},{13,9},{14,10},{15,11},{20,16},{21,... | collective-permute-start | bytes 884744 | tf_op jit(solution)/shard_map/ppermute | solution.py:912
  478.3 44.0 %collective-permute-start.45 = (bf16[384,1536]{1,0:T(8,128)(2,1)}, bf16[384,1536]{1,0:T(8,128)(2,1)}, u32[]{:S(2)}, u32[]{:S(2)}) collective-permute-start(bf16[384,1536]{1,0:T(8,128)(2,1)} %add_convert_fusion.1.refs_2_), channel_id=1, source_target_pairs={{0,24},{1,25},{2,26},{3,27}} | collective-permute-start | bytes 3538952 | tf_op jit(solution)/shard_map/ppermute | solution.py:912
  679.8 32.6 %all-to-all-start.1 = ((bf16[32,48,384]{2,1,0:T(8,128)(2,1)}), bf16[32,48,384]{2,1,0:T(8,128)(2,1)}, u32[]{:S(2)}, u32[]{:S(2)}) async-start(bf16[32,48,384]{2,1,0:T(8,128)(2,1)} %get-tuple-element.96), calls=%async_computation.1 | async-start | bytes 2359296 | tf_op jit(solution)/shard_map/all_to_all | solution.py:1216
  (126 other events, 2550.4 us)

commit v2 on v1

--- a/solution.py
+++ b/solution.py
@@ -413,121 +413,231 @@
 bf = jnp.bfloat16
 f32 = jnp.float32
 TOK = 1024
-NN=(((1,),(0,)),((),())); NT=(((1,),(1,)),((),())); TN=(((0,),(0,)),((),()))
-def dot(a,b,dims=NN): return lax.dot_general(a,b,dims,preferred_element_type=f32)
-
-def gelu_pair(v):
-    sq=v*v
-    th=jnp.tanh(v*(0.7978845608028654+0.035677408136300125*sq))
-    half=0.5*th+0.5
-    act=v*half
-    slope=half+act*(1.0-half)*(1.5957691216057308+0.21406444881780075*sq)
-    return act,slope
-
-def moe_kernel(ids, t0,t1,t2,t3,m0,m1,m2,m3,ga,gb, p0,p1,p2,p3,dg_out,g_send,g_keep,g_b1,g_b2,g_sh,
-               tok,meta,up,dn,ups,dns,gup,gdn,gups,gdns,acc,part,dgs,gst,tsem,wsem,osem,gsem, *, RB, FC):
-    n=ids[0]; z=ids[1]; x=ids[2]
-    tin=(t0,t1,t2,t3); mins=(m0,m1,m2,m3)
-    tcop=[pltpu.make_async_copy(tin[i],tok.at[i],tsem.at[i,0]) for i in range(4)]
-    mcop=[pltpu.make_async_copy(mins[i],meta.at[i],tsem.at[i,1]) for i in range(4)]
-    tcop[0].start(); mcop[0].start()
-    wc=[]
-    for src,xx in ((ga,x),(gb,1-x)):
-        for d in range(4):
-            row=pl.multiple_of((2*lax.rem(z-d+4,4)+xx)*48,16)
-            for m in range(4):
-                tgt=(ups,dns)[m%2]
-                wc.append(pltpu.make_async_copy(src.at[d,4,m],tgt.at[pl.ds(row,48),pl.ds((m//2)*384,384)],wsem.at[0]))
+ROWS = 512
+UNITS = 512
+NN = (((1,), (0,)), ((), ()))
+NT = (((1,), (1,)), ((), ()))
+TN = (((0,), (0,)), ((), ()))
+
+
+def dot(a, b, dims=NN):
+    return lax.dot_general(a, b, dims, preferred_element_type=f32)
+
+
+def gelu_pair(pre):
+    sq = pre * pre
+    th = jnp.tanh(pre * (0.7978845608028654 + 0.035677408136300125 * sq))
+    half = 0.5 * th + 0.5
+    act = pre * half
+    slope = half + act * (1.0 - half) * (1.5957691216057308 + 0.21406444881780075 * sq)
+    return act, slope
+
+
+def moe_kernel(last, ids, *refs):
+    hidden, d_mix, metas = refs[0:2], refs[2:4], refs[4:6]
+    gathered = refs[6]
+    prior = refs[7:12] if last else ()
+    refs = refs[7 + len(prior) :]
+    part_out, d_gate_out, refs = refs[0:2], refs[2], refs[3:]
+    grads = refs[: 6 if last else 5]
+    refs = refs[len(grads) :]
+    tok, meta, up, down, up_s, down_s, g_up, g_down, g_up_s, g_down_s = refs[:10]
+    acc, part, d_gate, stage, tok_sem, w_sem, out_sem, g_sem = refs[10:]
+    n, x = ids[0], ids[2]
+
+    def token_copies(i):
+        return [
+            pltpu.make_async_copy(hidden[i], tok.at[i, :, pl.ds(0, D)], tok_sem.at[i, 0]),
+            pltpu.make_async_copy(d_mix[i], tok.at[i, :, pl.ds(D, D)], tok_sem.at[i, 1]),
+            pltpu.make_async_copy(metas[i], meta.at[i], tok_sem.at[i, 2]),
+        ]
+
+    for copy in token_copies(0):
+        copy.start()
+    loads = []
+    for w in range(8):
+        rows = pl.ds(48 * w, 48)
+        for e in range(2):
+            for m, whole, shared in ((0, up, up_s), (1, down, down_s)):
+                slot = 2 * e + m
+                loads.append((gathered.at[w, 4, slot], shared.at[rows, pl.ds(e * D, D)]))
                 for k in range(4):
-                    tgt=(up,dn)[m%2]
-                    wc.append(pltpu.make_async_copy(src.at[d,k,m],tgt.at[m//2,pl.ds(row,48),pl.ds(k*384,384)],wsem.at[1]))
-    for c in wc: c.start()
-    for i in range(1,4): tcop[i].start(); mcop[i].start()
-    gup[...]=jnp.zeros_like(gup); gdn[...]=jnp.zeros_like(gdn); gups[...]=jnp.zeros_like(gups); gdns[...]=jnp.zeros_like(gdns)
-    for c in wc: c.wait()
-
-    def per_src(s,_):
-        pltpu.make_async_copy(t0,tok.at[s],tsem.at[s,0]).wait()
-        pltpu.make_async_copy(m0,meta.at[s],tsem.at[s,1]).wait()
-        def shared(r,_):
-            rows=pl.ds(pl.multiple_of(r*RB,RB),RB)
-            xs=tok[s,rows,:D]; ds=tok[s,rows,D:]
-            out=jnp.zeros((RB,D),f32); dx=jnp.zeros((RB,D),f32)
-            for f in range(0,768,FC):
-                fs=slice(f,f+FC)
-                pre=dot(xs,ups[:,fs]); da=dot(ds,dns[:,fs])
-                act,slope=gelu_pair(pre)
-                ab=act.astype(bf); pb=(slope*da).astype(bf)
-                out=out+dot(ab,dns[:,fs],NT); dx=dx+dot(pb,ups[:,fs],NT)
-                gups[:,fs]+=dot(xs,pb,TN); gdns[:,fs]+=dot(ds,ab,TN)
-            acc[rows,:D]=out; acc[rows,D:]=dx
-            return 0
-        lax.fori_loop(0,TOK//RB,shared,0)
-        def routed(e,_):
-            ex=2*n+e
-            pos=meta[s,pl.ds(ex,1),:]; gat=meta[s,pl.ds(8+ex,1),:]
-            slot=lax.broadcasted_iota(jnp.int32,(CAP,TOK),0).astype(f32)
-            hit=slot==pos
-            hot=hit.astype(f32).astype(bf)
-            gsl=jnp.sum(jnp.where(hit,gat,0.0),axis=1,keepdims=True)
-            xd=dot(hot,tok[s])
-            xs=xd[:,:D].astype(bf); dmx=xd[:,D:]
-            ds=(dmx*gsl).astype(bf)
-            out=jnp.zeros((CAP,D),f32); dx=jnp.zeros((CAP,D),f32)
-            for f in range(0,FF,FC):
-                fs=slice(f,f+FC)
-                pre=dot(xs,up[e,:,fs]); da=dot(ds,dn[e,:,fs])
-                act,slope=gelu_pair(pre)
-                ab=act.astype(bf); pb=(slope*da).astype(bf)
-                out=out+dot(ab,dn[e,:,fs],NT); dx=dx+dot(pb,up[e,:,fs],NT)
-                gup[e,:,fs]+=dot(xs,pb,TN); gdn[e,:,fs]+=dot(ds,ab,TN)
-            dgate=jnp.sum(out*dmx,axis=1,keepdims=True)
-            dgs[s,pl.ds(e,1),:]=jnp.sum(jnp.where(hit,dgate,0.0),axis=0,keepdims=True)
-            both=jnp.concatenate([(out*gsl).astype(bf),dx.astype(bf)],axis=1)
-            acc[...]+=dot(hot,both,TN)
-            return 0
-        lax.fori_loop(0,2,routed,0)
-        part[s]=acc[...].astype(bf)
-        for i,dst in enumerate((p0,p1,p2,p3)):
-            @pl.when(s==i)
+                    target = whole.at[e, rows, pl.ds(k * D, D)]
+                    loads.append((gathered.at[w, k, slot], target))
+    loads = [pltpu.make_async_copy(source, target, w_sem.at[0]) for source, target in loads]
+    for copy in loads:
+        copy.start()
+    for copy in token_copies(1):
+        copy.start()
+    carried = [
+        pltpu.make_async_copy(source, stage.at[i], g_sem.at[i]) for i, source in enumerate(prior)
+    ]
+    for copy in carried:
+        copy.start()
+    if last:
+        for copy in carried:
+            copy.wait()
+        for e in range(2):
+            g_up[e] = stage[2 * e].astype(f32)
+            g_down[e] = stage[2 * e + 1].astype(f32)
+            g_up_s[:, e * D : e * D + D] = stage[4, :, 2 * e * D : 2 * e * D + D].astype(f32)
+            g_down_s[:, e * D : e * D + D] = stage[
+                4, :, 2 * e * D + D : 2 * e * D + 2 * D
+            ].astype(f32)
+    else:
+        for total in (g_up, g_down, g_up_s, g_down_s):
+            total[...] = jnp.zeros_like(total)
+    for copy in loads:
+        copy.wait()
+    for i in range(2):
+        for copy in token_copies(i):
+            copy.wait()
+
+    def units(xs, ds, up_ref, down_ref, g_up_ref, g_down_ref, count):
+        out = jnp.zeros(xs.shape, f32)
+        dx = jnp.zeros(xs.shape, f32)
+        for first in range(0, count, UNITS):
+            lanes = slice(first, min(first + UNITS, count))
+            act, slope = gelu_pair(dot(xs, up_ref[:, lanes]))
+            act = act.astype(bf)
+            d_pre = (slope * dot(ds, down_ref[:, lanes])).astype(bf)
+            out = out + dot(act, down_ref[:, lanes], NT)
+            dx = dx + dot(d_pre, up_ref[:, lanes], NT)
+            g_up_ref[:, lanes] += dot(xs, d_pre, TN)
+            g_down_ref[:, lanes] += dot(ds, act, TN)
+        return out, dx
+
+    def one_source(s, carry):
+        def shared(r, carry):
+            rows = pl.ds(pl.multiple_of(r * ROWS, ROWS), ROWS)
+            out, dx = units(
+                tok[s, rows, :D], tok[s, rows, D:], up_s, down_s, g_up_s, g_down_s, 2 * D
+            )
+            acc[rows, :D] = out
+            acc[rows, D:] = dx
+            return carry
+
+        lax.fori_loop(0, TOK // ROWS, shared, 0)
+
+        def routed(e, carry):
+            place = meta[s, pl.ds(2 * n + e, 1), :]
+            gate = meta[s, pl.ds(8 + 2 * n + e, 1), :]
+            slot = lax.broadcasted_iota(jnp.int32, (CAP, TOK), 0).astype(f32)
+            hit = slot == place
+            hot = hit.astype(f32).astype(bf)
+            gates = jnp.sum(jnp.where(hit, gate, 0.0), axis=1, keepdims=True)
+            rows = dot(hot, tok[s])
+            d_rows = rows[:, D:]
+            out, dx = units(
+                rows[:, :D].astype(bf),
+                (d_rows * gates).astype(bf),
+                up.at[e],
+                down.at[e],
+                g_up.at[e],
+                g_down.at[e],
+                FF,
+            )
+            d_slot = jnp.sum(out * d_rows, axis=1, keepdims=True)
+            d_gate[s, pl.ds(e, 1), :] = jnp.sum(
+                jnp.where(hit, d_slot, 0.0), axis=0, keepdims=True
+            )
+            both = jnp.concatenate([(out * gates).astype(bf), dx.astype(bf)], axis=1)
+            acc[...] += dot(hot, both, TN)
+            return carry
+
+        lax.fori_loop(0, 2, routed, 0)
+        part[s] = acc[...].astype(bf)
+        for i in range(2):
+
+            @pl.when(s == i)
             def _():
-                pltpu.make_async_copy(part.at[i],dst,osem.at[i]).start()
-        return 0
-    lax.fori_loop(0,4,per_src,0)
-    outs=[pltpu.make_async_copy(part.at[i],dst,osem.at[i]) for i,dst in enumerate((p0,p1,p2,p3))]
-    cd=pltpu.make_async_copy(dgs,dg_out,osem.at[4]); cd.start(); outs.append(cd)
-    def to(slot,dst): return pltpu.make_async_copy(gst.at[slot],dst,gsem.at[slot])
+                pltpu.make_async_copy(part.at[i], part_out[i], out_sem.at[i]).start()
+
+        return carry
+
+    lax.fori_loop(0, 2, one_source, 0)
+    gate_copy = pltpu.make_async_copy(d_gate, d_gate_out, out_sem.at[2])
+    gate_copy.start()
     for e in range(2):
-        for m,src in ((0,gup),(1,gdn)):
-            gst[2*e+m]=src[e].astype(bf)
-    for sh in range(2):
-        for m,src in ((0,gups),(1,gdns)):
-            gst[4,:,pl.ds((2*sh+m)*384,384)]=src[:,sh*384:(sh+1)*384].astype(bf)
-    @pl.when(x==0)
-    def _():
-        to(0,g_keep).start(); to(3,g_send).start()
-    @pl.when(x!=0)
-    def _():
-        to(0,g_send).start(); to(3,g_keep).start()
-    to(1,g_b1).start(); to(2,g_b2).start(); to(4,g_sh).start()
-    for slot,dst in ((0,g_keep),(3,g_send),(1,g_b1),(2,g_b2),(4,g_sh)): to(slot,dst).wait()
-    for c in outs: c.wait()
-
-def moe(ids,toks,metas,ga,gb,RB=512,FC=512):
-    anyspec=pl.BlockSpec(memory_space=pl.ANY)
+        stage[2 * e] = g_up[e].astype(bf)
+        stage[2 * e + 1] = g_down[e].astype(bf)
+        stage[4, :, 2 * e * D : 2 * e * D + D] = g_up_s[:, e * D : e * D + D].astype(bf)
+        stage[4, :, 2 * e * D + D : 2 * e * D + 2 * D] = g_down_s[
+            :, e * D : e * D + D
+        ].astype(bf)
+
+    def store(slot, target, sem):
+        return pltpu.make_async_copy(slot, target, g_sem.at[sem])
+
+    if last:
+        g_send, g_keep, g_second, g_left, g_right, g_shared = grads
+
+        @pl.when(x == 0)
+        def _():
+            store(stage.at[0], g_keep, 0).start()
+            store(stage.at[3], g_send, 1).start()
+
+        @pl.when(x != 0)
+        def _():
+            store(stage.at[3], g_keep, 0).start()
+            store(stage.at[0], g_send, 1).start()
+
+        rest = [
+            store(stage.at[1], g_second, 2),
+            store(stage.at[2, :, pl.ds(0, FF // 2)], g_left, 3),
+            store(stage.at[2, :, pl.ds(FF // 2, FF // 2)], g_right, 5),
+            store(stage.at[4], g_shared, 4),
+        ]
+        for copy in rest:
+            copy.start()
+        rest += [store(stage.at[0], g_keep, 0), store(stage.at[3], g_send, 1)]
+    else:
+        rest = [store(stage.at[i], grads[i], i) for i in range(5)]
+        for copy in rest:
+            copy.start()
+    for copy in rest:
+        copy.wait()
+    for i in range(2):
+        pltpu.make_async_copy(part.at[i], part_out[i], out_sem.at[i]).wait()
+    gate_copy.wait()
+
+
+def moe(ids, hidden, d_mix, metas, gathered, prior=()):
+    last = len(prior) > 0
+    anyspec = pl.BlockSpec(memory_space=pl.ANY)
+    whole = jax.ShapeDtypeStruct((D, FF), bf)
+    half = jax.ShapeDtypeStruct((D, FF // 2), bf)
+    grads = [whole, whole, whole, half, half, whole] if last else [whole] * 5
+    shapes = [jax.ShapeDtypeStruct((TOK, 2 * D), bf)] * 2
+    shapes += [jax.ShapeDtypeStruct((2, 8, TOK), f32)] + grads
     return pl.pallas_call(
-        partial(moe_kernel,RB=RB,FC=FC),
-        out_shape=[jax.ShapeDtypeStruct((TOK,2*D),bf)]*4+[jax.ShapeDtypeStruct((4,8,TOK),f32)]+[jax.ShapeDtypeStruct((D,FF),bf)]*5,
-        in_specs=[pl.BlockSpec(memory_space=pltpu.SMEM)]+[anyspec]*10,
-        out_specs=[anyspec]*10,
-        scratch_shapes=[pltpu.VMEM((4,TOK,2*D),bf),pltpu.VMEM((4,16,TOK),f32),
-            pltpu.VMEM((2,D,FF),bf),pltpu.VMEM((2,D,FF),bf),pltpu.VMEM((D,768),bf),pltpu.VMEM((D,768),bf),
-            pltpu.VMEM((2,D,FF),f32),pltpu.VMEM((2,D,FF),f32),pltpu.VMEM((D,768),f32),pltpu.VMEM((D,768),f32),
-            pltpu.VMEM((TOK,2*D),f32),pltpu.VMEM((4,TOK,2*D),bf),pltpu.VMEM((4,8,TOK),f32),pltpu.VMEM((5,D,FF),bf),
-            pltpu.SemaphoreType.DMA((4,2)),pltpu.SemaphoreType.DMA((2,)),pltpu.SemaphoreType.DMA((5,)),pltpu.SemaphoreType.DMA((5,))],
-        compiler_params=pltpu.CompilerParams(vmem_limit_bytes=63*1024*1024),
-        name="moe",
-    )(ids,*toks,*metas,ga,gb)
+        partial(moe_kernel, last),
+        out_shape=shapes,
+        in_specs=[pl.BlockSpec(memory_space=pltpu.SMEM)] + [anyspec] * (7 + len(prior)),
+        out_specs=[anyspec] * len(shapes),
+        scratch_shapes=[
+            pltpu.VMEM((2, TOK, 2 * D), bf),
+            pltpu.VMEM((2, 16, TOK), f32),
+            pltpu.VMEM((2, D, FF), bf),
+            pltpu.VMEM((2, D, FF), bf),
+            pltpu.VMEM((D, 2 * D), bf),
+            pltpu.VMEM((D, 2 * D), bf),
+            pltpu.VMEM((2, D, FF), f32),
+            pltpu.VMEM((2, D, FF), f32),
+            pltpu.VMEM((D, 2 * D), f32),
+            pltpu.VMEM((D, 2 * D), f32),
+            pltpu.VMEM((TOK, 2 * D), f32),
+            pltpu.VMEM((2, TOK, 2 * D), bf),
+            pltpu.VMEM((2, 8, TOK), f32),
+            pltpu.VMEM((5, D, FF), bf),
+            pltpu.SemaphoreType.DMA((2, 3)),
+            pltpu.SemaphoreType.DMA((1,)),
+            pltpu.SemaphoreType.DMA((3,)),
+            pltpu.SemaphoreType.DMA((6,)),
+        ],
+        compiler_params=pltpu.CompilerParams(vmem_limit_bytes=56 * 1024 * 1024),
+        name="moe_last" if last else "moe_first",
+    )(ids, *hidden, *d_mix, *metas, gathered, *prior)
 
 
 def head_only(block, head):
@@ -724,33 +834,42 @@
 
 
 def owned_grad_kernel(ids, *refs):
-    held, received = refs[:3], refs[3:12]
-    dense, small, full_out, cut_out, buf, sems = refs[12:]
+    pieces = refs[:8]
+    dense, small, extra, full_out, cut_out, buf, sems = refs[8:]
     n, z, x = ids[0], ids[1], ids[2]
     is_small = (z == 1) | ((z == 3) & (x == 1))
-
-    def fetch(group):
-        sources = [held[group]] + list(received[3 * group : 3 * group + 3])
-        return [
-            pltpu.make_async_copy(source, buf.at[i], sems.at[i])
-            for i, source in enumerate(sources)
-        ]
-
-    for group, owner in enumerate((0, 2, 3)):
+    left, right = buf.at[:, :, pl.ds(0, FF // 2)], buf.at[:, :, pl.ds(FF // 2, FF // 2)]
+    groups = (
+        (0, [(pieces[0], buf.at[0]), (pieces[1], buf.at[1])]),
+        (2, [(pieces[2], buf.at[0]), (pieces[3], buf.at[1])]),
+        (
+            3,
+            [
+                (pieces[4], left.at[0]),
+                (pieces[5], left.at[1]),
+                (pieces[6], right.at[0]),
+                (pieces[7], right.at[1]),
+            ],
+        ),
+    )
+    for owner, moves in groups:
 
         @pl.when((z == owner) & jnp.logical_not(is_small))
         def _():
-            for copy in fetch(group):
+            copies = [
+                pltpu.make_async_copy(source, target, sems.at[i])
+                for i, (source, target) in enumerate(moves)
+            ]
+            for copy in copies:
                 copy.start()
-            for copy in fetch(group):
+            for copy in copies:
                 copy.wait()
 
     @pl.when(jnp.logical_not(is_small))
     def _():
         for k in range(4):
             lanes = slice(k * D, k * D + D)
-            total = buf[0, :, lanes].astype(f32) + buf[1, :, lanes].astype(f32)
-            full_out[k] = total + buf[2, :, lanes].astype(f32) + buf[3, :, lanes].astype(f32)
+            full_out[k] = buf[0, :, lanes].astype(f32) + buf[1, :, lanes].astype(f32)
 
     @pl.when(is_small)
     def _():
@@ -788,26 +907,27 @@
 
     for w in range(8):
         for m in range(4):
-            cut_out[4 * w + m] = full_out[m ^ n, 48 * w : 48 * w + 48, :].astype(bf)
-
-
-def owned_grad(ids, held, received, dense, small):
+            cut_out[4 * w + m, :48] = full_out[m ^ n, 48 * w : 48 * w + 48, :].astype(bf)
+            cut_out[4 * w + m, 48:] = extra[...]
+
+
+def owned_grad(ids, pieces, dense, small, extra):
     anyspec, vmem = pl.BlockSpec(memory_space=pl.ANY), pl.BlockSpec(memory_space=pltpu.VMEM)
     return pl.pallas_call(
         owned_grad_kernel,
         out_shape=(
             jax.ShapeDtypeStruct((4, D, D), f32),
-            jax.ShapeDtypeStruct((32, 48, D), bf),
+            jax.ShapeDtypeStruct((32, 56, D), bf),
         ),
-        in_specs=[pl.BlockSpec(memory_space=pltpu.SMEM)] + [anyspec] * 12 + [vmem] * 2,
+        in_specs=[pl.BlockSpec(memory_space=pltpu.SMEM)] + [anyspec] * 8 + [vmem] * 3,
         out_specs=[vmem, vmem],
-        scratch_shapes=[pltpu.VMEM((4, D, FF), bf), pltpu.SemaphoreType.DMA((4,))],
+        scratch_shapes=[pltpu.VMEM((2, D, FF), bf), pltpu.SemaphoreType.DMA((4,))],
         compiler_params=pltpu.CompilerParams(vmem_limit_bytes=40 * 1024 * 1024),
         name="owned_grad",
-    )(ids, *held, *received, dense, small)
-
-
-def ortho_kernel(ids, grad, moment, extra, cut_out, cur, poly):
+    )(ids, *pieces, dense, small, extra)
+
+
+def ortho_kernel(ids, grad, moment, cut_out, cur, high, low, cross):
     n = ids[0]
     for k in range(4):
         cur[k] = grad[k]
@@ -819,40 +939,49 @@
     for k in range(4):
         total = total + jnp.sum(cur[k] * cur[k], axis=0, keepdims=True)
     factor = 1.0 / (jnp.sqrt(jnp.sum(total, axis=1, keepdims=True)) + 1e-07)
+
+    def keep(k, value):
+        cur[k] = value
+        high[:, k * D : k * D + D], low[:, k * D : k * D + D] = halves(value)
+
     for k in range(4):
-        cur[k] = cur[k] * factor
+        keep(k, cur[k] * factor)
 
     def sweep(_, carry):
-        gram = jnp.zeros((D, D), f32)
+        cross[...] = dot(high[...], low[...], NT)
+        gram = dot(high[...], high[...], NT) + (cross[...] + cross[...].T)
+        gram_high, gram_low = halves(gram)
+        cross[...] = dot(gram_high, gram_low)
+        square = dot(gram_high, gram_high) + (cross[...] + cross[...].T)
+        poly = halves(NS_SECOND * gram + NS_THIRD * square)
         for k in range(4):
-            part = halves(cur[k])
-            gram = gram + dot_three(part, part, NT)
-        split = halves(gram)
-        poly[...] = NS_SECOND * gram + NS_THIRD * dot_three(split, split)
-        split = halves(poly[...])
-        for k in range(4):
-            block = cur[k]
-            cur[k] = NS_FIRST * block + dot_three(split, halves(block))
+            lanes = slice(k * D, k * D + D)
+            step = dot_three(poly, (high[:, lanes], low[:, lanes]))
+            keep(k, NS_FIRST * cur[k] + step)
         return carry
 
     lax.fori_loop(0, 5, sweep, 0)
     for w in range(8):
         for m in range(4):
-            cut_out[4 * w + m, :48] = cur[m ^ n, 48 * w : 48 * w + 48, :].astype(bf)
-            cut_out[4 * w + m, 48:] = extra[...]
-
-
-def ortho_owned(ids, grad, moment, extra):
+            cut_out[4 * w + m] = cur[m ^ n, 48 * w : 48 * w + 48, :].astype(bf)
+
+
+def ortho_owned(ids, grad, moment):
     vmem = pl.BlockSpec(memory_space=pltpu.VMEM)
     return pl.pallas_call(
         ortho_kernel,
-        out_shape=jax.ShapeDtypeStruct((32, 56, D), bf),
-        in_specs=[pl.BlockSpec(memory_space=pltpu.SMEM), vmem, vmem, vmem],
+        out_shape=jax.ShapeDtypeStruct((32, 48, D), bf),
+        in_specs=[pl.BlockSpec(memory_space=pltpu.SMEM), vmem, vmem],
         out_specs=vmem,
-        scratch_shapes=[pltpu.VMEM((4, D, D), f32), pltpu.VMEM((D, D), f32)],
+        scratch_shapes=[
+            pltpu.VMEM((4, D, D), f32),
+            pltpu.VMEM((D, FF), bf),
+            pltpu.VMEM((D, FF), bf),
+            pltpu.VMEM((D, D), f32),
+        ],
         compiler_params=pltpu.CompilerParams(vmem_limit_bytes=40 * 1024 * 1024),
         name="ortho_owned",
-    )(ids, grad, moment, extra)
+    )(ids, grad, moment)
 
 
 def update_kernel(decay_ref, grads, orthos, *refs):
@@ -869,16 +998,16 @@
 
     for j in range(9):
         own = square_owner(j)
-        step(0, j, grads[own, :, :96], orthos[own, :48, :96], small_rate)
-    step(1, slice(None), grads[OUT_OWNER, :, :96], orthos[OUT_OWNER, :48, :96], small_rate)
+        step(0, j, grads[own, :48, :96], orthos[own, :48, :96], small_rate)
+    step(1, slice(None), grads[OUT_OWNER, :48, :96], orthos[OUT_OWNER, :48, :96], small_rate)
 
     def router_rows(source):
         return source[ROUTER_OWNER, :48, :128].astype(f32).T[:2]
 
     step(2, slice(None), router_rows(grads), router_rows(orthos), small_rate)
     for e in range(10):
-        step(3, e, grads[up_owner(e)], orthos[up_owner(e), :48], large_rate)
-        step(4, e, grads[down_owner(e)], orthos[down_owner(e), :48], large_rate)
+        step(3, e, grads[up_owner(e), :48], orthos[up_owner(e), :48], large_rate)
+        step(4, e, grads[down_owner(e), :48], orthos[down_owner(e), :48], large_rate)
 
 
 def update(decay, grads, orthos, weights, moments, emas):
@@ -1017,9 +1146,8 @@
             out_t.reshape(-1, 96),
         ]
     )
-    by_y = jnp.stack(in_order(flat, send(flat, to_y), y))
-    by_yc = in_order(by_y, send(by_y, to_core), c)
-    rows = jnp.concatenate([by_yc[0][0], by_yc[1][0], by_yc[0][1], by_yc[1][1]], axis=1)
+    lanes = jnp.stack([flat] + [send(flat, move) for move in NARROW_MOVES[1:]])
+    rows = jnp.concatenate(list(xor_blocks(lanes, 0, y, c)), axis=1)
 
     def my_half(block):
         return pick(block.reshape(5, 2, 24, D), c, 1).reshape(120, D)
@@ -1044,9 +1172,7 @@
     shared_t = jnp.stack([up_t[8:], down_t[8:]], axis=1).reshape(4, 48, D)
     mine = [pick(routed_t, narrow)]
     mine += [send(pick(routed_t, narrow ^ k), NARROW_MOVES[k]) for k in (1, 2, 3)]
-    blocks = jnp.stack(mine + [shared_t])
-    near = jnp.stack([blocks] + [send(blocks, to_z(step)) for step in (1, 2, 3)])
-    far = send(near, to_x)
+    gathered = lax.all_gather(jnp.stack(mine + [shared_t]), WIDE)
 
     moment_parts = (
         turned(moment_square),
@@ -1078,9 +1204,16 @@
     hidden_one = first_mod.reshape(-1, D).astype(bf)
     query_maps = first_maps[:3].reshape(3 * D, D)
     projected = dot(hidden_one, query_maps, NT).astype(bf)
+    gate_one, gate_two = last_four[:, 0:1], last_four[:, 3:4]
+    grad_out = cotangent.astype(f32)
+    grad_seg = grad_out.reshape(segments, SHORT, D)
+    d_mixture = (grad_seg * gate_two).reshape(-1, D).astype(bf)
+    d_mix_core = send(d_mixture, to_core)
+    d_mix_y = send(d_mixture, to_y)
     attended, log_total = attend_fast(resolution, projected)
+    attended, d_mix_y = lax.optimization_barrier((attended, d_mix_y))
+    d_mix_diag = send(d_mix_y, to_core)
     attn_out = dot(attended, out_map, NT)
-    gate_one, gate_two = last_four[:, 0:1], last_four[:, 3:4]
     mid_state = token_f + (attn_out.reshape(segments, SHORT, D) * gate_one).reshape(-1, D)
     second_mod, second_back = jax.vjp(
         modulate, mid_state.reshape(segments, SHORT, D), last_four[:, 1:2], last_four[:, 2:3]
@@ -1098,33 +1231,39 @@
     gates = expo / jnp.sum(expo, axis=0, keepdims=True)
     meta = jnp.concatenate([jnp.where(named, place, -1.0), gates])
 
-    grad_out = cotangent.astype(f32)
-    grad_seg = grad_out.reshape(segments, SHORT, D)
-    d_mixture = (grad_seg * gate_two).reshape(-1, D).astype(bf)
-    pack = jnp.concatenate([hidden_two, d_mixture], axis=1)
-    pack_core, meta_core = send(pack, to_core), send(meta, to_core)
-    pack_y, meta_y = send(pack, to_y), send(meta, to_y)
-    pack_diag, meta_diag = send(pack_y, to_core), send(meta_y, to_core)
+    hidden_core, meta_core = send(hidden_two, to_core), send(meta, to_core)
+    hidden_y, meta_y = send(hidden_two, to_y), send(meta, to_y)
+    meta_diag = send(meta, to_diag)
+    hidden_y, _ = lax.optimization_barrier((hidden_y, meta))
+    hidden_diag = send(hidden_y, to_core)
     place_ids = jnp.stack([narrow, z, x]).astype(jnp.int32)
-    pack, moments = lax.optimization_barrier((pack, moments))
+    hidden_diag, moments = lax.optimization_barrier((hidden_diag, moments))
     moments = lax.all_to_all(moments, AXES, 0, 0, tiled=True)
-    part_own, part_core, part_y, part_diag, d_gate_rows, *grads = moe(
+    part_y, part_diag, gate_far, *first_grads = moe(
+        place_ids, (hidden_y, hidden_diag), (d_mix_y, d_mix_diag), (meta_y, meta_diag), gathered
+    )
+    over = (part_y.astype(f32) + send(part_diag, to_core).astype(f32)).astype(bf)
+    over, moments, hidden_mine = lax.optimization_barrier((over, moments, hidden_two))
+    returned = send(over, to_y)
+    part_own, part_core, gate_near, *grads = moe(
         place_ids,
-        (pack, pack_core, pack_y, pack_diag),
-        (meta, meta_core, meta_y, meta_diag),
-        near,
-        far,
-    )
-    over = (part_y.astype(f32) + send(part_diag, to_core).astype(f32)).astype(bf)
+        (hidden_mine, hidden_core),
+        (d_mixture, d_mix_core),
+        (meta, meta_core),
+        gathered,
+        first_grads,
+    )
+    part_own, part_core, gate_near, grads, returned = lax.optimization_barrier(
+        (part_own, part_core, gate_near, grads, returned)
+    )
     own = part_own.astype(f32) + send(part_core, to_core).astype(f32)
-    total = own + send(over, to_y).astype(f32)
+    total = own + returned.astype(f32)
     mixture, d_hidden = total[:, :D], total[:, D:]
-    d_rows = [d_gate_rows[0, :2]]
-    d_rows += [send(d_gate_rows[k, :2], NARROW_MOVES[k]) for k in (1, 2, 3)]
+    d_rows = [gate_near[0, :2], send(gate_near[1, :2], to_core)]
+    d_rows += [send(gate_far[0, :2], to_y), send(gate_far[1, :2], to_diag)]
     d_gates = xor_blocks(jnp.stack(d_rows), 0, y, c).reshape(ROUTED, TOK)
 
-    g_send, g_keep, g_second, g_third, g_shared = grads
-    g_shared, over = lax.optimization_barrier((g_shared, over))
+    g_send, g_keep, g_second, g_left, g_right, g_shared = grads
 
     def shared_part(k):
         return lax.dynamic_slice_in_dim(g_shared, (narrow ^ k) * D, D, 1)
@@ -1136,25 +1275,24 @@
     def back_x(z_, x_, y_, c_):
         return (z_, 0, y_, c_) if x_ == 1 else None
 
+    def along_z(hops, sides=(0, 1)):
+        table = dict(hops)
+
+        def move(z_, x_, y_, c_):
+            return (table[z_], x_, y_, c_) if z_ in table and x_ in sides else None
+
+        return move
+
     def added(kept, other):
         return (kept.astype(f32) + other.astype(f32)).astype(bf)
 
-    held_one = added(g_keep, send(g_send, to_x))
-    held_three = added(g_third, send(g_third, back_x))
-    held_two = added(
-        jnp.where(x == 0, g_second, shared_grad),
-        send(jnp.where(x == 0, shared_grad, g_second), to_x),
-    )
-    received = []
-    for held, owner in ((held_one, 0), (held_two, 2), (held_three, 3)):
-        for step in (1, 2, 3):
-
-            def move(z_, x_, y_, c_, owner=owner, step=step):
-                if (z_ + step) % 4 != owner or (owner == 3 and x_ == 1):
-                    return None
-                return (owner, x_, y_, c_)
-
-            received.append(send(held, move))
+    def to_owner(held, pairs, last_hop, sides=(0, 1)):
+        held = added(held, send(held, along_z(pairs, sides)))
+        return held, send(held, along_z(last_hop, sides))
+
+    received_one = send(g_send, to_x)
+    received_two = send(jnp.where(x == 0, shared_grad, g_second), to_x)
+    kept_two = jnp.where(x == 0, g_second, shared_grad)
 
     output = (
         mid_state + (mixture.reshape(segments, SHORT, D) * gate_two).reshape(-1, D)
@@ -1171,7 +1309,14 @@
     d_attn = (d_mid_seg * gate_one).reshape(-1, D).astype(bf)
     g_out = dot(d_attn, attended, TN)
     d_attended = jnp.dot(d_attn, out_map, preferred_element_type=f32).astype(bf)
+    received_left, received_right = send(g_left, back_x), send(g_right, back_x)
     d_heads = attend_back_fast(resolution, projected, log_total, d_attended)
+    d_heads, received_one, received_left, received_right = lax.optimization_barrier(
+        (d_heads, received_one, received_left, received_right)
+    )
+    held_one = added(g_keep, received_one)
+    held_left = added(g_left, received_left)
+    held_right = added(g_right, received_right)
     g_qkv = jnp.stack([dot(d_head, hidden_one, TN) for d_head in d_heads])
     d_hidden_one = sum(
         jnp.dot(d_head, first_maps[j], preferred_element_type=f32)
@@ -1191,6 +1336,8 @@
     dense = jnp.concatenate([g_qkv, g_out[None]]).reshape(2, 2, D, D)
     dense = pick(dense, c, 1) + send(pick(dense, 1 - c, 1).astype(bf), to_core).astype(f32)
     dense = pick(dense, y) + send(pick(dense, 1 - y).astype(bf), to_y).astype(f32)
+    dense, received_two = lax.optimization_barrier((dense, received_two))
+    held_two = added(kept_two, received_two)
     dense = dense + send(dense.astype(bf), back_x).astype(f32)
     dense_low = dense.astype(bf)
     for step in (1, 2, 3):
@@ -1210,26 +1357,29 @@
     small = jnp.concatenate([payload, bias_part], axis=3).reshape(32, 8, 512)
     small = lax.all_to_all(small, AXES, 0, 0, tiled=True)
     g_bias = jnp.sum(small[:, 0, D : D + 72], axis=0)
-    grad_full, grad_cut = owned_grad(
-        place_ids, (held_one, held_two, held_three), received, dense, small.reshape(256, 512)
-    )
-    grad_parts = lax.all_to_all(grad_cut, AXES, 0, 0, tiled=True)
-
+    pieces = to_owner(held_one, ((3, 2), (1, 0)), ((2, 0),))
+    pieces += to_owner(held_two, ((0, 1), (3, 2)), ((1, 2),))
+    pieces += to_owner(held_left, ((0, 1), (2, 3)), ((1, 3),), (0,))
+    pieces += to_owner(held_right, ((0, 1), (2, 3)), ((1, 3),), (0,))
     state_bias = MOMENTUM_VECTOR * moment_bias + g_bias
     part_sum = jnp.sum(state_bias * state_bias)
     sum_high = part_sum.astype(bf)
     sum_low = (part_sum - sum_high.astype(f32)).astype(bf)
 
     extra = jnp.pad(jnp.stack([sum_high, sum_low])[None], ((0, 7), (0, D - 2)))
-    ortho_cut = ortho_owned(place_ids, grad_full, moments, extra)
+    grad_full, grad_cut = owned_grad(place_ids, pieces, dense, small.reshape(256, 512), extra)
+    grad_parts = lax.all_to_all(grad_cut, AXES, 0, 0, tiled=True)
+
+    ortho_cut = ortho_owned(place_ids, grad_full, moments)
+    ortho_cut, grad_parts = lax.optimization_barrier((ortho_cut, grad_parts))
     ortho_parts = lax.all_to_all(ortho_cut, AXES, 0, 0, tiled=True)
-    square_total = jnp.sum(ortho_parts[:, 48, :2].astype(f32))
+    square_total = jnp.sum(grad_parts[:, 48, :2].astype(f32))
 
     step_value = step_count[0].astype(f32)
     decay = jnp.minimum(0.9999, (1.0 + step_value) / (10.0 + step_value))
-    weights = (turned(w_square), turned(w_out), w_router, turned(w_up), turned(w_down))
+    masters = (turned(w_square), turned(w_out), w_router, turned(w_up), turned(w_down))
     emas = (turned(ema_square), turned(ema_out), ema_router, turned(ema_up), turned(ema_down))
-    updated = update(decay[None], grad_parts, ortho_parts, weights, moment_parts, emas)
+    updated = update(decay[None], grad_parts, ortho_parts, masters, moment_parts, emas)
     results = []
     for which in range(5):
         results += [

time: 726 us -> 546 us (0.75)
  waiting for transfers between devices: 281 us -> 126 us
  blocking collectives: 84.9 us -> 0 us
  starting transfers between devices: 84.6 us -> 107 us
  between operations: 6.5 us -> 19.6 us
  other arithmetic: 46 us -> 57 us
  local copies, waits for them, and re-layouts: 33.8 us -> 42.5 us
    ppermute x52, waiting for transfers between devices: 250 us -> 87.4 us  [send(): return lax.ppermute(array, AXES, route_pairs(move))]
    all_to_all x1 -> x0, blocking collectives: 84.9 us -> none  [fast_device(): ortho_parts = lax.all_to_all(ortho_cut, AXES, 0, 0, tiled=True)]
    all_to_all x0 -> x1, waiting for transfers between devices: none -> 21.7 us  [fast_device(): ortho_parts = lax.all_to_all(ortho_cut, AXES, 0, 0, tiled=True)]
    all_to_all x1, waiting for transfers between devices: 21.6 us -> 8.03 us  [fast_device(): grad_parts = lax.all_to_all(grad_cut, AXES, 0, 0, tiled=True)]
    all_to_all x1, starting transfers between devices: 3.54 us -> 11.6 us  [fast_device(): grad_parts = lax.all_to_all(grad_cut, AXES, 0, 0, tiled=True)]
    convert_element_type x3 -> x8, other arithmetic: 5.96 us -> 13.5 us  [added(): return (kept.astype(f32) + other.astype(f32)).astype(bf)]
    pallas_call x2 -> x3, Pallas kernels: 111 us -> 115 us  [the longest x2 90.1 us: moe(): pl.pallas_call(partial(moe_kernel, last), out_shape=shapes, in_specs=[pl....]
    unnamed x213 -> x195, local copies, waits for them, and re-layouts: 19 us -> 20.3 us
  transfers between devices with their start and end apart: 55 -> 57, of which waited for: 22 -> 17; matrix products, arithmetic and copies ran while one was open for 10% -> 18% of each run, Pallas kernels for 8% -> 31%
where the time goes in v2:
time: 546 us; the launch traced here: 541 us
  Pallas kernels  174 us (32%)
  waiting for transfers between devices  126 us (23%)
  starting transfers between devices  107 us (20%)
  other arithmetic  57 us (10%)
  local copies, waits for them, and re-layouts  42.5 us (8%)
  between operations  19.6 us (4%)
  matrix products  15.1 us (3%)
    pallas_call x2, Pallas kernels, moe(): pl.pallas_call(partial(moe_kernel, last), out_shape=shapes, in_specs=[pl....  90.1 us
    ppermute x52, waiting for transfers between devices, send(): return lax.ppermute(array, AXES, route_pairs(move))  87.4 us
    ppermute x52, starting transfers between devices, send(): return lax.ppermute(array, AXES, route_pairs(move))  75.9 us
    pallas_call x1, Pallas kernels, attend_back_fast(): pl.pallas_call(attend_back_kernel, grid_spec=pltpu.PrefetchScalarGridSpec...  26 us
    pallas_call x1, Pallas kernels, ortho_owned(): pl.pallas_call(ortho_kernel, out_shape=jax.ShapeDtypeStruct((32, 48, D),...  25.3 us
    pallas_call x1, Pallas kernels, attend_fast(): pl.pallas_call(attend_kernel, grid_spec=pltpu.PrefetchScalarGridSpec(num_...  23 us
    all_to_all x1, waiting for transfers between devices, fast_device(): ortho_parts = lax.all_to_all(ortho_cut, AXES, 0, 0, tiled=True)  21.7 us
    unnamed x195, local copies, waits for them, and re-layouts  20.3 us
  transfers between devices with their start and end apart: 57, of which 17 were waited for; matrix products, arithmetic and copies ran while one was open for 18% of the time, Pallas kernels for 31%

profile of v2, /device:TPU:0, one launch (start us, length us, event | category | flops | bytes accessed | tf_op | source)
XLA Modules:
  0.0 541.0 jit_solution(3540885640488378711)
XLA Ops:
  45.2 14.5 %collective-permute-done.11 = bf16[4,120,384]{2,1,0:T(8,128)(2,1)} collective-permute-done((bf16[4,120,384]{2,1,0:T(8,128)(2,1)}, bf16[4,120,384]{2,1,0:T(8,128)(2,1)}, u32[]{:S(2)}, u32[]{:S(2)}) %collective-permute-start.11) | collective-permute-done | bytes 368672 | tf_op jit(solution)/shard_map/ppermute | solution.py:1041
  61.0 5.7 %collective-permute-done.6 = bf16[4,128,384]{2,1,0:T(8,128)(2,1)S(1)} collective-permute-done((bf16[4,128,384]{2,1,0:T(8,128)(2,1)}, bf16[4,128,384]{2,1,0:T(8,128)(2,1)S(1)}, u32[]{:S(2)}, u32[]{:S(2)}) %collective-permute-start.6) | collective-permute-done | bytes 393248 | tf_op jit(solution)/shard_map/ppermute | solution.py:1041
  80.7 23.0 %attend_fast.1 = (bf16[1024,384]{1,0:T(8,128)(2,1)S(1)}, f32[3,8,1024]{2,1,0:T(8,128)S(1)}) custom-call(s32[1]{0:T(128)S(6)} %copy.111.res, bf16[1024,1152]{1,0:T(8,128)(2,1)S(1)} %convolution_convert_fusion.q_ref.k_ref.v_ref, bf16[1024,1152]{1,0:T(8,128)(2,1)S(1)} %convolution_convert_fusion.q_ref.k_ref.v_ref, ...), custom_call_target="tpu_custom_call" | custom-call | tf_op jit(solution)/shard_map/attend_fast/pallas_call | solution.py:678
  113.5 15.6 %collective-permute-done.14.refs_0_ = bf16[1024,384]{1,0:T(8,128)(2,1)} collective-permute-done((bf16[1024,384]{1,0:T(8,128)(2,1)}, bf16[1024,384]{1,0:T(8,128)(2,1)}, u32[]{:S(2)}, u32[]{:S(2)}) %collective-permute-start.14) | collective-permute-done | bytes 786464 | tf_op jit(solution)/shard_map/ppermute | solution.py:1041
  134.2 5.3 all-to-all-start
  142.3 14.4 %collective-permute-done.18.refs_5_ = f32[16,1024]{1,0:T(8,128)} collective-permute-done((f32[16,1024]{1,0:T(8,128)}, f32[16,1024]{1,0:T(8,128)}, u32[]{:S(2)}, u32[]{:S(2)}) %collective-permute-start.18) | collective-permute-done | bytes 65568 | tf_op jit(solution)/shard_map/ppermute | solution.py:1041
  159.2 43.6 %moe_first.1 = (bf16[1024,768]{1,0:T(8,128)(2,1)}, bf16[1024,768]{1,0:T(8,128)(2,1)}, f32[2,8,1024]{2,1,0:T(8,128)}, bf16[384,1536]{1,0:T(8,128)(2,1)}, bf16[384...) custom-call(s32[3]{0:T(128)} %pad_add_fusion.ids, ...), custom_call_target="tpu_custom_call" | custom-call | tf_op jit(solution)/shard_map/moe_first/pallas_call | solution.py:613
  202.9 3.6 collective-permute-done.22
  219.8 46.5 %moe_last.1 = (bf16[1024,768]{1,0:T(8,128)(2,1)}, bf16[1024,768]{1,0:T(8,128)(2,1)}, f32[2,8,1024]{2,1,0:T(8,128)}, bf16[384,1536]{1,0:T(8,128)(2,1)}, bf16[384,...) custom-call(s32[3]{0:T(128)} %pad_add_fusion.ids, ...), custom_call_target="tpu_custom_call" | custom-call | tf_op jit(solution)/shard_map/moe_last/pallas_call | solution.py:613
  281.7 5.4 %collective-permute-done.37 = bf16[384,384]{1,0:T(8,128)(2,1)} collective-permute-done((bf16[384,384]{1,0:T(8,128)(2,1)}, bf16[384,384]{1,0:T(8,128)(2,1)}, u32[]{:S(2)}, u32[]{:S(2)}) %collective-permute-start.37) | collective-permute-done | bytes 294944 | tf_op jit(solution)/shard_map/ppermute | solution.py:1041
  304.5 26.0 %attend_back_fast.1 = (bf16[1024,384]{1,0:T(8,128)(2,1)S(1)}, bf16[1024,384]{1,0:T(8,128)(2,1)S(1)}, bf16[1024,384]{1,0:T(8,128)(2,1)S(1)}) custom-call(s32[1]{0:T(128)S(6)} %copy.111.res, bf16[1024,1152]{1,0:T(8,128)(2,1)S(1)} %convolution_convert_fusion.q_ref.k_ref.v_ref, bf16[1024,1152]{1,0:T(8,128)(2,1)S(1)} %convolution_convert_fusion.q_ref.k_ref.v_ref, ...), custom_call_target="tpu_custom_call" | custom-call | tf_op jit(solution)/shard_map/attend_back_fast/pallas_call | solution.py:760
  348.5 6.3 %collective-permute-done.40 = bf16[384,384]{1,0:T(8,128)(2,1)S(1)} collective-permute-done((bf16[384,384]{1,0:T(8,128)(2,1)S(1)}, bf16[384,384]{1,0:T(8,128)(2,1)S(1)}, u32[]{:S(2)}, u32[]{:S(2)}) %collective-permute-start.40) | collective-permute-done | bytes 294944 | tf_op jit(solution)/shard_map/ppermute | solution.py:1041
  361.2 10.2 %all-to-all-start.1 = ((f32[32,8,512]{2,1,0:T(8,128)}), f32[32,8,512]{2,1,0:T(8,128)}, u32[]{:S(2)}, u32[]{:S(2)}) async-start(f32[32,8,512]{2,1,0:T(8,128)} %bitcast.112), calls=%async_computation.1 | async-start | bytes 1048576 | tf_op jit(solution)/shard_map/all_to_all | solution.py:1358
  372.7 3.6 collective-permute-start.46
  392.9 12.9 %collective-permute-done.46 = bf16[384,768]{1,0:T(8,128)(2,1)S(1)} collective-permute-done((bf16[384,768]{1,0:T(8,128)(2,1)S(1)}, bf16[384,768]{1,0:T(8,128)(2,1)S(1)}, u32[]{:S(2)}, u32[]{:S(2)}) %collective-permute-start.46) | collective-permute-done | bytes 589856 | tf_op jit(solution)/shard_map/ppermute | solution.py:1041
  408.1 8.4 %all-to-all-done.1 = f32[32,8,512]{2,1,0:T(8,128)} async-done(((f32[32,8,512]{2,1,0:T(8,128)}), f32[32,8,512]{2,1,0:T(8,128)}, u32[]{:S(2)}, u32[]{:S(2)}) %all-to-all-start.1) | async-done | bytes 524320 | tf_op jit(solution)/shard_map/all_to_all | solution.py:1358
  419.0 18.3 %collective-permute-start.49 = (bf16[384,384]{1,0:T(8,128)(2,1)}, bf16[384,384]{1,0:T(8,128)(2,1)}, u32[]{:S(2)}, u32[]{:S(2)}) collective-permute-start(bf16[384,384]{1,0:T(8,128)(2,1)} %fusion.14), channel_id=1, source_target_pairs={{0,8},{1,9},{2,10},{3,11}} | collective-permute-start | bytes 884744 | tf_op jit(solution)/shard_map/ppermute | solution.py:1041
  448.9 11.6 %all-to-all-start.2 = ((bf16[32,56,384]{2,1,0:T(8,128)(2,1)}), bf16[32,56,384]{2,1,0:T(8,128)(2,1)}, u32[]{:S(2)}, u32[]{:S(2)}) async-start(bf16[32,56,384]{2,1,0:T(8,128)(2,1)} %copy-done.7), calls=%async_computation.2 | async-start | bytes 2752512 | tf_op jit(solution)/shard_map/all_to_all | solution.py:1371
  460.5 25.3 %ortho_owned.1 = bf16[32,48,384]{2,1,0:T(8,128)(2,1)} custom-call(s32[3]{0:T(128)S(1)} %copy-done.18, f32[4,384,384]{2,1,0:T(8,128)S(1)} %copy-done.6, f32[32,48,384]{2,1,0:T(8,128)} %all-to-all-done.moment), custom_call_target="tpu_custom_call" | custom-call | tf_op jit(solution)/shard_map/ortho_owned/pallas_call | solution.py:971
  485.8 8.0 %all-to-all-done.2.grads = bf16[32,56,384]{2,1,0:T(8,128)(2,1)} async-done(((bf16[32,56,384]{2,1,0:T(8,128)(2,1)}), bf16[32,56,384]{2,1,0:T(8,128)(2,1)}, u32[]{:S(2)}, u32[]{:S(2)}) %all-to-all-start.2) | async-done | bytes 1376288 | tf_op jit(solution)/shard_map/all_to_all | solution.py:1371
  493.8 3.7 all-to-all-start.3
  498.3 3.8 add_add_fusion.2
  504.9 21.7 %all-to-all-done.3.orthos = bf16[32,48,384]{2,1,0:T(8,128)(2,1)} async-done(((bf16[32,48,384]{2,1,0:T(8,128)(2,1)}), bf16[32,48,384]{2,1,0:T(8,128)(2,1)}, u32[]{:S(2)}, u32[]{:S(2)}) %all-to-all-start.3) | async-done | bytes 1179680 | tf_op jit(solution)/shard_map/all_to_all | solution.py:1375
  529.8 4.1 update.1
  (449 shorter events, 179.8 us)
Async XLA Ops:
  7.2 152.0 %all-gather.3.cloned.1.call-start = ((), (), s32[]{:S(2)}) async-start(), calls=%async_computation.4 | async-start | bytes 6635520 | tf_op jit(solution)/shard_map/all_gather | solution.py:1175
  43.2 23.5 %collective-permute-start.6 = (bf16[4,128,384]{2,1,0:T(8,128)(2,1)}, bf16[4,128,384]{2,1,0:T(8,128)(2,1)S(1)}, u32[]{:S(2)}, u32[]{:S(2)}) collective-permute-start(bf16[4,128,384]{2,1,0:T(8,128)(2,1)} %constant_dynamic-slice_fusion.6), channel_id=1, source_target_pairs={{0,4},{1,5},{2,6},{3,7},{4,0},{5,1},{6,2},{7,3},{8,12},{9,13},{10,... | collective-permute-start | bytes 1179656 | tf_op jit(solution)/shard_map/ppermute | solution.py:1041
  76.8 27.0 %collective-permute-start.13 = (bf16[1024,384]{1,0:T(8,128)(2,1)S(1)}, bf16[1024,384]{1,0:T(8,128)(2,1)S(1)}, u32[]{:S(2)}, u32[]{:S(2)}) collective-permute-start(bf16[1024,384]{1,0:T(8,128)(2,1)S(1)} %fusion.3.refs_2_), channel_id=1, source_target_pairs={{0,2},{1,3},{2,0},{3,1},{4,6},{5,7},{6,4},{7,5},{8,10},{9,11},{10,... | collective-permute-start | bytes 2359304 | tf_op jit(solution)/shard_map/ppermute | solution.py:1041
  134.2 75.3 %all-to-all-start = ((f32[32,48,384]{2,1,0:T(8,128)}), f32[32,48,384]{2,1,0:T(8,128)}, u32[]{:S(2)}, u32[]{:S(2)}) async-start(f32[32,48,384]{2,1,0:T(8,128)} %pack_owned.1), calls=%async_computation | async-start | bytes 4718592 | tf_op jit(solution)/shard_map/all_to_all | solution.py:1241
  209.5 56.8 %collective-permute-start.26 = (bf16[1024,768]{1,0:T(8,128)(2,1)}, bf16[1024,768]{1,0:T(8,128)(2,1)}, u32[]{:S(2)}, u32[]{:S(2)}) collective-permute-start(bf16[1024,768]{1,0:T(8,128)(2,1)} %add_convert_fusion), channel_id=1, source_target_pairs={{0,2},{1,3},{2,0},{3,1},{4,6},{5,7},{6,4},{7,5},{8,10},{9,11},{10,... | collective-permute-start | bytes 4718600 | tf_op jit(solution)/shard_map/ppermute | solution.py:1041
  217.3 54.0 %collective-permute-start.29 = (f32[2,1024]{1,0:T(2,128)S(1)}, f32[2,1024]{1,0:T(2,128)S(1)}, u32[]{:S(2)}, u32[]{:S(2)}) collective-permute-start(f32[2,1024]{1,0:T(2,128)S(1)} %get-tuple-element.234), channel_id=1, source_target_pairs={{0,2},{1,3},{2,0},{3,1},{4,6},{5,7},{6,4},{7,5},{8,10},{9,11},{10,... | collective-permute-start | bytes 24584 | tf_op jit(solution)/shard_map/ppermute | solution.py:1041
  218.0 53.8 %collective-permute-start.30 = (f32[2,1024]{1,0:T(2,128)S(1)}, f32[2,1024]{1,0:T(2,128)S(1)}, u32[]{:S(2)}, u32[]{:S(2)}) collective-permute-start(f32[2,1024]{1,0:T(2,128)S(1)} %get-tuple-element.235), channel_id=1, source_target_pairs={{0,3},{1,2},{2,1},{3,0},{4,7},{5,6},{6,5},{7,4},{8,11},{9,10},{10,... | collective-permute-start | bytes 24584 | tf_op jit(solution)/shard_map/ppermute | solution.py:1041
  266.3 27.4 %collective-permute-start.27 = (bf16[1024,768]{1,0:T(8,128)(2,1)}, bf16[1024,768]{1,0:T(8,128)(2,1)}, u32[]{:S(2)}, u32[]{:S(2)}) collective-permute-start(bf16[1024,768]{1,0:T(8,128)(2,1)} %get-tuple-element.136), channel_id=1, source_target_pairs={{0,1},{1,0},{2,3},{3,2},{4,5},{5,4},{6,7},{7,6},{8,9},{9,8},{10,11... | collective-permute-start | bytes 4718600 | tf_op jit(solution)/shard_map/ppermute | solution.py:1041
  267.6 63.5 %collective-permute-start.32 = (bf16[384,768]{1,0:T(8,128)(2,1)}, bf16[384,768]{1,0:T(8,128)(2,1)}, u32[]{:S(2)}, u32[]{:S(2)}) collective-permute-start(bf16[384,768]{1,0:T(8,128)(2,1)} %get-tuple-element.145), channel_id=1, source_target_pairs={{4,0},{5,1},{6,2},{7,3},{12,8},{13,9},{14,10},{15,11},{20,16},{21,... | collective-permute-start | bytes 1769480 | tf_op jit(solution)/shard_map/ppermute | solution.py:1041
  280.4 50.7 %collective-permute-start.33 = (bf16[384,768]{1,0:T(8,128)(2,1)}, bf16[384,768]{1,0:T(8,128)(2,1)S(1)}, u32[]{:S(2)}, u32[]{:S(2)}) collective-permute-start(bf16[384,768]{1,0:T(8,128)(2,1)} %get-tuple-element.146), channel_id=1, source_target_pairs={{4,0},{5,1},{6,2},{7,3},{12,8},{13,9},{14,10},{15,11},{20,16},{21,... | collective-permute-start | bytes 1769480 | tf_op jit(solution)/shard_map/ppermute | solution.py:1041
  287.2 44.0 %collective-permute-start.31 = (bf16[384,1536]{1,0:T(8,128)(2,1)}, bf16[384,1536]{1,0:T(8,128)(2,1)S(1)}, u32[]{:S(2)}, u32[]{:S(2)}) collective-permute-start(bf16[384,1536]{1,0:T(8,128)(2,1)} %get-tuple-element.144), channel_id=1, source_target_pairs={{0,4},{1,5},{2,6},{3,7},{4,0},{5,1},{6,2},{7,3},{8,12},{9,13},{10,... | collective-permute-start | bytes 3538952 | tf_op jit(solution)/shard_map/ppermute | solution.py:1041
  293.3 61.5 %collective-permute-start.41 = (bf16[384,1536]{1,0:T(8,128)(2,1)}, bf16[384,1536]{1,0:T(8,128)(2,1)}, u32[]{:S(2)}, u32[]{:S(2)}) collective-permute-start(bf16[384,1536]{1,0:T(8,128)(2,1)} %broadcast_select_fusion), channel_id=1, source_target_pairs={{0,4},{1,5},{2,6},{3,7},{4,0},{5,1},{6,2},{7,3},{8,12},{9,13},{10,... | collective-permute-start | bytes 3538952 | tf_op jit(solution)/shard_map/ppermute | solution.py:1041
  341.7 34.6 %collective-permute-start.44 = (bf16[384,768]{1,0:T(8,128)(2,1)}, bf16[384,768]{1,0:T(8,128)(2,1)}, u32[]{:S(2)}, u32[]{:S(2)}) collective-permute-start(bf16[384,768]{1,0:T(8,128)(2,1)} %add_convert_fusion.8), channel_id=1, source_target_pairs={{0,8},{1,9},{2,10},{3,11},{16,24},{17,25},{18,26},{19,27}} | collective-permute-start | bytes 1769480 | tf_op jit(solution)/shard_map/ppermute | solution.py:1041
  347.0 34.4 %collective-permute-start.34 = (bf16[384,1536]{1,0:T(8,128)(2,1)S(1)}, bf16[384,1536]{1,0:T(8,128)(2,1)}, u32[]{:S(2)}, u32[]{:S(2)}) collective-permute-start(bf16[384,1536]{1,0:T(8,128)(2,1)S(1)} %add_convert_fusion.4), channel_id=1, source_target_pairs={{8,0},{9,1},{10,2},{11,3},{12,4},{13,5},{14,6},{15,7},{24,16},{25,... | collective-permute-start | bytes 3538952 | tf_op jit(solution)/shard_map/ppermute | solution.py:1041
  358.0 28.1 %collective-permute-start.42 = (bf16[384,1536]{1,0:T(8,128)(2,1)}, bf16[384,1536]{1,0:T(8,128)(2,1)}, u32[]{:S(2)}, u32[]{:S(2)}) collective-permute-start(bf16[384,1536]{1,0:T(8,128)(2,1)} %add_convert_fusion.2), channel_id=1, source_target_pairs={{0,8},{1,9},{2,10},{3,11},{4,12},{5,13},{6,14},{7,15},{24,16},{25,... | collective-permute-start | bytes 3538952 | tf_op jit(solution)/shard_map/ppermute | solution.py:1041
  361.2 55.3 %all-to-all-start.1 = ((f32[32,8,512]{2,1,0:T(8,128)}), f32[32,8,512]{2,1,0:T(8,128)}, u32[]{:S(2)}, u32[]{:S(2)}) async-start(f32[32,8,512]{2,1,0:T(8,128)} %bitcast.112), calls=%async_computation.1 | async-start | bytes 1048576 | tf_op jit(solution)/shard_map/all_to_all | solution.py:1358
  372.7 33.1 %collective-permute-start.46 = (bf16[384,768]{1,0:T(8,128)(2,1)S(1)}, bf16[384,768]{1,0:T(8,128)(2,1)S(1)}, u32[]{:S(2)}, u32[]{:S(2)}) collective-permute-start(bf16[384,768]{1,0:T(8,128)(2,1)S(1)} %add_convert_fusion.6), channel_id=1, source_target_pairs={{0,8},{1,9},{2,10},{3,11},{16,24},{17,25},{18,26},{19,27}} | collective-permute-start | bytes 1769480 | tf_op jit(solution)/shard_map/ppermute | solution.py:1041
  378.5 64.8 %collective-permute-start.45 = (bf16[384,768]{1,0:T(8,128)(2,1)}, bf16[384,768]{1,0:T(8,128)(2,1)}, u32[]{:S(2)}, u32[]{:S(2)}) collective-permute-start(bf16[384,768]{1,0:T(8,128)(2,1)} %add_convert_fusion.7.refs_4_), channel_id=1, source_target_pairs={{8,24},{9,25},{10,26},{11,27}} | collective-permute-start | bytes 1769480 | tf_op jit(solution)/shard_map/ppermute | solution.py:1041
  383.0 60.4 %collective-permute-start.35 = (bf16[384,1536]{1,0:T(8,128)(2,1)S(1)}, bf16[384,1536]{1,0:T(8,128)(2,1)}, u32[]{:S(2)}, u32[]{:S(2)}) collective-permute-start(bf16[384,1536]{1,0:T(8,128)(2,1)S(1)} %add_convert_fusion.3.refs_0_), channel_id=1, source_target_pairs={{16,0},{17,1},{18,2},{19,3},{20,4},{21,5},{22,6},{23,7}} | collective-permute-start | bytes 3538952 | tf_op jit(solution)/shard_map/ppermute | solution.py:1041
  388.0 55.5 %collective-permute-start.43 = (bf16[384,1536]{1,0:T(8,128)(2,1)S(1)}, bf16[384,1536]{1,0:T(8,128)(2,1)}, u32[]{:S(2)}, u32[]{:S(2)}) collective-permute-start(bf16[384,1536]{1,0:T(8,128)(2,1)S(1)} %add_convert_fusion.1.refs_2_), channel_id=1, source_target_pairs={{8,16},{9,17},{10,18},{11,19},{12,20},{13,21},{14,22},{15,23}} | collective-permute-start | bytes 3538952 | tf_op jit(solution)/shard_map/ppermute | solution.py:1041
  391.5 26.0 %collective-permute-start.51 = (bf16[384,384]{1,0:T(8,128)(2,1)}, bf16[384,384]{1,0:T(8,128)(2,1)}, u32[]{:S(2)}, u32[]{:S(2)}) collective-permute-start(bf16[384,384]{1,0:T(8,128)(2,1)} %fusion.14), channel_id=1, source_target_pairs={{16,8},{17,9},{18,10},{19,11}} | collective-permute-start | bytes 884744 | tf_op jit(solution)/shard_map/ppermute | solution.py:1041
  417.5 25.9 %collective-permute-start.47 = (bf16[384,768]{1,0:T(8,128)(2,1)}, bf16[384,768]{1,0:T(8,128)(2,1)}, u32[]{:S(2)}, u32[]{:S(2)}) collective-permute-start(bf16[384,768]{1,0:T(8,128)(2,1)} %add_convert_fusion.5.refs_6_), channel_id=1, source_target_pairs={{8,24},{9,25},{10,26},{11,27}} | collective-permute-start | bytes 1769480 | tf_op jit(solution)/shard_map/ppermute | solution.py:1041
  448.9 44.9 %all-to-all-start.2 = ((bf16[32,56,384]{2,1,0:T(8,128)(2,1)}), bf16[32,56,384]{2,1,0:T(8,128)(2,1)}, u32[]{:S(2)}, u32[]{:S(2)}) async-start(bf16[32,56,384]{2,1,0:T(8,128)(2,1)} %copy-done.7), calls=%async_computation.2 | async-start | bytes 2752512 | tf_op jit(solution)/shard_map/all_to_all | solution.py:1371
  493.8 32.8 %all-to-all-start.3 = ((bf16[32,48,384]{2,1,0:T(8,128)(2,1)}), bf16[32,48,384]{2,1,0:T(8,128)(2,1)}, u32[]{:S(2)}, u32[]{:S(2)}) async-start(bf16[32,48,384]{2,1,0:T(8,128)(2,1)} %ortho_owned.1), calls=%async_computation.3 | async-start | bytes 2359296 | tf_op jit(solution)/shard_map/all_to_all | solution.py:1375
  (119 other events, 1182.6 us)
Sparse Core Ops, SparseCore 0:
  33.9 96.4 all-gather.2

commit v3 on v2

--- a/solution.py
+++ b/solution.py
@@ -433,91 +433,62 @@
     return act, slope
 
 
-def moe_kernel(last, ids, *refs):
-    hidden, d_mix, metas = refs[0:2], refs[2:4], refs[4:6]
-    gathered = refs[6]
-    prior = refs[7:12] if last else ()
-    refs = refs[7 + len(prior) :]
-    part_out, d_gate_out, refs = refs[0:2], refs[2], refs[3:]
-    grads = refs[: 6 if last else 5]
-    refs = refs[len(grads) :]
-    tok, meta, up, down, up_s, down_s, g_up, g_down, g_up_s, g_down_s = refs[:10]
-    acc, part, d_gate, stage, tok_sem, w_sem, out_sem, g_sem = refs[10:]
+def units(xs, ds, up_ref, down_ref, g_up_ref, g_down_ref, count):
+    out = jnp.zeros(xs.shape, f32)
+    dx = jnp.zeros(xs.shape, f32)
+    for first in range(0, count, UNITS):
+        lanes = slice(first, min(first + UNITS, count))
+        act, slope = gelu_pair(dot(xs, up_ref[:, lanes]))
+        act = act.astype(bf)
+        d_pre = (slope * dot(ds, down_ref[:, lanes])).astype(bf)
+        out = out + dot(act, down_ref[:, lanes], NT)
+        dx = dx + dot(d_pre, up_ref[:, lanes], NT)
+        g_up_ref[:, lanes] += dot(xs, d_pre, TN)
+        g_down_ref[:, lanes] += dot(ds, act, TN)
+    return out, dx
+
+
+def start_all(copies):
+    copies = [pltpu.make_async_copy(*copy) for copy in copies]
+    for copy in copies:
+        copy.start()
+    return copies
+
+
+def wait_all(copies):
+    for copy in copies:
+        copy.wait()
+
+
+def routed_kernel(ids, *refs):
+    hidden, d_mix, metas, priors = refs[0:4], refs[4:8], refs[8:12], refs[12:16]
+    gathered, mix_out, dx_out, d_gate_out = refs[16], refs[17:21], refs[21:25], refs[25]
+    g_send, g_keep, g_second, g_third = refs[26:30]
+    tok, meta, up, down, g_up, g_down, acc, part, d_gate, stage = refs[30:40]
+    tok_sem, w_sem, out_sem, g_sem = refs[40:]
     n, x = ids[0], ids[2]
-
-    def token_copies(i):
-        return [
-            pltpu.make_async_copy(hidden[i], tok.at[i, :, pl.ds(0, D)], tok_sem.at[i, 0]),
-            pltpu.make_async_copy(d_mix[i], tok.at[i, :, pl.ds(D, D)], tok_sem.at[i, 1]),
-            pltpu.make_async_copy(metas[i], meta.at[i], tok_sem.at[i, 2]),
-        ]
-
-    for copy in token_copies(0):
-        copy.start()
     loads = []
     for w in range(8):
-        rows = pl.ds(48 * w, 48)
         for e in range(2):
-            for m, whole, shared in ((0, up, up_s), (1, down, down_s)):
-                slot = 2 * e + m
-                loads.append((gathered.at[w, 4, slot], shared.at[rows, pl.ds(e * D, D)]))
-                for k in range(4):
-                    target = whole.at[e, rows, pl.ds(k * D, D)]
-                    loads.append((gathered.at[w, k, slot], target))
-    loads = [pltpu.make_async_copy(source, target, w_sem.at[0]) for source, target in loads]
-    for copy in loads:
-        copy.start()
-    for copy in token_copies(1):
-        copy.start()
-    carried = [
-        pltpu.make_async_copy(source, stage.at[i], g_sem.at[i]) for i, source in enumerate(prior)
-    ]
-    for copy in carried:
-        copy.start()
-    if last:
-        for copy in carried:
-            copy.wait()
-        for e in range(2):
-            g_up[e] = stage[2 * e].astype(f32)
-            g_down[e] = stage[2 * e + 1].astype(f32)
-            g_up_s[:, e * D : e * D + D] = stage[4, :, 2 * e * D : 2 * e * D + D].astype(f32)
-            g_down_s[:, e * D : e * D + D] = stage[
-                4, :, 2 * e * D + D : 2 * e * D + 2 * D
-            ].astype(f32)
-    else:
-        for total in (g_up, g_down, g_up_s, g_down_s):
-            total[...] = jnp.zeros_like(total)
-    for copy in loads:
-        copy.wait()
-    for i in range(2):
-        for copy in token_copies(i):
-            copy.wait()
-
-    def units(xs, ds, up_ref, down_ref, g_up_ref, g_down_ref, count):
-        out = jnp.zeros(xs.shape, f32)
-        dx = jnp.zeros(xs.shape, f32)
-        for first in range(0, count, UNITS):
-            lanes = slice(first, min(first + UNITS, count))
-            act, slope = gelu_pair(dot(xs, up_ref[:, lanes]))
-            act = act.astype(bf)
-            d_pre = (slope * dot(ds, down_ref[:, lanes])).astype(bf)
-            out = out + dot(act, down_ref[:, lanes], NT)
-            dx = dx + dot(d_pre, up_ref[:, lanes], NT)
-            g_up_ref[:, lanes] += dot(xs, d_pre, TN)
-            g_down_ref[:, lanes] += dot(ds, act, TN)
-        return out, dx
+            for k in range(4):
+                where = (e, pl.ds(48 * w, 48), pl.ds(k * D, D))
+                loads.append((gathered.at[w, k, 2 * e], up.at[where], w_sem.at[0]))
+                loads.append((gathered.at[w, k, 2 * e + 1], down.at[where], w_sem.at[0]))
+    token_loads = []
+    for i in range(4):
+        token_loads.append((hidden[i], tok.at[i, :, pl.ds(0, D)], tok_sem.at[i, 0]))
+        token_loads.append((d_mix[i], tok.at[i, :, pl.ds(D, D)], tok_sem.at[i, 1]))
+        token_loads.append((metas[i], meta.at[i], tok_sem.at[i, 2]))
+        token_loads.append((priors[i], part.at[i], tok_sem.at[i, 3]))
+    loads = start_all(loads)
+    tokens = start_all(token_loads)
+    g_up[...] = jnp.zeros_like(g_up)
+    g_down[...] = jnp.zeros_like(g_down)
+    wait_all(loads)
+    wait_all(tokens)
 
     def one_source(s, carry):
-        def shared(r, carry):
-            rows = pl.ds(pl.multiple_of(r * ROWS, ROWS), ROWS)
-            out, dx = units(
-                tok[s, rows, :D], tok[s, rows, D:], up_s, down_s, g_up_s, g_down_s, 2 * D
-            )
-            acc[rows, :D] = out
-            acc[rows, D:] = dx
-            return carry
-
-        lax.fori_loop(0, TOK // ROWS, shared, 0)
+        acc[...] = part[s].astype(f32)
 
         def routed(e, carry):
             place = meta[s, pl.ds(2 * n + e, 1), :]
@@ -528,15 +499,8 @@
             gates = jnp.sum(jnp.where(hit, gate, 0.0), axis=1, keepdims=True)
             rows = dot(hot, tok[s])
             d_rows = rows[:, D:]
-            out, dx = units(
-                rows[:, :D].astype(bf),
-                (d_rows * gates).astype(bf),
-                up.at[e],
-                down.at[e],
-                g_up.at[e],
-                g_down.at[e],
-                FF,
-            )
+            xs, ds = rows[:, :D].astype(bf), (d_rows * gates).astype(bf)
+            out, dx = units(xs, ds, up.at[e], down.at[e], g_up.at[e], g_down.at[e], FF)
             d_slot = jnp.sum(out * d_rows, axis=1, keepdims=True)
             d_gate[s, pl.ds(e, 1), :] = jnp.sum(
                 jnp.where(hit, d_slot, 0.0), axis=0, keepdims=True
@@ -547,97 +511,129 @@
 
         lax.fori_loop(0, 2, routed, 0)
         part[s] = acc[...].astype(bf)
-        for i in range(2):
-
-            @pl.when(s == i)
-            def _():
-                pltpu.make_async_copy(part.at[i], part_out[i], out_sem.at[i]).start()
-
         return carry
 
-    lax.fori_loop(0, 2, one_source, 0)
-    gate_copy = pltpu.make_async_copy(d_gate, d_gate_out, out_sem.at[2])
-    gate_copy.start()
+    lax.fori_loop(0, 4, one_source, 0)
+    outs = start_all(
+        [(part.at[i, :, pl.ds(0, D)], mix_out[i], out_sem.at[i]) for i in range(4)]
+        + [(part.at[i, :, pl.ds(D, D)], dx_out[i], out_sem.at[5 + i]) for i in range(4)]
+        + [(d_gate, d_gate_out, out_sem.at[4])]
+    )
     for e in range(2):
         stage[2 * e] = g_up[e].astype(bf)
         stage[2 * e + 1] = g_down[e].astype(bf)
-        stage[4, :, 2 * e * D : 2 * e * D + D] = g_up_s[:, e * D : e * D + D].astype(bf)
-        stage[4, :, 2 * e * D + D : 2 * e * D + 2 * D] = g_down_s[
-            :, e * D : e * D + D
-        ].astype(bf)
-
-    def store(slot, target, sem):
-        return pltpu.make_async_copy(slot, target, g_sem.at[sem])
-
-    if last:
-        g_send, g_keep, g_second, g_left, g_right, g_shared = grads
-
-        @pl.when(x == 0)
-        def _():
-            store(stage.at[0], g_keep, 0).start()
-            store(stage.at[3], g_send, 1).start()
-
-        @pl.when(x != 0)
-        def _():
-            store(stage.at[3], g_keep, 0).start()
-            store(stage.at[0], g_send, 1).start()
-
-        rest = [
-            store(stage.at[1], g_second, 2),
-            store(stage.at[2, :, pl.ds(0, FF // 2)], g_left, 3),
-            store(stage.at[2, :, pl.ds(FF // 2, FF // 2)], g_right, 5),
-            store(stage.at[4], g_shared, 4),
-        ]
-        for copy in rest:
-            copy.start()
-        rest += [store(stage.at[0], g_keep, 0), store(stage.at[3], g_send, 1)]
-    else:
-        rest = [store(stage.at[i], grads[i], i) for i in range(5)]
-        for copy in rest:
-            copy.start()
-    for copy in rest:
-        copy.wait()
-    for i in range(2):
-        pltpu.make_async_copy(part.at[i], part_out[i], out_sem.at[i]).wait()
-    gate_copy.wait()
-
-
-def moe(ids, hidden, d_mix, metas, gathered, prior=()):
-    last = len(prior) > 0
+
+    @pl.when(x == 0)
+    def _():
+        wait_all(
+            start_all([(stage.at[0], g_keep, g_sem.at[0]), (stage.at[3], g_send, g_sem.at[1])])
+        )
+
+    @pl.when(x != 0)
+    def _():
+        wait_all(
+            start_all([(stage.at[3], g_keep, g_sem.at[0]), (stage.at[0], g_send, g_sem.at[1])])
+        )
+
+    outs += start_all(
+        [(stage.at[1], g_second, g_sem.at[2]), (stage.at[2], g_third, g_sem.at[3])]
+    )
+    wait_all(outs)
+
+
+def shared_kernel(*refs):
+    hidden, d_mix, gathered, part_out, g_out = refs[0:4], refs[4:8], refs[8], refs[9:13], refs[13]
+    tok, up, down, g_up, g_down, part, stage, tok_sem, w_sem, out_sem = refs[14:]
+    loads = []
+    for w in range(8):
+        for s in range(2):
+            where = (pl.ds(48 * w, 48), pl.ds(s * D, D))
+            loads.append((gathered.at[w, 4, 2 * s], up.at[where], w_sem.at[0]))
+            loads.append((gathered.at[w, 4, 2 * s + 1], down.at[where], w_sem.at[0]))
+    loads = start_all(loads)
+    token_loads = []
+    for i in range(4):
+        token_loads.append((hidden[i], tok.at[i, :, pl.ds(0, D)], tok_sem.at[i, 0]))
+        token_loads.append((d_mix[i], tok.at[i, :, pl.ds(D, D)], tok_sem.at[i, 1]))
+    tokens = start_all(token_loads)
+    g_up[...] = jnp.zeros_like(g_up)
+    g_down[...] = jnp.zeros_like(g_down)
+    wait_all(loads)
+    outs = []
+    for i in range(4):
+        wait_all(tokens[2 * i : 2 * i + 2])
+
+        def some_rows(r, carry, i=i):
+            rows = pl.ds(pl.multiple_of(r * ROWS, ROWS), ROWS)
+            out, dx = units(tok[i, rows, :D], tok[i, rows, D:], up, down, g_up, g_down, 2 * D)
+            part[i, rows, :D] = out.astype(bf)
+            part[i, rows, D:] = dx.astype(bf)
+            return carry
+
+        lax.fori_loop(0, TOK // ROWS, some_rows, 0)
+        outs += start_all([(part.at[i], part_out[i], out_sem.at[i])])
+    for s in range(2):
+        stage[:, 2 * s * D : 2 * s * D + D] = g_up[:, s * D : s * D + D].astype(bf)
+        stage[:, 2 * s * D + D : 2 * s * D + 2 * D] = g_down[:, s * D : s * D + D].astype(bf)
+    wait_all(outs + start_all([(stage, g_out, w_sem.at[1])]))
+
+
+def routed_experts(ids, hidden, d_mix, metas, priors, gathered):
     anyspec = pl.BlockSpec(memory_space=pl.ANY)
+    hbm = pl.BlockSpec(memory_space=pltpu.HBM)
     whole = jax.ShapeDtypeStruct((D, FF), bf)
-    half = jax.ShapeDtypeStruct((D, FF // 2), bf)
-    grads = [whole, whole, whole, half, half, whole] if last else [whole] * 5
-    shapes = [jax.ShapeDtypeStruct((TOK, 2 * D), bf)] * 2
-    shapes += [jax.ShapeDtypeStruct((2, 8, TOK), f32)] + grads
+    shapes = [jax.ShapeDtypeStruct((TOK, D), bf)] * 8
+    shapes += [jax.ShapeDtypeStruct((4, 8, TOK), f32)] + [whole] * 4
     return pl.pallas_call(
-        partial(moe_kernel, last),
+        routed_kernel,
         out_shape=shapes,
-        in_specs=[pl.BlockSpec(memory_space=pltpu.SMEM)] + [anyspec] * (7 + len(prior)),
-        out_specs=[anyspec] * len(shapes),
+        in_specs=[pl.BlockSpec(memory_space=pltpu.SMEM)] + [anyspec] * 17,
+        out_specs=[hbm] * len(shapes),
         scratch_shapes=[
-            pltpu.VMEM((2, TOK, 2 * D), bf),
-            pltpu.VMEM((2, 16, TOK), f32),
+            pltpu.VMEM((4, TOK, 2 * D), bf),
+            pltpu.VMEM((4, 16, TOK), f32),
             pltpu.VMEM((2, D, FF), bf),
             pltpu.VMEM((2, D, FF), bf),
+            pltpu.VMEM((2, D, FF), f32),
+            pltpu.VMEM((2, D, FF), f32),
+            pltpu.VMEM((TOK, 2 * D), f32),
+            pltpu.VMEM((4, TOK, 2 * D), bf),
+            pltpu.VMEM((4, 8, TOK), f32),
+            pltpu.VMEM((4, D, FF), bf),
+            pltpu.SemaphoreType.DMA((4, 4)),
+            pltpu.SemaphoreType.DMA((1,)),
+            pltpu.SemaphoreType.DMA((9,)),
+            pltpu.SemaphoreType.DMA((4,)),
+        ],
+        compiler_params=pltpu.CompilerParams(vmem_limit_bytes=58 * 1024 * 1024),
+        name="routed_experts",
+    )(ids, *hidden, *d_mix, *metas, *priors, gathered)
+
+
+def shared_units(hidden, d_mix, gathered):
+    anyspec = pl.BlockSpec(memory_space=pl.ANY)
+    hbm = pl.BlockSpec(memory_space=pltpu.HBM)
+    shapes = [jax.ShapeDtypeStruct((TOK, 2 * D), bf)] * 4 + [jax.ShapeDtypeStruct((D, FF), bf)]
+    return pl.pallas_call(
+        shared_kernel,
+        out_shape=shapes,
+        in_specs=[anyspec] * 9,
+        out_specs=[hbm] * 5,
+        scratch_shapes=[
+            pltpu.VMEM((4, TOK, 2 * D), bf),
             pltpu.VMEM((D, 2 * D), bf),
             pltpu.VMEM((D, 2 * D), bf),
-            pltpu.VMEM((2, D, FF), f32),
-            pltpu.VMEM((2, D, FF), f32),
             pltpu.VMEM((D, 2 * D), f32),
             pltpu.VMEM((D, 2 * D), f32),
-            pltpu.VMEM((TOK, 2 * D), f32),
-            pltpu.VMEM((2, TOK, 2 * D), bf),
-            pltpu.VMEM((2, 8, TOK), f32),
-            pltpu.VMEM((5, D, FF), bf),
-            pltpu.SemaphoreType.DMA((2, 3)),
-            pltpu.SemaphoreType.DMA((1,)),
-            pltpu.SemaphoreType.DMA((3,)),
-            pltpu.SemaphoreType.DMA((6,)),
+            pltpu.VMEM((4, TOK, 2 * D), bf),
+            pltpu.VMEM((D, FF), bf),
+            pltpu.SemaphoreType.DMA((4, 2)),
+            pltpu.SemaphoreType.DMA((2,)),
+            pltpu.SemaphoreType.DMA((4,)),
         ],
-        compiler_params=pltpu.CompilerParams(vmem_limit_bytes=56 * 1024 * 1024),
-        name="moe_last" if last else "moe_first",
-    )(ids, *hidden, *d_mix, *metas, gathered, *prior)
+        compiler_params=pltpu.CompilerParams(vmem_limit_bytes=58 * 1024 * 1024),
+        name="shared_units",
+    )(*hidden, *d_mix, gathered)
 
 
 def head_only(block, head):
@@ -834,31 +830,17 @@
 
 
 def owned_grad_kernel(ids, *refs):
-    pieces = refs[:8]
-    dense, small, extra, full_out, cut_out, buf, sems = refs[8:]
+    pieces = refs[:6]
+    dense, small, extra, full_out, cut_out, buf, sems = refs[6:]
     n, z, x = ids[0], ids[1], ids[2]
     is_small = (z == 1) | ((z == 3) & (x == 1))
-    left, right = buf.at[:, :, pl.ds(0, FF // 2)], buf.at[:, :, pl.ds(FF // 2, FF // 2)]
-    groups = (
-        (0, [(pieces[0], buf.at[0]), (pieces[1], buf.at[1])]),
-        (2, [(pieces[2], buf.at[0]), (pieces[3], buf.at[1])]),
-        (
-            3,
-            [
-                (pieces[4], left.at[0]),
-                (pieces[5], left.at[1]),
-                (pieces[6], right.at[0]),
-                (pieces[7], right.at[1]),
-            ],
-        ),
-    )
-    for owner, moves in groups:
+    for group, owner in enumerate((0, 2, 3)):
 
         @pl.when((z == owner) & jnp.logical_not(is_small))
         def _():
             copies = [
-                pltpu.make_async_copy(source, target, sems.at[i])
-                for i, (source, target) in enumerate(moves)
+                pltpu.make_async_copy(pieces[2 * group + i], buf.at[i], sems.at[i])
+                for i in range(2)
             ]
             for copy in copies:
                 copy.start()
@@ -912,16 +894,16 @@
 
 
 def owned_grad(ids, pieces, dense, small, extra):
-    anyspec, vmem = pl.BlockSpec(memory_space=pl.ANY), pl.BlockSpec(memory_space=pltpu.VMEM)
+    anyspec, vmem = pl.BlockSpec(memory_space=pltpu.HBM), pl.BlockSpec(memory_space=pltpu.VMEM)
     return pl.pallas_call(
         owned_grad_kernel,
         out_shape=(
             jax.ShapeDtypeStruct((4, D, D), f32),
             jax.ShapeDtypeStruct((32, 56, D), bf),
         ),
-        in_specs=[pl.BlockSpec(memory_space=pltpu.SMEM)] + [anyspec] * 8 + [vmem] * 3,
+        in_specs=[pl.BlockSpec(memory_space=pltpu.SMEM)] + [anyspec] * 6 + [vmem] * 3,
         out_specs=[vmem, vmem],
-        scratch_shapes=[pltpu.VMEM((2, D, FF), bf), pltpu.SemaphoreType.DMA((4,))],
+        scratch_shapes=[pltpu.VMEM((2, D, FF), bf), pltpu.SemaphoreType.DMA((2,))],
         compiler_params=pltpu.CompilerParams(vmem_limit_bytes=40 * 1024 * 1024),
         name="owned_grad",
     )(ids, *pieces, dense, small, extra)
@@ -1021,6 +1003,96 @@
         compiler_params=pltpu.CompilerParams(vmem_limit_bytes=48 * 1024 * 1024),
         name="update",
     )(decay, grads, orthos, *weights, *moments, *emas)
+
+
+def first_back_kernel(
+    ids, dq, dk, dv, hidden, tokens, d_mid, maps, scales, g_out, mods, cond, g_router, *refs
+):
+    grad_in, keep, out_send, payload, g_acc, sums = refs
+    i = pl.program_id(0)
+    heads = (dq, dk, dv)
+    d_hidden = jnp.zeros((SHORT, D), f32)
+    for j in range(3):
+        d_hidden = d_hidden + dot(heads[j][...], maps[j * D : j * D + D, :])
+
+    @pl.when(i == 0)
+    def _():
+        for j in range(3):
+            g_acc[j] = dot(heads[j][...], hidden[...], TN)
+
+    @pl.when(i != 0)
+    def _():
+        for j in range(3):
+            g_acc[j] += dot(heads[j][...], hidden[...], TN)
+
+    rows = tokens[...].astype(f32)
+    center = rows - jnp.mean(rows, axis=1, keepdims=True)
+    inverse = lax.rsqrt(jnp.mean(center * center, axis=1, keepdims=True) + EPSILON)
+    normed = center * inverse
+    d_normed = d_hidden * (1.0 + scales[pl.ds(i, 1), :])
+    inner = d_normed - jnp.mean(d_normed, axis=1, keepdims=True)
+    inner = inner - normed * jnp.mean(d_normed * normed, axis=1, keepdims=True)
+    grad_in[...] = d_mid[...] + inverse * inner
+    sums[0, pl.ds(i, 1), :] = jnp.sum(d_hidden, axis=0, keepdims=True)
+    sums[1, pl.ds(i, 1), :] = jnp.sum(d_hidden * normed, axis=0, keepdims=True)
+
+    @pl.when(i == 3)
+    def _():
+        c = lax.rem(ids[0], 2)
+        for m in range(4):
+
+            def total(m=m):
+                return g_acc[m] if m < 3 else g_out[...]
+
+            @pl.when(c == m % 2)
+            def _():
+                keep[m // 2] = total()
+
+            @pl.when(c != m % 2)
+            def _():
+                out_send[m // 2] = total().astype(bf)
+
+        rows = [sums[0, :4, :], sums[1, :4, :]] + [mods[j] for j in range(4)]
+        payload[...] = jnp.zeros_like(payload)
+        for j, slot in enumerate((12, 13, 14, 15, 28, 29)):
+            payload[slot, :4, :D] = rows[j]
+            payload[slot, 4:, :D] = cond[...]
+        payload[30, :, :D] = g_router[...]
+        bias = jnp.concatenate([jnp.sum(row, axis=0, keepdims=True) for row in rows], axis=1)
+        for slot in range(32):
+            payload[slot, 0:1, D : D + 72] = bias[:, slot * 72 : slot * 72 + 72]
+
+
+def first_back_fast(ids, d_heads, hidden, tokens, d_mid, maps, scales, g_out, mods, cond, g_router):
+    block = pl.BlockSpec((SHORT, D), lambda i: (i, 0))
+
+    def whole(*shape):
+        return pl.BlockSpec(shape, lambda i: (0,) * len(shape))
+
+    return pl.pallas_call(
+        first_back_kernel,
+        grid=(4,),
+        out_shape=(
+            jax.ShapeDtypeStruct((TOK, D), f32),
+            jax.ShapeDtypeStruct((2, D, D), f32),
+            jax.ShapeDtypeStruct((2, D, D), bf),
+            jax.ShapeDtypeStruct((32, 8, 512), f32),
+        ),
+        in_specs=[pl.BlockSpec(memory_space=pltpu.SMEM)]
+        + [block] * 6
+        + [
+            whole(3 * D, D),
+            whole(4, D),
+            whole(D, D),
+            whole(4, 4, D),
+            whole(4, D),
+            whole(8, D),
+        ],
+        out_specs=[block, whole(2, D, D), whole(2, D, D), whole(32, 8, 512)],
+        scratch_shapes=[pltpu.VMEM((3, D, D), f32), pltpu.VMEM((2, 8, D), f32)],
+        compiler_params=pltpu.CompilerParams(vmem_limit_bytes=40 * 1024 * 1024),
+        name="first_back",
+    )(ids, *d_heads, hidden, tokens, d_mid, maps, scales, g_out, mods, cond, g_router)
 
 
 AXES = (WIDE, NARROW)
@@ -1149,11 +1221,22 @@
     lanes = jnp.stack([flat] + [send(flat, move) for move in NARROW_MOVES[1:]])
     rows = jnp.concatenate(list(xor_blocks(lanes, 0, y, c)), axis=1)
 
+    moment_parts = (
+        turned(moment_square),
+        turned(moment_out),
+        moment_router,
+        turned(moment_up),
+        turned(moment_down),
+    )
+    router_block = lanes_to(turned(moment_router), D)
+    moments = pack_owned(*moment_parts[:2], router_block, *moment_parts[3:])
+
     def my_half(block):
         return pick(block.reshape(5, 2, 24, D), c, 1).reshape(120, D)
 
     first_rows = jnp.concatenate([my_half(rows[:240]), rows[240:248]])
     first_all = gather_rows(first_rows, z, x, c)
+    first_all, moments = lax.optimization_barrier((first_all, moments))
     second_all = gather_rows(my_half(rows[248:]), z, x, c)
 
     def assemble(gathered):
@@ -1173,16 +1256,6 @@
     mine = [pick(routed_t, narrow)]
     mine += [send(pick(routed_t, narrow ^ k), NARROW_MOVES[k]) for k in (1, 2, 3)]
     gathered = lax.all_gather(jnp.stack(mine + [shared_t]), WIDE)
-
-    moment_parts = (
-        turned(moment_square),
-        turned(moment_out),
-        moment_router,
-        turned(moment_up),
-        turned(moment_down),
-    )
-    router_block = lanes_to(turned(moment_router), D)
-    moments = pack_owned(*moment_parts[:2], router_block, *moment_parts[3:])
 
     res_group = resolution[0]
     token_f = tokens.astype(f32)
@@ -1200,7 +1273,7 @@
     last_four = modulation_of(second_maps[:4], bias_rows[2:])
     out_map = second_maps[4]
     seg_rows = token_f.reshape(segments, SHORT, D)
-    first_mod, first_back = jax.vjp(modulate, seg_rows, first_two[:, 0:1], first_two[:, 1:2])
+    first_mod = modulate(seg_rows, first_two[:, 0:1], first_two[:, 1:2])
     hidden_one = first_mod.reshape(-1, D).astype(bf)
     query_maps = first_maps[:3].reshape(3 * D, D)
     projected = dot(hidden_one, query_maps, NT).astype(bf)
@@ -1237,67 +1310,68 @@
     hidden_y, _ = lax.optimization_barrier((hidden_y, meta))
     hidden_diag = send(hidden_y, to_core)
     place_ids = jnp.stack([narrow, z, x]).astype(jnp.int32)
-    hidden_diag, moments = lax.optimization_barrier((hidden_diag, moments))
+    hiddens = (hidden_two, hidden_core, hidden_y, hidden_diag)
+    d_mixes = (d_mixture, d_mix_core, d_mix_y, d_mix_diag)
+    metas = (meta, meta_core, meta_y, meta_diag)
+    hiddens, d_mixes, metas, moments = lax.optimization_barrier((hiddens, d_mixes, metas, moments))
     moments = lax.all_to_all(moments, AXES, 0, 0, tiled=True)
-    part_y, part_diag, gate_far, *first_grads = moe(
-        place_ids, (hidden_y, hidden_diag), (d_mix_y, d_mix_diag), (meta_y, meta_diag), gathered
-    )
-    over = (part_y.astype(f32) + send(part_diag, to_core).astype(f32)).astype(bf)
-    over, moments, hidden_mine = lax.optimization_barrier((over, moments, hidden_two))
-    returned = send(over, to_y)
-    part_own, part_core, gate_near, *grads = moe(
-        place_ids,
-        (hidden_mine, hidden_core),
-        (d_mixture, d_mix_core),
-        (meta, meta_core),
-        gathered,
-        first_grads,
-    )
-    part_own, part_core, gate_near, grads, returned = lax.optimization_barrier(
-        (part_own, part_core, gate_near, grads, returned)
-    )
-    own = part_own.astype(f32) + send(part_core, to_core).astype(f32)
-    total = own + returned.astype(f32)
-    mixture, d_hidden = total[:, :D], total[:, D:]
-    d_rows = [gate_near[0, :2], send(gate_near[1, :2], to_core)]
-    d_rows += [send(gate_far[0, :2], to_y), send(gate_far[1, :2], to_diag)]
-    d_gates = xor_blocks(jnp.stack(d_rows), 0, y, c).reshape(ROUTED, TOK)
-
-    g_send, g_keep, g_second, g_left, g_right, g_shared = grads
+    *priors, g_shared = shared_units(hiddens, d_mixes, gathered)
+
+    def back_x(z_, x_, y_, c_):
+        return (z_, 0, y_, c_) if x_ == 1 else None
+
+    def forth_x(z_, x_, y_, c_):
+        return (z_, 1, y_, c_) if x_ == 0 else None
+
+    def along_z(hops, sides=(0, 1)):
+        table = dict(hops)
+
+        def move(z_, x_, y_, c_):
+            return (table[z_], x_, y_, c_) if z_ in table and x_ in sides else None
+
+        return move
+
+    def added(kept, other):
+        return (kept.astype(f32) + other.astype(f32)).astype(bf)
 
     def shared_part(k):
         return lax.dynamic_slice_in_dim(g_shared, (narrow ^ k) * D, D, 1)
 
-    shared_grad = jnp.concatenate(
-        [shared_part(0)] + [send(shared_part(k), NARROW_MOVES[k]) for k in (1, 2, 3)], axis=1
-    )
-
-    def back_x(z_, x_, y_, c_):
-        return (z_, 0, y_, c_) if x_ == 1 else None
-
-    def along_z(hops, sides=(0, 1)):
-        table = dict(hops)
-
-        def move(z_, x_, y_, c_):
-            return (table[z_], x_, y_, c_) if z_ in table and x_ in sides else None
-
-        return move
-
-    def added(kept, other):
-        return (kept.astype(f32) + other.astype(f32)).astype(bf)
-
-    def to_owner(held, pairs, last_hop, sides=(0, 1)):
-        held = added(held, send(held, along_z(pairs, sides)))
-        return held, send(held, along_z(last_hop, sides))
-
+    def over_core(parts):
+        over = (parts[2].astype(f32) + send(parts[3], to_core).astype(f32)).astype(bf)
+        return parts[0].astype(f32) + send(parts[1], to_core).astype(f32), over
+
+    gate = lax.optimization_barrier
+    shared_parts = [shared_part(0)]
+    shared_parts += [send(shared_part(k), NARROW_MOVES[k]) for k in (1, 2, 3)]
+    *routed_outs, d_gate_rows, g_send, g_keep, g_second, g_third = routed_experts(
+        place_ids, hiddens, d_mixes, metas, priors, gathered
+    )
+    routed_outs, shared_parts, moments, d_gate_rows, g_send = gate(
+        (routed_outs, shared_parts, moments, d_gate_rows, g_send)
+    )
+    pairs_one, pairs_two, pairs_three = ((3, 2), (1, 0)), ((0, 1), (3, 2)), ((0, 1), (2, 3))
     received_one = send(g_send, to_x)
-    received_two = send(jnp.where(x == 0, shared_grad, g_second), to_x)
-    kept_two = jnp.where(x == 0, g_second, shared_grad)
-
-    output = (
-        mid_state + (mixture.reshape(segments, SHORT, D) * gate_two).reshape(-1, D)
-    ).astype(bf)
-    d_gate_two = jnp.sum(grad_seg * mixture.reshape(segments, SHORT, D), axis=1)
+    step_three = send(g_third, along_z(pairs_three))
+    d_rows = [d_gate_rows[0, :2]]
+    d_rows += [send(d_gate_rows[k, :2], NARROW_MOVES[k]) for k in (1, 2, 3)]
+    own_hidden, over_hidden = over_core(routed_outs[4:])
+    own_hidden, over_hidden, mix_outs, shared_parts, g_keep, g_second, d_rows = gate(
+        (own_hidden, over_hidden, routed_outs[:4], shared_parts, g_keep, g_second, d_rows)
+    )
+    far_hidden = send(over_hidden, to_y)
+    shared_grad = jnp.concatenate(shared_parts, axis=1)
+    received_second = send(g_second, back_x)
+    received_shared = send(shared_grad, forth_x)
+    own_mix, over_mix = over_core(mix_outs)
+    d_gates = xor_blocks(jnp.stack(d_rows), 0, y, c).reshape(ROUTED, TOK)
+    far_hidden, own_mix, over_mix, received_one, step_three, shared_grad, d_gates = gate(
+        (far_hidden, own_mix, over_mix, received_one, step_three, shared_grad, d_gates)
+    )
+    held_one = added(g_keep, received_one)
+    held_three = added(g_third, step_three)
+    d_hidden = own_hidden + far_hidden.astype(f32)
+
     d_logits = gates * (d_gates - jnp.sum(gates * d_gates, axis=0, keepdims=True))
     d_logits = d_logits.astype(bf)
     g_router = jnp.dot(d_logits, hidden_two, preferred_element_type=f32)
@@ -1309,36 +1383,62 @@
     d_attn = (d_mid_seg * gate_one).reshape(-1, D).astype(bf)
     g_out = dot(d_attn, attended, TN)
     d_attended = jnp.dot(d_attn, out_map, preferred_element_type=f32).astype(bf)
-    received_left, received_right = send(g_left, back_x), send(g_right, back_x)
+    d_attended, held_one, held_three, over_mix = gate(
+        (d_attended, held_one, held_three, over_mix)
+    )
+    step_one = send(held_one, along_z(pairs_one))
+    last_three = send(held_three, along_z(((1, 3),)))
+    far_mix = send(over_mix, to_y)
     d_heads = attend_back_fast(resolution, projected, log_total, d_attended)
-    d_heads, received_one, received_left, received_right = lax.optimization_barrier(
-        (d_heads, received_one, received_left, received_right)
-    )
-    held_one = added(g_keep, received_one)
-    held_left = added(g_left, received_left)
-    held_right = added(g_right, received_right)
-    g_qkv = jnp.stack([dot(d_head, hidden_one, TN) for d_head in d_heads])
-    d_hidden_one = sum(
-        jnp.dot(d_head, first_maps[j], preferred_element_type=f32)
-        for j, d_head in enumerate(d_heads)
-    )
-    d_rows_one, d_shift_one, d_scale_one = first_back(d_hidden_one.reshape(segments, SHORT, D))
-    grad_in = d_mid + d_rows_one.reshape(-1, D)
-    d_modulation = [
-        d_shift_one[:, 0],
-        d_scale_one[:, 0],
-        d_gate_one,
-        d_shift_two[:, 0],
-        d_scale_two[:, 0],
-        d_gate_two,
-    ]
-
-    dense = jnp.concatenate([g_qkv, g_out[None]]).reshape(2, 2, D, D)
-    dense = pick(dense, c, 1) + send(pick(dense, 1 - c, 1).astype(bf), to_core).astype(f32)
-    dense = pick(dense, y) + send(pick(dense, 1 - y).astype(bf), to_y).astype(f32)
-    dense, received_two = lax.optimization_barrier((dense, received_two))
-    held_two = added(kept_two, received_two)
-    dense = dense + send(dense.astype(bf), back_x).astype(f32)
+    d_heads, step_one, last_three, received_second, received_shared, far_mix = gate(
+        (d_heads, step_one, last_three, received_second, received_shared, far_mix)
+    )
+    held_two = added(
+        jnp.where(x == 0, g_second, shared_grad), jnp.where(x == 0, received_second, received_shared)
+    )
+    held_one = added(held_one, step_one)
+    held_three = added(held_three, last_three)
+    d_heads, held_one, held_two, held_three = gate((d_heads, held_one, held_two, held_three))
+
+    def cross_x(z_, x_, y_, c_):
+        return (z_, 0, y_, c_) if x_ == 1 and z_ == 3 else None
+
+    step_two = send(held_two, along_z(pairs_two))
+    last_one = send(held_one, along_z(((2, 0),)))
+    cross_three = send(held_three, cross_x)
+    mixture = own_mix + far_mix.astype(f32)
+    output = (
+        mid_state + (mixture.reshape(segments, SHORT, D) * gate_two).reshape(-1, D)
+    ).astype(bf)
+    d_gate_two = jnp.sum(grad_seg * mixture.reshape(segments, SHORT, D), axis=1)
+    mods = jnp.stack([d_gate_one, d_shift_two[:, 0], d_scale_two[:, 0], d_gate_two])
+    grad_in, dense_keep, dense_send, small = first_back_fast(
+        place_ids,
+        d_heads,
+        hidden_one,
+        tokens,
+        d_mid,
+        query_maps,
+        first_two[:, 1],
+        g_out,
+        mods,
+        cond_low.astype(f32),
+        g_router,
+    )
+
+    dense_recv = send(dense_send, to_core)
+    small, dense_recv = gate((small, dense_recv))
+    dense = dense_keep + dense_recv.astype(f32)
+    dense_far = send(pick(dense, 1 - y).astype(bf), to_y)
+    small = lax.all_to_all(small, AXES, 0, 0, tiled=True)
+    g_bias = jnp.sum(small[:, 0, D : D + 72], axis=0)
+    dense_far, step_two = gate((dense_far, step_two))
+    held_two = added(held_two, step_two)
+    last_two = send(held_two, along_z(((1, 2),)))
+    dense = pick(dense, y) + dense_far.astype(f32)
+    dense_side = send(dense.astype(bf), back_x)
+    pieces = (held_one, last_one, held_two, last_two, held_three, cross_three)
+    dense = dense + dense_side.astype(f32)
     dense_low = dense.astype(bf)
     for step in (1, 2, 3):
 
@@ -1347,20 +1447,6 @@
 
         dense = dense + send(dense_low, to_second).astype(f32)
 
-    cond_rows = cond_low.astype(f32)
-    ada_rows = [jnp.concatenate([d_mod, cond_rows]) for d_mod in d_modulation]
-    payload = jnp.zeros((8, 4, 8, D), f32)
-    payload = payload.at[3].set(jnp.stack(ada_rows[:4]))
-    payload = payload.at[7, :3].set(jnp.stack(ada_rows[4:] + [g_router]))
-    bias_part = jnp.concatenate([jnp.sum(d_mod, axis=0) for d_mod in d_modulation])
-    bias_part = jnp.pad(bias_part.reshape(8, 4, 1, 72), ((0, 0), (0, 0), (0, 7), (0, 56)))
-    small = jnp.concatenate([payload, bias_part], axis=3).reshape(32, 8, 512)
-    small = lax.all_to_all(small, AXES, 0, 0, tiled=True)
-    g_bias = jnp.sum(small[:, 0, D : D + 72], axis=0)
-    pieces = to_owner(held_one, ((3, 2), (1, 0)), ((2, 0),))
-    pieces += to_owner(held_two, ((0, 1), (3, 2)), ((1, 2),))
-    pieces += to_owner(held_left, ((0, 1), (2, 3)), ((1, 3),), (0,))
-    pieces += to_owner(held_right, ((0, 1), (2, 3)), ((1, 3),), (0,))
     state_bias = MOMENTUM_VECTOR * moment_bias + g_bias
     part_sum = jnp.sum(state_bias * state_bias)
     sum_high = part_sum.astype(bf)

time: 546 us -> 504 us (0.923)
  waiting for transfers between devices: 126 us -> 108 us
  starting transfers between devices: 107 us -> 93.9 us
  other arithmetic: 57 us -> 50.5 us
  Pallas kernels: 174 us -> 180 us
  matrix products: 15.1 us -> 9.15 us
    ppermute x52 -> x53, waiting for transfers between devices: 87.4 us -> 75.8 us  [send(): return lax.ppermute(array, AXES, route_pairs(move))]
    all_to_all x1, waiting for transfers between devices: 8.44 us -> 0.89 us  [fast_device(): small = lax.all_to_all(small, AXES, 0, 0, tiled=True)]
    ppermute x52 -> x53, starting transfers between devices: 75.9 us -> 70.1 us  [send(): return lax.ppermute(array, AXES, route_pairs(move))]
    pallas_call x2 -> x3, Pallas kernels: 90.1 us -> 95.3 us  [the longest x1 61.5 us: routed_experts(): pl.pallas_call(routed_kernel, out_shape=shapes, in_specs=[pl.BlockSpec(me...]
    unnamed x195 -> x147, local copies, waits for them, and re-layouts: 20.3 us -> 22 us
    convert_element_type x8 -> x6, other arithmetic: 13.5 us -> 11.9 us  [added(): return (kept.astype(f32) + other.astype(f32)).astype(bf)]
  transfers between devices with their start and end apart: 57 -> 58, of which waited for: 17 -> 17; matrix products, arithmetic and copies ran while one was open for 18% -> 14% of each run, Pallas kernels for 31% -> 33%
where the time goes in v3:
time: 504 us; the launch traced here: 499 us
  Pallas kernels  180 us (36%)
  waiting for transfers between devices  108 us (21%)
  starting transfers between devices  93.9 us (19%)
  other arithmetic  50.5 us (10%)
  local copies, waits for them, and re-layouts  38 us (8%)
  between operations  19.4 us (4%)
  matrix products  9.15 us (2%)
    ppermute x53, waiting for transfers between devices, send(): return lax.ppermute(array, AXES, route_pairs(move))  75.8 us
    ppermute x53, starting transfers between devices, send(): return lax.ppermute(array, AXES, route_pairs(move))  70.1 us
    pallas_call x1, Pallas kernels, routed_experts(): pl.pallas_call(routed_kernel, out_shape=shapes, in_specs=[pl.BlockSpec(me...  61.5 us
    pallas_call x1, Pallas kernels, shared_units(): pl.pallas_call(shared_kernel, out_shape=shapes, in_specs=[anyspec] * 9, o...  26.3 us
    pallas_call x1, Pallas kernels, attend_back_fast(): pl.pallas_call(attend_back_kernel, grid_spec=pltpu.PrefetchScalarGridSpec...  26.1 us
    pallas_call x1, Pallas kernels, ortho_owned(): pl.pallas_call(ortho_kernel, out_shape=jax.ShapeDtypeStruct((32, 48, D),...  25.2 us
    pallas_call x1, Pallas kernels, attend_fast(): pl.pallas_call(attend_kernel, grid_spec=pltpu.PrefetchScalarGridSpec(num_...  23 us
    all_to_all x1, waiting for transfers between devices, fast_device(): ortho_parts = lax.all_to_all(ortho_cut, AXES, 0, 0, tiled=True)  22.1 us
  transfers between devices with their start and end apart: 58, of which 17 were waited for; matrix products, arithmetic and copies ran while one was open for 14% of the time, Pallas kernels for 33%

profile of v3, /device:TPU:0, one launch (start us, length us, event | category | flops | bytes accessed | tf_op | source)
XLA Modules:
  0.0 498.6 jit_solution(14657850360291366737)
XLA Ops:
  27.8 3.6 collective-permute-start.3
  36.9 4.9 collective-permute-done.8
  41.7 4.7 collective-permute-start.10
  54.2 7.8 %collective-permute-done.11 = bf16[4,120,384]{2,1,0:T(8,128)(2,1)} collective-permute-done((bf16[4,120,384]{2,1,0:T(8,128)(2,1)}, bf16[4,120,384]{2,1,0:T(8,128)(2,1)}, u32[]{:S(2)}, u32[]{:S(2)}) %collective-permute-start.11) | collective-permute-done | bytes 368672 | tf_op jit(solution)/shard_map/ppermute | solution.py:1113
  63.3 11.6 %collective-permute-done.6 = bf16[4,128,384]{2,1,0:T(8,128)(2,1)} collective-permute-done((bf16[4,128,384]{2,1,0:T(8,128)(2,1)}, bf16[4,128,384]{2,1,0:T(8,128)(2,1)}, u32[]{:S(2)}, u32[]{:S(2)}) %collective-permute-start.6) | collective-permute-done | bytes 393248 | tf_op jit(solution)/shard_map/ppermute | solution.py:1113
  88.5 23.0 %attend_fast.1 = (bf16[1024,384]{1,0:T(8,128)(2,1)S(1)}, f32[3,8,1024]{2,1,0:T(8,128)S(1)}) custom-call(s32[1]{0:T(128)S(6)} %copy.104.res, bf16[1024,1152]{1,0:T(8,128)(2,1)S(1)} %convolution_convert_fusion.q_ref.k_ref.v_ref, bf16[1024,1152]{1,0:T(8,128)(2,1)S(1)} %convolution_convert_fusion.q_ref.k_ref.v_ref, ...), custom_call_target="tpu_custom_call" | custom-call | tf_op jit(solution)/shard_map/attend_fast/pallas_call | solution.py:674
  120.0 16.6 %collective-permute-done.15.refs_2_ = bf16[1024,384]{1,0:T(8,128)(2,1)} collective-permute-done((bf16[1024,384]{1,0:T(8,128)(2,1)}, bf16[1024,384]{1,0:T(8,128)(2,1)}, u32[]{:S(2)}, u32[]{:S(2)}) %collective-permute-start.15) | collective-permute-done | bytes 786464 | tf_op jit(solution)/shard_map/ppermute | solution.py:1113
  143.2 4.0 all-to-all-start
  148.5 26.3 %shared_units.1 = (bf16[1024,768]{1,0:T(8,128)(2,1)}, bf16[1024,768]{1,0:T(8,128)(2,1)}, bf16[1024,768]{1,0:T(8,128)(2,1)}, bf16[1024,768]{1,0:T(8,128)(2,1)}, bf16[384,1536]{1,0:T(8,128)(2,1)}) custom-call(bf16[1024,384]{1,0:T(8,128)(2,1)} %fusion.11.refs_0_, bf16[1024,384]{1,0:T(8,128)(2,1)} %collective-permute-done.14.refs_1_, ...), custom_call_target="tpu_custom_call" | custom-call | tf_op jit(solution)/shard_map/shared_units/pallas_call | solution.py:617
  179.5 61.5 %routed_experts.1 = (bf16[1024,384]{1,0:T(8,128)(2,1)}, bf16[1024,384]{1,0:T(8,128)(2,1)}, bf16[1024,384]{1,0:T(8,128)(2,1)}, bf16[1024,384]{1,0:T(8,128)(2,1)},...) custom-call(s32[3]{0:T(128)} %pad_add_fusion.ids, ...), custom_call_target="tpu_custom_call" | custom-call | tf_op jit(solution)/shard_map/routed_experts/pallas_call | solution.py:587
  272.0 7.7 %collective-permute-done.36 = bf16[384,1536]{1,0:T(8,128)(2,1)} collective-permute-done((bf16[384,1536]{1,0:T(8,128)(2,1)}, bf16[384,1536]{1,0:T(8,128)(2,1)}, u32[]{:S(2)}, u32[]{:S(2)}) %collective-permute-start.36) | collective-permute-done | bytes 1179680 | tf_op jit(solution)/shard_map/ppermute | solution.py:1113
  293.5 26.1 %attend_back_fast.1 = (bf16[1024,384]{1,0:T(8,128)(2,1)S(1)}, bf16[1024,384]{1,0:T(8,128)(2,1)S(1)}, bf16[1024,384]{1,0:T(8,128)(2,1)S(1)}) custom-call(s32[1]{0:T(128)S(6)} %copy.104.res, bf16[1024,1152]{1,0:T(8,128)(2,1)S(1)} %convolution_convert_fusion.q_ref.k_ref.v_ref, bf16[1024,1152]{1,0:T(8,128)(2,1)S(1)} %convolution_convert_fusion.q_ref.k_ref.v_ref, ...), custom_call_target="tpu_custom_call" | custom-call | tf_op jit(solution)/shard_map/attend_back_fast/pallas_call | solution.py:756
  329.7 7.5 %first_back.1 = (f32[1024,384]{1,0:T(8,128)}, f32[2,384,384]{2,1,0:T(8,128)S(1)}, bf16[2,384,384]{2,1,0:T(8,128)(2,1)}, f32[32,8,512]{2,1,0:T(8,128)}) custom-call(s32[3]{0:T(128)S(1)} %copy-done.24, bf16[1024,384]{1,0:T(8,128)(2,1)S(1)} %get-tuple-element.234.dq, bf16[1024,384]{1,0:T(8,128)(2,1)S(1)} %get-tuple-element.235.dk, ...), custom_call_target="tpu_custom_call" | custom-call | tf_op jit(solution)/shard_map/first_back/pallas_call | solution.py:1072
  338.3 10.3 %collective-permute-start.46 = (bf16[384,1536]{1,0:T(8,128)(2,1)}, bf16[384,1536]{1,0:T(8,128)(2,1)}, u32[]{:S(2)}, u32[]{:S(2)}) collective-permute-start(bf16[384,1536]{1,0:T(8,128)(2,1)} %add_convert_fusion.2), channel_id=1, source_target_pairs={{0,8},{1,9},{2,10},{3,11},{4,12},{5,13},{6,14},{7,15},{24,16},{25,... | collective-permute-start | bytes 3538952 | tf_op jit(solution)/shard_map/ppermute | solution.py:1113
  354.7 7.5 %all-to-all-start.1 = ((f32[32,8,512]{2,1,0:T(8,128)}), f32[32,8,512]{2,1,0:T(8,128)}, u32[]{:S(2)}, u32[]{:S(2)}) async-start(f32[32,8,512]{2,1,0:T(8,128)} %get-tuple-element.247), calls=%async_computation.1 | async-start | bytes 1048576 | tf_op jit(solution)/shard_map/all_to_all | solution.py:1433
  362.3 11.9 %collective-permute-done.46 = bf16[384,1536]{1,0:T(8,128)(2,1)} collective-permute-done((bf16[384,1536]{1,0:T(8,128)(2,1)}, bf16[384,1536]{1,0:T(8,128)(2,1)}, u32[]{:S(2)}, u32[]{:S(2)}) %collective-permute-start.46) | collective-permute-done | bytes 1179680 | tf_op jit(solution)/shard_map/ppermute | solution.py:1113
  380.2 5.4 %collective-permute-done.49 = bf16[384,384]{1,0:T(8,128)(2,1)S(1)} collective-permute-done((bf16[384,384]{1,0:T(8,128)(2,1)S(1)}, bf16[384,384]{1,0:T(8,128)(2,1)S(1)}, u32[]{:S(2)}, u32[]{:S(2)}) %collective-permute-start.49) | collective-permute-done | bytes 294944 | tf_op jit(solution)/shard_map/ppermute | solution.py:1113
  387.4 5.6 %collective-permute-start.50 = (bf16[384,384]{1,0:T(8,128)(2,1)}, bf16[384,384]{1,0:T(8,128)(2,1)}, u32[]{:S(2)}, u32[]{:S(2)}) collective-permute-start(bf16[384,384]{1,0:T(8,128)(2,1)} %fusion.15), channel_id=1, source_target_pairs={{0,8},{1,9},{2,10},{3,11}} | collective-permute-start | bytes 884744 | tf_op jit(solution)/shard_map/ppermute | solution.py:1113
  409.6 8.5 %all-to-all-start.2 = ((bf16[32,56,384]{2,1,0:T(8,128)(2,1)}), bf16[32,56,384]{2,1,0:T(8,128)(2,1)}, u32[]{:S(2)}, u32[]{:S(2)}) async-start(bf16[32,56,384]{2,1,0:T(8,128)(2,1)} %copy-done.12), calls=%async_computation.2 | async-start | bytes 2752512 | tf_op jit(solution)/shard_map/all_to_all | solution.py:1457
  418.1 25.2 %ortho_owned.1 = bf16[32,48,384]{2,1,0:T(8,128)(2,1)} custom-call(s32[3]{0:T(128)S(1)} %copy-done.24, f32[4,384,384]{2,1,0:T(8,128)S(1)} %copy-done.11, f32[32,48,384]{2,1,0:T(8,128)} %all-to-all-done.moment), custom_call_target="tpu_custom_call" | custom-call | tf_op jit(solution)/shard_map/ortho_owned/pallas_call | solution.py:953
  443.3 8.0 %all-to-all-done.2.grads = bf16[32,56,384]{2,1,0:T(8,128)(2,1)} async-done(((bf16[32,56,384]{2,1,0:T(8,128)(2,1)}), bf16[32,56,384]{2,1,0:T(8,128)(2,1)}, u32[]{:S(2)}, u32[]{:S(2)}) %all-to-all-start.2) | async-done | bytes 1376288 | tf_op jit(solution)/shard_map/all_to_all | solution.py:1457
  451.3 3.8 all-to-all-start.3
  462.1 22.1 %all-to-all-done.3.orthos = bf16[32,48,384]{2,1,0:T(8,128)(2,1)} async-done(((bf16[32,48,384]{2,1,0:T(8,128)(2,1)}), bf16[32,48,384]{2,1,0:T(8,128)(2,1)}, u32[]{:S(2)}, u32[]{:S(2)}) %all-to-all-start.3) | async-done | bytes 1179680 | tf_op jit(solution)/shard_map/all_to_all | solution.py:1461
  487.4 4.1 update.1
  (382 shorter events, 161.5 us)
Async XLA Ops:
  7.2 141.3 %all-gather.3.cloned.1.call-start = ((), (), s32[]{:S(2)}) async-start(), calls=%async_computation.4 | async-start | bytes 6635520 | tf_op jit(solution)/shard_map/all_gather | solution.py:1258
  27.8 23.9 %collective-permute-start.3 = (bf16[128,384]{1,0:T(8,128)(2,1)S(1)}, bf16[128,384]{1,0:T(8,128)(2,1)S(1)}, u32[]{:S(2)}, u32[]{:S(2)}) collective-permute-start(bf16[128,384]{1,0:T(8,128)(2,1)S(1)} %fusion.25), channel_id=1, source_target_pairs={{0,24},{1,25},{2,26},{3,27},{4,28},{5,29},{6,30},{7,31},{8,0},{9,1... | collective-permute-start | bytes 294920 | tf_op jit(solution)/shard_map/ppermute | solution.py:1113
  84.0 27.5 %collective-permute-start.13 = (bf16[1024,384]{1,0:T(8,128)(2,1)}, bf16[1024,384]{1,0:T(8,128)(2,1)S(1)}, u32[]{:S(2)}, u32[]{:S(2)}) collective-permute-start(bf16[1024,384]{1,0:T(8,128)(2,1)} %fusion.7.refs_4_), channel_id=1, source_target_pairs={{0,2},{1,3},{2,0},{3,1},{4,6},{5,7},{6,4},{7,5},{8,10},{9,11},{10,... | collective-permute-start | bytes 2359304 | tf_op jit(solution)/shard_map/ppermute | solution.py:1113
  117.8 24.7 %collective-permute-start.14 = (bf16[1024,384]{1,0:T(8,128)(2,1)}, bf16[1024,384]{1,0:T(8,128)(2,1)}, u32[]{:S(2)}, u32[]{:S(2)}) collective-permute-start(bf16[1024,384]{1,0:T(8,128)(2,1)} %fusion.11.refs_0_), channel_id=1, source_target_pairs={{0,1},{1,0},{2,3},{3,2},{4,5},{5,4},{6,7},{7,6},{8,9},{9,8},{10,11... | collective-permute-start | bytes 2359304 | tf_op jit(solution)/shard_map/ppermute | solution.py:1113
  118.4 24.8 %collective-permute-start.18 = (bf16[1024,384]{1,0:T(8,128)(2,1)}, bf16[1024,384]{1,0:T(8,128)(2,1)}, u32[]{:S(2)}, u32[]{:S(2)}) collective-permute-start(bf16[1024,384]{1,0:T(8,128)(2,1)} %copy-done.37), channel_id=1, source_target_pairs={{0,1},{1,0},{2,3},{3,2},{4,5},{5,4},{6,7},{7,6},{8,9},{9,8},{10,11... | collective-permute-start | bytes 2359304 | tf_op jit(solution)/shard_map/ppermute | solution.py:1113
  143.2 97.8 %all-to-all-start = ((f32[32,48,384]{2,1,0:T(8,128)}), f32[32,48,384]{2,1,0:T(8,128)}, u32[]{:S(2)}, u32[]{:S(2)}) async-start(f32[32,48,384]{2,1,0:T(8,128)} %pack_owned.1), calls=%async_computation | async-start | bytes 4718592 | tf_op jit(solution)/shard_map/all_to_all | solution.py:1317
  177.1 63.9 %collective-permute-start.25 = (bf16[384,384]{1,0:T(8,128)(2,1)}, bf16[384,384]{1,0:T(8,128)(2,1)}, u32[]{:S(2)}, u32[]{:S(2)}) collective-permute-start(bf16[384,384]{1,0:T(8,128)(2,1)} %get-tuple-element.289), channel_id=1, source_target_pairs={{0,1},{1,0},{2,3},{3,2},{4,5},{5,4},{6,7},{7,6},{8,9},{9,8},{10,11... | collective-permute-start | bytes 884744 | tf_op jit(solution)/shard_map/ppermute | solution.py:1113
  177.1 64.0 %collective-permute-start.26 = (bf16[384,384]{1,0:T(8,128)(2,1)}, bf16[384,384]{1,0:T(8,128)(2,1)}, u32[]{:S(2)}, u32[]{:S(2)}) collective-permute-start(bf16[384,384]{1,0:T(8,128)(2,1)} %get-tuple-element.288), channel_id=1, source_target_pairs={{0,2},{1,3},{2,0},{3,1},{4,6},{5,7},{6,4},{7,5},{8,10},{9,11},{10,... | collective-permute-start | bytes 884744 | tf_op jit(solution)/shard_map/ppermute | solution.py:1113
  178.7 62.3 %collective-permute-start.27 = (bf16[384,384]{1,0:T(8,128)(2,1)}, bf16[384,384]{1,0:T(8,128)(2,1)}, u32[]{:S(2)}, u32[]{:S(2)}) collective-permute-start(bf16[384,384]{1,0:T(8,128)(2,1)} %get-tuple-element.287), channel_id=1, source_target_pairs={{0,3},{1,2},{2,1},{3,0},{4,7},{5,6},{6,5},{7,4},{8,11},{9,10},{10,... | collective-permute-start | bytes 884744 | tf_op jit(solution)/shard_map/ppermute | solution.py:1113
  241.6 30.4 %collective-permute-start.37 = (bf16[384,1536]{1,0:T(8,128)(2,1)}, bf16[384,1536]{1,0:T(8,128)(2,1)}, u32[]{:S(2)}, u32[]{:S(2)}) collective-permute-start(bf16[384,1536]{1,0:T(8,128)(2,1)} %get-tuple-element.199), channel_id=1, source_target_pairs={{0,8},{1,9},{2,10},{3,11},{4,12},{5,13},{6,14},{7,15},{16,24},{17,... | collective-permute-start | bytes 3538952 | tf_op jit(solution)/shard_map/ppermute | solution.py:1113
  250.7 29.1 %collective-permute-start.36 = (bf16[384,1536]{1,0:T(8,128)(2,1)}, bf16[384,1536]{1,0:T(8,128)(2,1)}, u32[]{:S(2)}, u32[]{:S(2)}) collective-permute-start(bf16[384,1536]{1,0:T(8,128)(2,1)} %get-tuple-element.198), channel_id=1, source_target_pairs={{0,4},{1,5},{2,6},{3,7},{4,0},{5,1},{6,2},{7,3},{8,12},{9,13},{10,... | collective-permute-start | bytes 3538952 | tf_op jit(solution)/shard_map/ppermute | solution.py:1113
  255.1 24.7 %collective-permute-start.33 = (bf16[1024,384]{1,0:T(8,128)(2,1)}, bf16[1024,384]{1,0:T(8,128)(2,1)S(1)}, u32[]{:S(2)}, u32[]{:S(2)}) collective-permute-start(bf16[1024,384]{1,0:T(8,128)(2,1)} %add_convert_fusion.7), channel_id=1, source_target_pairs={{0,2},{1,3},{2,0},{3,1},{4,6},{5,7},{6,4},{7,5},{8,10},{9,11},{10,... | collective-permute-start | bytes 2359304 | tf_op jit(solution)/shard_map/ppermute | solution.py:1113
  263.6 58.0 %collective-permute-start.41 = (bf16[384,1536]{1,0:T(8,128)(2,1)}, bf16[384,1536]{1,0:T(8,128)(2,1)}, u32[]{:S(2)}, u32[]{:S(2)}) collective-permute-start(bf16[384,1536]{1,0:T(8,128)(2,1)} %constant_dynamic-update-slice_fusion.2), channel_id=1, source_target_pairs={{0,4},{1,5},{2,6},{3,7},{8,12},{9,13},{10,14},{11,15},{16,20},{17,... | collective-permute-start | bytes 3538952 | tf_op jit(solution)/shard_map/ppermute | solution.py:1113
  269.3 52.4 %collective-permute-start.40 = (bf16[384,1536]{1,0:T(8,128)(2,1)}, bf16[384,1536]{1,0:T(8,128)(2,1)}, u32[]{:S(2)}, u32[]{:S(2)}) collective-permute-start(bf16[384,1536]{1,0:T(8,128)(2,1)} %get-tuple-element.223), channel_id=1, source_target_pairs={{4,0},{5,1},{6,2},{7,3},{12,8},{13,9},{14,10},{15,11},{20,16},{21,... | collective-permute-start | bytes 3538952 | tf_op jit(solution)/shard_map/ppermute | solution.py:1113
  289.1 32.6 %collective-permute-start.38 = (bf16[384,1536]{1,0:T(8,128)(2,1)S(1)}, bf16[384,1536]{1,0:T(8,128)(2,1)}, u32[]{:S(2)}, u32[]{:S(2)}) collective-permute-start(bf16[384,1536]{1,0:T(8,128)(2,1)S(1)} %add_convert_fusion.5), channel_id=1, source_target_pairs={{8,0},{9,1},{10,2},{11,3},{12,4},{13,5},{14,6},{15,7},{24,16},{25,... | collective-permute-start | bytes 3538952 | tf_op jit(solution)/shard_map/ppermute | solution.py:1113
  290.4 31.3 %collective-permute-start.39 = (bf16[384,1536]{1,0:T(8,128)(2,1)S(1)}, bf16[384,1536]{1,0:T(8,128)(2,1)}, u32[]{:S(2)}, u32[]{:S(2)}) collective-permute-start(bf16[384,1536]{1,0:T(8,128)(2,1)S(1)} %add_convert_fusion.4), channel_id=1, source_target_pairs={{8,24},{9,25},{10,26},{11,27},{12,28},{13,29},{14,30},{15,31}} | collective-permute-start | bytes 3538952 | tf_op jit(solution)/shard_map/ppermute | solution.py:1113
  292.1 29.6 %collective-permute-start.42 = (bf16[1024,384]{1,0:T(8,128)(2,1)}, bf16[1024,384]{1,0:T(8,128)(2,1)S(1)}, u32[]{:S(2)}, u32[]{:S(2)}) collective-permute-start(bf16[1024,384]{1,0:T(8,128)(2,1)} %add_convert_fusion.6), channel_id=1, source_target_pairs={{0,2},{1,3},{2,0},{3,1},{4,6},{5,7},{6,4},{7,5},{8,10},{9,11},{10,... | collective-permute-start | bytes 2359304 | tf_op jit(solution)/shard_map/ppermute | solution.py:1113
  338.3 35.9 %collective-permute-start.46 = (bf16[384,1536]{1,0:T(8,128)(2,1)}, bf16[384,1536]{1,0:T(8,128)(2,1)}, u32[]{:S(2)}, u32[]{:S(2)}) collective-permute-start(bf16[384,1536]{1,0:T(8,128)(2,1)} %add_convert_fusion.2), channel_id=1, source_target_pairs={{0,8},{1,9},{2,10},{3,11},{4,12},{5,13},{6,14},{7,15},{24,16},{25,... | collective-permute-start | bytes 3538952 | tf_op jit(solution)/shard_map/ppermute | solution.py:1113
  351.8 52.3 %collective-permute-start.43 = (bf16[384,1536]{1,0:T(8,128)(2,1)S(1)}, bf16[384,1536]{1,0:T(8,128)(2,1)}, u32[]{:S(2)}, u32[]{:S(2)}) collective-permute-start(bf16[384,1536]{1,0:T(8,128)(2,1)S(1)} %add_convert_fusion.3.refs_0_), channel_id=1, source_target_pairs={{16,0},{17,1},{18,2},{19,3},{20,4},{21,5},{22,6},{23,7}} | collective-permute-start | bytes 3538952 | tf_op jit(solution)/shard_map/ppermute | solution.py:1113
  353.1 51.0 %collective-permute-start.48 = (bf16[384,1536]{1,0:T(8,128)(2,1)S(1)}, bf16[384,1536]{1,0:T(8,128)(2,1)}, u32[]{:S(2)}, u32[]{:S(2)}) collective-permute-start(bf16[384,1536]{1,0:T(8,128)(2,1)S(1)} %add_convert_fusion.1.refs_4_), channel_id=1, source_target_pairs={{28,24},{29,25},{30,26},{31,27}} | collective-permute-start | bytes 3538952 | tf_op jit(solution)/shard_map/ppermute | solution.py:1113
  354.7 40.6 %all-to-all-start.1 = ((f32[32,8,512]{2,1,0:T(8,128)}), f32[32,8,512]{2,1,0:T(8,128)}, u32[]{:S(2)}, u32[]{:S(2)}) async-start(f32[32,8,512]{2,1,0:T(8,128)} %get-tuple-element.247), calls=%async_computation.1 | async-start | bytes 1048576 | tf_op jit(solution)/shard_map/all_to_all | solution.py:1433
  378.5 25.6 %collective-permute-start.47 = (bf16[384,1536]{1,0:T(8,128)(2,1)S(1)}, bf16[384,1536]{1,0:T(8,128)(2,1)}, u32[]{:S(2)}, u32[]{:S(2)}) collective-permute-start(bf16[384,1536]{1,0:T(8,128)(2,1)S(1)} %add_convert_fusion.refs_2_), channel_id=1, source_target_pairs={{8,16},{9,17},{10,18},{11,19},{12,20},{13,21},{14,22},{15,23}} | collective-permute-start | bytes 3538952 | tf_op jit(solution)/shard_map/ppermute | solution.py:1113
  409.6 41.8 %all-to-all-start.2 = ((bf16[32,56,384]{2,1,0:T(8,128)(2,1)}), bf16[32,56,384]{2,1,0:T(8,128)(2,1)}, u32[]{:S(2)}, u32[]{:S(2)}) async-start(bf16[32,56,384]{2,1,0:T(8,128)(2,1)} %copy-done.12), calls=%async_computation.2 | async-start | bytes 2752512 | tf_op jit(solution)/shard_map/all_to_all | solution.py:1457
  451.3 32.8 %all-to-all-start.3 = ((bf16[32,48,384]{2,1,0:T(8,128)(2,1)}), bf16[32,48,384]{2,1,0:T(8,128)(2,1)}, u32[]{:S(2)}, u32[]{:S(2)}) async-start(bf16[32,48,384]{2,1,0:T(8,128)(2,1)} %ortho_owned.1), calls=%async_computation.3 | async-start | bytes 2359296 | tf_op jit(solution)/shard_map/all_to_all | solution.py:1461
  (97 other events, 1054.0 us)
Sparse Core Ops, SparseCore 0:
  54.4 94.0 all-gather.2

commit v4 on v3

--- a/solution.py
+++ b/solution.py
@@ -413,8 +413,7 @@
 bf = jnp.bfloat16
 f32 = jnp.float32
 TOK = 1024
-ROWS = 512
-UNITS = 512
+UNITS = 768
 NN = (((1,), (0,)), ((), ()))
 NT = (((1,), (1,)), ((), ()))
 TN = (((0,), (0,)), ((), ()))
@@ -481,13 +480,22 @@
         token_loads.append((metas[i], meta.at[i], tok_sem.at[i, 2]))
         token_loads.append((priors[i], part.at[i], tok_sem.at[i, 3]))
     loads = start_all(loads)
-    tokens = start_all(token_loads)
+    start_all(token_loads)
     g_up[...] = jnp.zeros_like(g_up)
     g_down[...] = jnp.zeros_like(g_down)
     wait_all(loads)
-    wait_all(tokens)
+
+    def results(i):
+        return [
+            pltpu.make_async_copy(part.at[i, :, pl.ds(0, D)], mix_out[i], out_sem.at[i]),
+            pltpu.make_async_copy(part.at[i, :, pl.ds(D, D)], dx_out[i], out_sem.at[5 + i]),
+        ]
 
     def one_source(s, carry):
+        pltpu.make_async_copy(hidden[0], tok.at[s, :, pl.ds(0, D)], tok_sem.at[s, 0]).wait()
+        pltpu.make_async_copy(d_mix[0], tok.at[s, :, pl.ds(D, D)], tok_sem.at[s, 1]).wait()
+        pltpu.make_async_copy(metas[0], meta.at[s], tok_sem.at[s, 2]).wait()
+        pltpu.make_async_copy(priors[0], part.at[s], tok_sem.at[s, 3]).wait()
         acc[...] = part[s].astype(f32)
 
         def routed(e, carry):
@@ -511,14 +519,19 @@
 
         lax.fori_loop(0, 2, routed, 0)
         part[s] = acc[...].astype(bf)
+        for i in range(4):
+
+            @pl.when(s == i)
+            def _():
+                for copy in results(i):
+                    copy.start()
+
         return carry
 
     lax.fori_loop(0, 4, one_source, 0)
-    outs = start_all(
-        [(part.at[i, :, pl.ds(0, D)], mix_out[i], out_sem.at[i]) for i in range(4)]
-        + [(part.at[i, :, pl.ds(D, D)], dx_out[i], out_sem.at[5 + i]) for i in range(4)]
-        + [(d_gate, d_gate_out, out_sem.at[4])]
-    )
+    outs = start_all([(d_gate, d_gate_out, out_sem.at[4])])
+    for i in range(4):
+        outs += results(i)
     for e in range(2):
         stage[2 * e] = g_up[e].astype(bf)
         stage[2 * e + 1] = g_down[e].astype(bf)
@@ -555,23 +568,26 @@
     for i in range(4):
         token_loads.append((hidden[i], tok.at[i, :, pl.ds(0, D)], tok_sem.at[i, 0]))
         token_loads.append((d_mix[i], tok.at[i, :, pl.ds(D, D)], tok_sem.at[i, 1]))
-    tokens = start_all(token_loads)
+    start_all(token_loads)
     g_up[...] = jnp.zeros_like(g_up)
     g_down[...] = jnp.zeros_like(g_down)
     wait_all(loads)
-    outs = []
-    for i in range(4):
-        wait_all(tokens[2 * i : 2 * i + 2])
-
-        def some_rows(r, carry, i=i):
-            rows = pl.ds(pl.multiple_of(r * ROWS, ROWS), ROWS)
-            out, dx = units(tok[i, rows, :D], tok[i, rows, D:], up, down, g_up, g_down, 2 * D)
-            part[i, rows, :D] = out.astype(bf)
-            part[i, rows, D:] = dx.astype(bf)
-            return carry
-
-        lax.fori_loop(0, TOK // ROWS, some_rows, 0)
-        outs += start_all([(part.at[i], part_out[i], out_sem.at[i])])
+    def one_source(i, carry):
+        pltpu.make_async_copy(hidden[0], tok.at[i, :, pl.ds(0, D)], tok_sem.at[i, 0]).wait()
+        pltpu.make_async_copy(d_mix[0], tok.at[i, :, pl.ds(D, D)], tok_sem.at[i, 1]).wait()
+        out, dx = units(tok[i, :, :D], tok[i, :, D:], up, down, g_up, g_down, 2 * D)
+        part[i, :, :D] = out.astype(bf)
+        part[i, :, D:] = dx.astype(bf)
+        for k in range(4):
+
+            @pl.when(i == k)
+            def _():
+                pltpu.make_async_copy(part.at[k], part_out[k], out_sem.at[k]).start()
+
+        return carry
+
+    lax.fori_loop(0, 4, one_source, 0)
+    outs = [pltpu.make_async_copy(part.at[k], part_out[k], out_sem.at[k]) for k in range(4)]
     for s in range(2):
         stage[:, 2 * s * D : 2 * s * D + D] = g_up[:, s * D : s * D + D].astype(bf)
         stage[:, 2 * s * D + D : 2 * s * D + 2 * D] = g_down[:, s * D : s * D + D].astype(bf)
@@ -1151,14 +1167,13 @@
     return jnp.concatenate(parts, axis=axis)
 
 
-def gather_rows(rows, z, x, c):
-    pieces = [send(rows, to_z(step)) for step in (3, 2, 1)] + [rows]
-    pieces = [pieces[2], pieces[1], pieces[0]]
-    recv = {step: send_piece for step, send_piece in zip((1, 2, 3), pieces)}
-    ring = jnp.stack([recv[3], recv[2], recv[1], rows])
-    doubled = jnp.concatenate([ring, ring])
-    by_z = lax.dynamic_slice_in_dim(doubled, (3 - z) % 4, 4, 0)
-    by_zx = jnp.stack(in_order(by_z, send(by_z, to_x), x), axis=1)
+def gather_z(rows, z):
+    ring = jnp.stack([send(rows, to_z(step)) for step in (3, 2, 1)] + [rows])
+    return lax.dynamic_slice_in_dim(jnp.concatenate([ring, ring]), (3 - z) % 4, 4, 0)
+
+
+def gather_core(by_z, received, x, c):
+    by_zx = jnp.stack(in_order(by_z, received, x), axis=1)
     return jnp.stack(in_order(by_zx, send(by_zx, to_core), c), axis=2)
 
 
@@ -1201,6 +1216,10 @@
     z, x = wide // 2, wide % 2
     y, c = narrow // 2, narrow % 2
 
+    up_t = turned(w_up).astype(bf)
+    down_t = turned(w_down).astype(bf)
+    routed_t = jnp.stack([up_t[:8], down_t[:8]], axis=1).reshape(4, 4, 48, D)
+    shared_t = jnp.stack([up_t[8:], down_t[8:]], axis=1).reshape(4, 48, D)
     square_t = turned(w_square).astype(bf)
     out_t = turned(w_out).astype(bf)[None]
     misc = jnp.concatenate(
@@ -1234,10 +1253,17 @@
     def my_half(block):
         return pick(block.reshape(5, 2, 24, D), c, 1).reshape(120, D)
 
+    mine = [pick(routed_t, narrow)]
+    mine += [send(pick(routed_t, narrow ^ k), NARROW_MOVES[k]) for k in (1, 2, 3)]
     first_rows = jnp.concatenate([my_half(rows[:240]), rows[240:248]])
-    first_all = gather_rows(first_rows, z, x, c)
-    first_all, moments = lax.optimization_barrier((first_all, moments))
-    second_all = gather_rows(my_half(rows[248:]), z, x, c)
+    first_z = gather_z(first_rows, z)
+    first_z, blocks = lax.optimization_barrier((first_z, jnp.stack(mine + [shared_t])))
+    gathered = lax.all_gather(blocks, WIDE)
+    first_x = send(first_z, to_x)
+    first_x, second_rows, moments = lax.optimization_barrier((first_x, rows[248:], moments))
+    second_z = gather_z(my_half(second_rows), z)
+    first_all = gather_core(first_z, first_x, x, c)
+    second_all = gather_core(second_z, send(second_z, to_x), x, c)
 
     def assemble(gathered):
         parts = gathered[..., :120, :].reshape(8, 2, 5, 24, D)
@@ -1248,14 +1274,6 @@
     misc_all = first_all[:, :, 0, 120:, :].reshape(8, 8, 4, 96)
     bias_low = misc_all[:, 0, :, :72].reshape(-1)
     router_low = jnp.transpose(misc_all[:, 1:3, :, :48], (2, 1, 0, 3)).reshape(ROUTED, D)
-
-    up_t = turned(w_up).astype(bf)
-    down_t = turned(w_down).astype(bf)
-    routed_t = jnp.stack([up_t[:8], down_t[:8]], axis=1).reshape(4, 4, 48, D)
-    shared_t = jnp.stack([up_t[8:], down_t[8:]], axis=1).reshape(4, 48, D)
-    mine = [pick(routed_t, narrow)]
-    mine += [send(pick(routed_t, narrow ^ k), NARROW_MOVES[k]) for k in (1, 2, 3)]
-    gathered = lax.all_gather(jnp.stack(mine + [shared_t]), WIDE)
 
     res_group = resolution[0]
     token_f = tokens.astype(f32)
@@ -1307,13 +1325,17 @@
     hidden_core, meta_core = send(hidden_two, to_core), send(meta, to_core)
     hidden_y, meta_y = send(hidden_two, to_y), send(meta, to_y)
     meta_diag = send(meta, to_diag)
-    hidden_y, _ = lax.optimization_barrier((hidden_y, meta))
+    hidden_y, meta_y, meta_core, meta_diag = lax.optimization_barrier(
+        (hidden_y, meta_y, meta_core, meta_diag)
+    )
     hidden_diag = send(hidden_y, to_core)
     place_ids = jnp.stack([narrow, z, x]).astype(jnp.int32)
     hiddens = (hidden_two, hidden_core, hidden_y, hidden_diag)
     d_mixes = (d_mixture, d_mix_core, d_mix_y, d_mix_diag)
     metas = (meta, meta_core, meta_y, meta_diag)
-    hiddens, d_mixes, metas, moments = lax.optimization_barrier((hiddens, d_mixes, metas, moments))
+    hiddens, d_mixes, metas, gathered, moments = lax.optimization_barrier(
+        (hiddens, d_mixes, metas, gathered, moments)
+    )
     moments = lax.all_to_all(moments, AXES, 0, 0, tiled=True)
     *priors, g_shared = shared_units(hiddens, d_mixes, gathered)
 

time: 504 us -> 497 us (0.986)
  waiting for transfers between devices: 108 us -> 118 us
  Pallas kernels: 180 us -> 172 us
  local copies, waits for them, and re-layouts: 38 us -> 31.2 us
    ppermute x53, waiting for transfers between devices: 75.8 us -> 88.2 us  [send(): return lax.ppermute(array, AXES, route_pairs(move))]
    pallas_call x1, Pallas kernels: 61.5 us -> 56.4 us  [routed_experts(): pl.pallas_call(routed_kernel, out_shape=shapes, in_specs=[pl.BlockSpec(me...]
    unnamed x147 -> x143, local copies, waits for them, and re-layouts: 22 us -> 22 us
  transfers between devices with their start and end apart: 58 -> 58, of which waited for: 17 -> 18; matrix products, arithmetic and copies ran while one was open for 14% -> 13% of each run, Pallas kernels for 33% -> 32%
where the time goes in v4:
time: 497 us; the launch traced here: 491 us
  Pallas kernels  172 us (35%)
  waiting for transfers between devices  118 us (24%)
  starting transfers between devices  92.4 us (19%)
  other arithmetic  48.5 us (10%)
  local copies, waits for them, and re-layouts  31.2 us (6%)
  between operations  19.3 us (4%)
  matrix products  9.21 us (2%)
    ppermute x53, waiting for transfers between devices, send(): return lax.ppermute(array, AXES, route_pairs(move))  88.2 us
    ppermute x53, starting transfers between devices, send(): return lax.ppermute(array, AXES, route_pairs(move))  69 us
    pallas_call x1, Pallas kernels, routed_experts(): pl.pallas_call(routed_kernel, out_shape=shapes, in_specs=[pl.BlockSpec(me...  56.4 us
    pallas_call x1, Pallas kernels, attend_back_fast(): pl.pallas_call(attend_back_kernel, grid_spec=pltpu.PrefetchScalarGridSpec...  26 us
    pallas_call x1, Pallas kernels, ortho_owned(): pl.pallas_call(ortho_kernel, out_shape=jax.ShapeDtypeStruct((32, 48, D),...  25.2 us
    pallas_call x1, Pallas kernels, shared_units(): pl.pallas_call(shared_kernel, out_shape=shapes, in_specs=[anyspec] * 9, o...  24.1 us
    pallas_call x1, Pallas kernels, attend_fast(): pl.pallas_call(attend_kernel, grid_spec=pltpu.PrefetchScalarGridSpec(num_...  23 us
    all_to_all x1, waiting for transfers between devices, fast_device(): ortho_parts = lax.all_to_all(ortho_cut, AXES, 0, 0, tiled=True)  22.1 us
  transfers between devices with their start and end apart: 58, of which 18 were waited for; matrix products, arithmetic and copies ran while one was open for 13% of the time, Pallas kernels for 32%

profile of v4, /device:TPU:0, one launch (start us, length us, event | category | flops | bytes accessed | tf_op | source)
XLA Modules:
  0.0 491.3 jit_solution(13913963421844779237)
XLA Ops:
  27.4 6.8 %collective-permute-done.4 = bf16[128,384]{1,0:T(8,128)(2,1)S(1)} collective-permute-done((bf16[128,384]{1,0:T(8,128)(2,1)S(1)}, bf16[128,384]{1,0:T(8,128)(2,1)S(1)}, u32[]{:S(2)}, u32[]{:S(2)}) %collective-permute-start.4) | collective-permute-done | bytes 98336 | tf_op jit(solution)/shard_map/ppermute | solution.py:1129
  42.0 8.3 %collective-permute-done.9 = bf16[4,128,384]{2,1,0:T(8,128)(2,1)S(1)} collective-permute-done((bf16[4,128,384]{2,1,0:T(8,128)(2,1)S(1)}, bf16[4,128,384]{2,1,0:T(8,128)(2,1)S(1)}, u32[]{:S(2)}, u32[]{:S(2)}) %collective-permute-start.9) | collective-permute-done | bytes 393248 | tf_op jit(solution)/shard_map/ppermute | solution.py:1129
  53.5 6.5 %collective-permute-done.11 = bf16[120,384]{1,0:T(8,128)(2,1)S(1)} collective-permute-done((bf16[120,384]{1,0:T(8,128)(2,1)S(1)}, bf16[120,384]{1,0:T(8,128)(2,1)S(1)}, u32[]{:S(2)}, u32[]{:S(2)}) %collective-permute-start.11) | collective-permute-done | bytes 92192 | tf_op jit(solution)/shard_map/ppermute | solution.py:1129
  59.9 9.3 %collective-permute-done.12 = bf16[120,384]{1,0:T(8,128)(2,1)S(1)} collective-permute-done((bf16[120,384]{1,0:T(8,128)(2,1)S(1)}, bf16[120,384]{1,0:T(8,128)(2,1)S(1)}, u32[]{:S(2)}, u32[]{:S(2)}) %collective-permute-start.12) | collective-permute-done | bytes 92192 | tf_op jit(solution)/shard_map/ppermute | solution.py:1129
  72.5 5.2 %collective-permute-done.14 = bf16[4,120,384]{2,1,0:T(8,128)(2,1)S(1)} collective-permute-done((bf16[4,120,384]{2,1,0:T(8,128)(2,1)S(1)}, bf16[4,120,384]{2,1,0:T(8,128)(2,1)S(1)}, u32[]{:S(2)}, u32[]{:S(2)}) %collective-permute-start.14) | collective-permute-done | bytes 368672 | tf_op jit(solution)/shard_map/ppermute | solution.py:1129
  89.2 23.0 %attend_fast.1 = (bf16[1024,384]{1,0:T(8,128)(2,1)S(1)}, f32[3,8,1024]{2,1,0:T(8,128)S(1)}) custom-call(s32[1]{0:T(128)S(6)} %copy.104.res, bf16[1024,1152]{1,0:T(8,128)(2,1)S(1)} %convolution_convert_fusion.q_ref.k_ref.v_ref, bf16[1024,1152]{1,0:T(8,128)(2,1)S(1)} %convolution_convert_fusion.q_ref.k_ref.v_ref, ...), custom_call_target="tpu_custom_call" | custom-call | tf_op jit(solution)/shard_map/attend_fast/pallas_call | solution.py:690
  121.1 17.3 %collective-permute-done.19.refs_10_ = f32[16,1024]{1,0:T(8,128)S(1)} collective-permute-done((f32[16,1024]{1,0:T(8,128)S(1)}, f32[16,1024]{1,0:T(8,128)S(1)}, u32[]{:S(2)}, u32[]{:S(2)}) %collective-permute-start.19) | collective-permute-done | bytes 65568 | tf_op jit(solution)/shard_map/ppermute | solution.py:1129
  143.3 3.9 all-to-all-start
  147.3 24.1 %shared_units.1 = (bf16[1024,768]{1,0:T(8,128)(2,1)}, bf16[1024,768]{1,0:T(8,128)(2,1)}, bf16[1024,768]{1,0:T(8,128)(2,1)}, bf16[1024,768]{1,0:T(8,128)(2,1)}, bf16[384,1536]{1,0:T(8,128)(2,1)}) custom-call(bf16[1024,384]{1,0:T(8,128)(2,1)} %fusion.11.refs_0_, bf16[1024,384]{1,0:T(8,128)(2,1)} %collective-permute-done.17.refs_1_, ...), custom_call_target="tpu_custom_call" | custom-call | tf_op jit(solution)/shard_map/shared_units/pallas_call | solution.py:633
  176.0 56.4 %routed_experts.1 = (bf16[1024,384]{1,0:T(8,128)(2,1)}, bf16[1024,384]{1,0:T(8,128)(2,1)}, bf16[1024,384]{1,0:T(8,128)(2,1)}, bf16[1024,384]{1,0:T(8,128)(2,1)},...) custom-call(s32[3]{0:T(128)} %pad_add_fusion.ids, ...), custom_call_target="tpu_custom_call" | custom-call | tf_op jit(solution)/shard_map/routed_experts/pallas_call | solution.py:603
  233.1 4.7 collective-permute-start.37
  264.6 7.8 %collective-permute-done.36 = bf16[384,1536]{1,0:T(8,128)(2,1)} collective-permute-done((bf16[384,1536]{1,0:T(8,128)(2,1)}, bf16[384,1536]{1,0:T(8,128)(2,1)}, u32[]{:S(2)}, u32[]{:S(2)}) %collective-permute-start.36) | collective-permute-done | bytes 1179680 | tf_op jit(solution)/shard_map/ppermute | solution.py:1129
  286.1 26.0 %attend_back_fast.1 = (bf16[1024,384]{1,0:T(8,128)(2,1)S(1)}, bf16[1024,384]{1,0:T(8,128)(2,1)S(1)}, bf16[1024,384]{1,0:T(8,128)(2,1)S(1)}) custom-call(s32[1]{0:T(128)S(6)} %copy.104.res, bf16[1024,1152]{1,0:T(8,128)(2,1)S(1)} %convolution_convert_fusion.q_ref.k_ref.v_ref, bf16[1024,1152]{1,0:T(8,128)(2,1)S(1)} %convolution_convert_fusion.q_ref.k_ref.v_ref, ...), custom_call_target="tpu_custom_call" | custom-call | tf_op jit(solution)/shard_map/attend_back_fast/pallas_call | solution.py:772
  322.1 7.5 %first_back.1 = (f32[1024,384]{1,0:T(8,128)}, f32[2,384,384]{2,1,0:T(8,128)S(1)}, bf16[2,384,384]{2,1,0:T(8,128)(2,1)}, f32[32,8,512]{2,1,0:T(8,128)}) custom-call(s32[3]{0:T(128)S(1)} %copy-done.24, bf16[1024,384]{1,0:T(8,128)(2,1)S(1)} %get-tuple-element.248.dq, bf16[1024,384]{1,0:T(8,128)(2,1)S(1)} %get-tuple-element.249.dk, ...), custom_call_target="tpu_custom_call" | custom-call | tf_op jit(solution)/shard_map/first_back/pallas_call | solution.py:1088
  330.6 10.3 %collective-permute-start.46 = (bf16[384,1536]{1,0:T(8,128)(2,1)}, bf16[384,1536]{1,0:T(8,128)(2,1)}, u32[]{:S(2)}, u32[]{:S(2)}) collective-permute-start(bf16[384,1536]{1,0:T(8,128)(2,1)} %add_convert_fusion.2), channel_id=1, source_target_pairs={{0,8},{1,9},{2,10},{3,11},{4,12},{5,13},{6,14},{7,15},{24,16},{25,... | collective-permute-start | bytes 3538952 | tf_op jit(solution)/shard_map/ppermute | solution.py:1129
  347.1 6.5 %all-to-all-start.1 = ((f32[32,8,512]{2,1,0:T(8,128)}), f32[32,8,512]{2,1,0:T(8,128)}, u32[]{:S(2)}, u32[]{:S(2)}) async-start(f32[32,8,512]{2,1,0:T(8,128)} %get-tuple-element.261), calls=%async_computation.1 | async-start | bytes 1048576 | tf_op jit(solution)/shard_map/all_to_all | solution.py:1455
  353.6 12.9 %collective-permute-done.46 = bf16[384,1536]{1,0:T(8,128)(2,1)} collective-permute-done((bf16[384,1536]{1,0:T(8,128)(2,1)}, bf16[384,1536]{1,0:T(8,128)(2,1)}, u32[]{:S(2)}, u32[]{:S(2)}) %collective-permute-start.46) | collective-permute-done | bytes 1179680 | tf_op jit(solution)/shard_map/ppermute | solution.py:1129
  372.5 5.6 %collective-permute-done.49 = bf16[384,384]{1,0:T(8,128)(2,1)S(1)} collective-permute-done((bf16[384,384]{1,0:T(8,128)(2,1)S(1)}, bf16[384,384]{1,0:T(8,128)(2,1)S(1)}, u32[]{:S(2)}, u32[]{:S(2)}) %collective-permute-start.49) | collective-permute-done | bytes 294944 | tf_op jit(solution)/shard_map/ppermute | solution.py:1129
  380.0 5.4 %collective-permute-start.50 = (bf16[384,384]{1,0:T(8,128)(2,1)}, bf16[384,384]{1,0:T(8,128)(2,1)}, u32[]{:S(2)}, u32[]{:S(2)}) collective-permute-start(bf16[384,384]{1,0:T(8,128)(2,1)} %fusion.15), channel_id=1, source_target_pairs={{0,8},{1,9},{2,10},{3,11}} | collective-permute-start | bytes 884744 | tf_op jit(solution)/shard_map/ppermute | solution.py:1129
  401.5 9.2 %all-to-all-start.2 = ((bf16[32,56,384]{2,1,0:T(8,128)(2,1)}), bf16[32,56,384]{2,1,0:T(8,128)(2,1)}, u32[]{:S(2)}, u32[]{:S(2)}) async-start(bf16[32,56,384]{2,1,0:T(8,128)(2,1)} %copy-done.12), calls=%async_computation.2 | async-start | bytes 2752512 | tf_op jit(solution)/shard_map/all_to_all | solution.py:1479
  410.7 25.2 %ortho_owned.1 = bf16[32,48,384]{2,1,0:T(8,128)(2,1)} custom-call(s32[3]{0:T(128)S(1)} %copy-done.24, f32[4,384,384]{2,1,0:T(8,128)S(1)} %copy-done.11, f32[32,48,384]{2,1,0:T(8,128)} %all-to-all-done.moment), custom_call_target="tpu_custom_call" | custom-call | tf_op jit(solution)/shard_map/ortho_owned/pallas_call | solution.py:969
  436.0 8.0 %all-to-all-done.2.grads = bf16[32,56,384]{2,1,0:T(8,128)(2,1)} async-done(((bf16[32,56,384]{2,1,0:T(8,128)(2,1)}), bf16[32,56,384]{2,1,0:T(8,128)(2,1)}, u32[]{:S(2)}, u32[]{:S(2)}) %all-to-all-start.2) | async-done | bytes 1376288 | tf_op jit(solution)/shard_map/all_to_all | solution.py:1479
  454.7 22.1 %all-to-all-done.3.orthos = bf16[32,48,384]{2,1,0:T(8,128)(2,1)} async-done(((bf16[32,48,384]{2,1,0:T(8,128)(2,1)}), bf16[32,48,384]{2,1,0:T(8,128)(2,1)}, u32[]{:S(2)}, u32[]{:S(2)}) %all-to-all-start.3) | async-done | bytes 1179680 | tf_op jit(solution)/shard_map/all_to_all | solution.py:1483
  480.1 4.1 update.1
  (377 shorter events, 155.9 us)
Async XLA Ops:
  7.2 136.1 %all-gather.3.cloned.1.call-start = ((), (), s32[]{:S(2)}) async-start(), calls=%async_computation.4 | async-start | bytes 6635520 | tf_op jit(solution)/shard_map/all_gather | solution.py:1261
  53.4 25.4 %collective-permute-start.10 = (bf16[4,2,128,384]{3,2,0,1:T(8,128)(2,1)S(1)}, bf16[4,2,128,384]{3,2,0,1:T(8,128)(2,1)S(1)}, u32[]{:S(2)}, u32[]{:S(2)}) collective-permute-start(bf16[4,2,128,384]{3,2,0,1:T(8,128)(2,1)S(1)} %pad_maximum_fusion.1), channel_id=1, source_target_pairs={{0,1},{1,0},{2,3},{3,2},{4,5},{5,4},{6,7},{7,6},{8,9},{9,8},{10,11... | collective-permute-start | bytes 2359304 | tf_op jit(solution)/shard_map/ppermute | solution.py:1129
  84.3 28.0 %collective-permute-start.16 = (bf16[1024,384]{1,0:T(8,128)(2,1)S(1)}, bf16[1024,384]{1,0:T(8,128)(2,1)S(1)}, u32[]{:S(2)}, u32[]{:S(2)}) collective-permute-start(bf16[1024,384]{1,0:T(8,128)(2,1)S(1)} %fusion.7.refs_4_), channel_id=1, source_target_pairs={{0,2},{1,3},{2,0},{3,1},{4,6},{5,7},{6,4},{7,5},{8,10},{9,11},{10,... | collective-permute-start | bytes 2359304 | tf_op jit(solution)/shard_map/ppermute | solution.py:1129
  116.8 22.3 %collective-permute-start.18 = (bf16[1024,384]{1,0:T(8,128)(2,1)}, bf16[1024,384]{1,0:T(8,128)(2,1)}, u32[]{:S(2)}, u32[]{:S(2)}) collective-permute-start(bf16[1024,384]{1,0:T(8,128)(2,1)} %fusion.11.refs_0_), channel_id=1, source_target_pairs={{0,2},{1,3},{2,0},{3,1},{4,6},{5,7},{6,4},{7,5},{8,10},{9,11},{10,... | collective-permute-start | bytes 2359304 | tf_op jit(solution)/shard_map/ppermute | solution.py:1129
  118.5 19.9 %collective-permute-start.19 = (f32[16,1024]{1,0:T(8,128)S(1)}, f32[16,1024]{1,0:T(8,128)S(1)}, u32[]{:S(2)}, u32[]{:S(2)}) collective-permute-start(f32[16,1024]{1,0:T(8,128)S(1)} %pad_maximum_fusion.7.refs_8_), channel_id=1, source_target_pairs={{0,2},{1,3},{2,0},{3,1},{4,6},{5,7},{6,4},{7,5},{8,10},{9,11},{10,... | collective-permute-start | bytes 196616 | tf_op jit(solution)/shard_map/ppermute | solution.py:1129
  143.3 89.2 %all-to-all-start = ((f32[32,48,384]{2,1,0:T(8,128)}), f32[32,48,384]{2,1,0:T(8,128)}, u32[]{:S(2)}, u32[]{:S(2)}) async-start(f32[32,48,384]{2,1,0:T(8,128)} %pack_owned.1), calls=%async_computation | async-start | bytes 4718592 | tf_op jit(solution)/shard_map/all_to_all | solution.py:1339
  173.5 58.9 %collective-permute-start.25 = (bf16[384,384]{1,0:T(8,128)(2,1)S(1)}, bf16[384,384]{1,0:T(8,128)(2,1)}, u32[]{:S(2)}, u32[]{:S(2)}) collective-permute-start(bf16[384,384]{1,0:T(8,128)(2,1)S(1)} %get-tuple-element.303), channel_id=1, source_target_pairs={{0,1},{1,0},{2,3},{3,2},{4,5},{5,4},{6,7},{7,6},{8,9},{9,8},{10,11... | collective-permute-start | bytes 884744 | tf_op jit(solution)/shard_map/ppermute | solution.py:1129
  173.7 58.7 %collective-permute-start.26 = (bf16[384,384]{1,0:T(8,128)(2,1)S(1)}, bf16[384,384]{1,0:T(8,128)(2,1)}, u32[]{:S(2)}, u32[]{:S(2)}) collective-permute-start(bf16[384,384]{1,0:T(8,128)(2,1)S(1)} %get-tuple-element.302), channel_id=1, source_target_pairs={{0,2},{1,3},{2,0},{3,1},{4,6},{5,7},{6,4},{7,5},{8,10},{9,11},{10,... | collective-permute-start | bytes 884744 | tf_op jit(solution)/shard_map/ppermute | solution.py:1129
  175.4 57.0 %collective-permute-start.27 = (bf16[384,384]{1,0:T(8,128)(2,1)S(1)}, bf16[384,384]{1,0:T(8,128)(2,1)}, u32[]{:S(2)}, u32[]{:S(2)}) collective-permute-start(bf16[384,384]{1,0:T(8,128)(2,1)S(1)} %get-tuple-element.301), channel_id=1, source_target_pairs={{0,3},{1,2},{2,1},{3,0},{4,7},{5,6},{6,5},{7,4},{8,11},{9,10},{10,... | collective-permute-start | bytes 884744 | tf_op jit(solution)/shard_map/ppermute | solution.py:1129
  233.1 31.5 %collective-permute-start.37 = (bf16[384,1536]{1,0:T(8,128)(2,1)}, bf16[384,1536]{1,0:T(8,128)(2,1)}, u32[]{:S(2)}, u32[]{:S(2)}) collective-permute-start(bf16[384,1536]{1,0:T(8,128)(2,1)} %get-tuple-element.213), channel_id=1, source_target_pairs={{0,8},{1,9},{2,10},{3,11},{4,12},{5,13},{6,14},{7,15},{16,24},{17,... | collective-permute-start | bytes 3538952 | tf_op jit(solution)/shard_map/ppermute | solution.py:1129
  243.2 29.1 %collective-permute-start.36 = (bf16[384,1536]{1,0:T(8,128)(2,1)}, bf16[384,1536]{1,0:T(8,128)(2,1)}, u32[]{:S(2)}, u32[]{:S(2)}) collective-permute-start(bf16[384,1536]{1,0:T(8,128)(2,1)} %get-tuple-element.212), channel_id=1, source_target_pairs={{0,4},{1,5},{2,6},{3,7},{4,0},{5,1},{6,2},{7,3},{8,12},{9,13},{10,... | collective-permute-start | bytes 3538952 | tf_op jit(solution)/shard_map/ppermute | solution.py:1129
  247.6 24.7 %collective-permute-start.33 = (bf16[1024,384]{1,0:T(8,128)(2,1)}, bf16[1024,384]{1,0:T(8,128)(2,1)S(1)}, u32[]{:S(2)}, u32[]{:S(2)}) collective-permute-start(bf16[1024,384]{1,0:T(8,128)(2,1)} %add_convert_fusion.7), channel_id=1, source_target_pairs={{0,2},{1,3},{2,0},{3,1},{4,6},{5,7},{6,4},{7,5},{8,10},{9,11},{10,... | collective-permute-start | bytes 2359304 | tf_op jit(solution)/shard_map/ppermute | solution.py:1129
  256.1 57.9 %collective-permute-start.41 = (bf16[384,1536]{1,0:T(8,128)(2,1)}, bf16[384,1536]{1,0:T(8,128)(2,1)}, u32[]{:S(2)}, u32[]{:S(2)}) collective-permute-start(bf16[384,1536]{1,0:T(8,128)(2,1)} %constant_dynamic-update-slice_fusion.2), channel_id=1, source_target_pairs={{0,4},{1,5},{2,6},{3,7},{8,12},{9,13},{10,14},{11,15},{16,20},{17,... | collective-permute-start | bytes 3538952 | tf_op jit(solution)/shard_map/ppermute | solution.py:1129
  261.8 52.2 %collective-permute-start.40 = (bf16[384,1536]{1,0:T(8,128)(2,1)}, bf16[384,1536]{1,0:T(8,128)(2,1)}, u32[]{:S(2)}, u32[]{:S(2)}) collective-permute-start(bf16[384,1536]{1,0:T(8,128)(2,1)} %get-tuple-element.237), channel_id=1, source_target_pairs={{4,0},{5,1},{6,2},{7,3},{12,8},{13,9},{14,10},{15,11},{20,16},{21,... | collective-permute-start | bytes 3538952 | tf_op jit(solution)/shard_map/ppermute | solution.py:1129
  281.6 32.5 %collective-permute-start.38 = (bf16[384,1536]{1,0:T(8,128)(2,1)S(1)}, bf16[384,1536]{1,0:T(8,128)(2,1)}, u32[]{:S(2)}, u32[]{:S(2)}) collective-permute-start(bf16[384,1536]{1,0:T(8,128)(2,1)S(1)} %add_convert_fusion.5), channel_id=1, source_target_pairs={{8,0},{9,1},{10,2},{11,3},{12,4},{13,5},{14,6},{15,7},{24,16},{25,... | collective-permute-start | bytes 3538952 | tf_op jit(solution)/shard_map/ppermute | solution.py:1129
  282.9 31.2 %collective-permute-start.39 = (bf16[384,1536]{1,0:T(8,128)(2,1)S(1)}, bf16[384,1536]{1,0:T(8,128)(2,1)}, u32[]{:S(2)}, u32[]{:S(2)}) collective-permute-start(bf16[384,1536]{1,0:T(8,128)(2,1)S(1)} %add_convert_fusion.4), channel_id=1, source_target_pairs={{8,24},{9,25},{10,26},{11,27},{12,28},{13,29},{14,30},{15,31}} | collective-permute-start | bytes 3538952 | tf_op jit(solution)/shard_map/ppermute | solution.py:1129
  284.6 29.5 %collective-permute-start.42 = (bf16[1024,384]{1,0:T(8,128)(2,1)}, bf16[1024,384]{1,0:T(8,128)(2,1)S(1)}, u32[]{:S(2)}, u32[]{:S(2)}) collective-permute-start(bf16[1024,384]{1,0:T(8,128)(2,1)} %add_convert_fusion.6), channel_id=1, source_target_pairs={{0,2},{1,3},{2,0},{3,1},{4,6},{5,7},{6,4},{7,5},{8,10},{9,11},{10,... | collective-permute-start | bytes 2359304 | tf_op jit(solution)/shard_map/ppermute | solution.py:1129
  330.6 35.8 %collective-permute-start.46 = (bf16[384,1536]{1,0:T(8,128)(2,1)}, bf16[384,1536]{1,0:T(8,128)(2,1)}, u32[]{:S(2)}, u32[]{:S(2)}) collective-permute-start(bf16[384,1536]{1,0:T(8,128)(2,1)} %add_convert_fusion.2), channel_id=1, source_target_pairs={{0,8},{1,9},{2,10},{3,11},{4,12},{5,13},{6,14},{7,15},{24,16},{25,... | collective-permute-start | bytes 3538952 | tf_op jit(solution)/shard_map/ppermute | solution.py:1129
  344.1 51.9 %collective-permute-start.43 = (bf16[384,1536]{1,0:T(8,128)(2,1)S(1)}, bf16[384,1536]{1,0:T(8,128)(2,1)}, u32[]{:S(2)}, u32[]{:S(2)}) collective-permute-start(bf16[384,1536]{1,0:T(8,128)(2,1)S(1)} %add_convert_fusion.3.refs_0_), channel_id=1, source_target_pairs={{16,0},{17,1},{18,2},{19,3},{20,4},{21,5},{22,6},{23,7}} | collective-permute-start | bytes 3538952 | tf_op jit(solution)/shard_map/ppermute | solution.py:1129
  345.4 50.7 %collective-permute-start.48 = (bf16[384,1536]{1,0:T(8,128)(2,1)S(1)}, bf16[384,1536]{1,0:T(8,128)(2,1)}, u32[]{:S(2)}, u32[]{:S(2)}) collective-permute-start(bf16[384,1536]{1,0:T(8,128)(2,1)S(1)} %add_convert_fusion.1.refs_4_), channel_id=1, source_target_pairs={{28,24},{29,25},{30,26},{31,27}} | collective-permute-start | bytes 3538952 | tf_op jit(solution)/shard_map/ppermute | solution.py:1129
  347.1 39.7 %all-to-all-start.1 = ((f32[32,8,512]{2,1,0:T(8,128)}), f32[32,8,512]{2,1,0:T(8,128)}, u32[]{:S(2)}, u32[]{:S(2)}) async-start(f32[32,8,512]{2,1,0:T(8,128)} %get-tuple-element.261), calls=%async_computation.1 | async-start | bytes 1048576 | tf_op jit(solution)/shard_map/all_to_all | solution.py:1455
  370.8 25.3 %collective-permute-start.47 = (bf16[384,1536]{1,0:T(8,128)(2,1)S(1)}, bf16[384,1536]{1,0:T(8,128)(2,1)}, u32[]{:S(2)}, u32[]{:S(2)}) collective-permute-start(bf16[384,1536]{1,0:T(8,128)(2,1)S(1)} %add_convert_fusion.refs_2_), channel_id=1, source_target_pairs={{8,16},{9,17},{10,18},{11,19},{12,20},{13,21},{14,22},{15,23}} | collective-permute-start | bytes 3538952 | tf_op jit(solution)/shard_map/ppermute | solution.py:1129
  401.5 42.5 %all-to-all-start.2 = ((bf16[32,56,384]{2,1,0:T(8,128)(2,1)}), bf16[32,56,384]{2,1,0:T(8,128)(2,1)}, u32[]{:S(2)}, u32[]{:S(2)}) async-start(bf16[32,56,384]{2,1,0:T(8,128)(2,1)} %copy-done.12), calls=%async_computation.2 | async-start | bytes 2752512 | tf_op jit(solution)/shard_map/all_to_all | solution.py:1479
  444.0 32.8 %all-to-all-start.3 = ((bf16[32,48,384]{2,1,0:T(8,128)(2,1)}), bf16[32,48,384]{2,1,0:T(8,128)(2,1)}, u32[]{:S(2)}, u32[]{:S(2)}) async-start(bf16[32,48,384]{2,1,0:T(8,128)(2,1)} %ortho_owned.1), calls=%async_computation.3 | async-start | bytes 2359296 | tf_op jit(solution)/shard_map/all_to_all | solution.py:1483
  (95 other events, 990.4 us)
Sparse Core Ops, SparseCore 0:
  34.6 101.5 all-gather.2

commit v5 on v4

--- a/solution.py
+++ b/solution.py
@@ -952,10 +952,11 @@
         cross[...] = dot(gram_high, gram_low)
         square = dot(gram_high, gram_high) + (cross[...] + cross[...].T)
         poly = halves(NS_SECOND * gram + NS_THIRD * square)
-        for k in range(4):
-            lanes = slice(k * D, k * D + D)
+        for pair in range(0, 4, 4):
+            lanes = slice(pair * D, pair * D + 4 * D)
             step = dot_three(poly, (high[:, lanes], low[:, lanes]))
-            keep(k, NS_FIRST * cur[k] + step)
+            for k in range(4):
+                keep(pair + k, NS_FIRST * cur[pair + k] + step[:, k * D : k * D + D])
         return carry
 
     lax.fori_loop(0, 5, sweep, 0)
@@ -1461,13 +1462,8 @@
     dense_side = send(dense.astype(bf), back_x)
     pieces = (held_one, last_one, held_two, last_two, held_three, cross_three)
     dense = dense + dense_side.astype(f32)
-    dense_low = dense.astype(bf)
-    for step in (1, 2, 3):
-
-        def to_second(z_, x_, y_, c_, step=step):
-            return (1, x_, y_, c_) if (z_ + step) % 4 == 1 and x_ == 0 else None
-
-        dense = dense + send(dense_low, to_second).astype(f32)
+    dense = dense + send(dense.astype(bf), along_z(pairs_two, (0,))).astype(f32)
+    dense = dense + send(dense.astype(bf), along_z(((2, 1),), (0,))).astype(f32)
 
     state_bias = MOMENTUM_VECTOR * moment_bias + g_bias
     part_sum = jnp.sum(state_bias * state_bias)

time: 497 us -> 499 us (level)
  Pallas kernels: 172 us -> 146 us
  starting transfers between devices: 92.4 us -> 111 us
  waiting for transfers between devices: 118 us -> 127 us
    pallas_call x1, Pallas kernels: 26 us -> 12 us  [attend_back_fast(): pl.pallas_call(attend_back_kernel, grid_spec=pltpu.PrefetchScalarGridSpec...]
    ppermute x53 -> x52, starting transfers between devices: 69 us -> 80.3 us  [send(): return lax.ppermute(array, AXES, route_pairs(move))]
    pallas_call x1, Pallas kernels: 23 us -> 12 us  [attend_fast(): pl.pallas_call(attend_kernel, grid_spec=pltpu.PrefetchScalarGridSpec(num_...]
    all_to_all x1, starting transfers between devices: 3.94 us -> 9.82 us  [fast_device(): moments = lax.all_to_all(moments, AXES, 0, 0, tiled=True)]
    ppermute x53 -> x52, waiting for transfers between devices: 88.2 us -> 91.2 us  [send(): return lax.ppermute(array, AXES, route_pairs(move))]
  transfers between devices with their start and end apart: 58 -> 57, of which waited for: 18 -> 23; matrix products, arithmetic and copies ran while one was open for 13% -> 13% of each run, Pallas kernels for 32% -> 27%
where the time goes in v5:
time: 499 us; the launch traced here: 493 us
  Pallas kernels  146 us (29%)
  waiting for transfers between devices  127 us (25%)
  starting transfers between devices  111 us (22%)
  other arithmetic  50.3 us (10%)
  local copies, waits for them, and re-layouts  31.2 us (6%)
  between operations  19.3 us (4%)
  matrix products  9.22 us (2%)
    ppermute x52, waiting for transfers between devices, send(): return lax.ppermute(array, AXES, route_pairs(move))  91.2 us
    ppermute x52, starting transfers between devices, send(): return lax.ppermute(array, AXES, route_pairs(move))  80.3 us
    pallas_call x1, Pallas kernels, routed_experts(): pl.pallas_call(routed_kernel, out_shape=shapes, in_specs=[pl.BlockSpec(me...  56.4 us
    pallas_call x1, Pallas kernels, shared_units(): pl.pallas_call(shared_kernel, out_shape=shapes, in_specs=[anyspec] * 9, o...  24.1 us
    pallas_call x1, Pallas kernels, ortho_owned(): pl.pallas_call(ortho_kernel, out_shape=jax.ShapeDtypeStruct((32, 48, D),...  23.7 us
    all_to_all x1, waiting for transfers between devices, fast_device(): ortho_parts = lax.all_to_all(ortho_cut, AXES, 0, 0, tiled=True)  22.1 us
    unnamed x143, local copies, waits for them, and re-layouts  22 us
    pallas_call x1, Pallas kernels, attend_back_fast(): pl.pallas_call(attend_back_kernel, grid_spec=pltpu.PrefetchScalarGridSpec...  12 us
  transfers between devices with their start and end apart: 57, of which 23 were waited for; matrix products, arithmetic and copies ran while one was open for 13% of the time, Pallas kernels for 27%

profile of v5, /device:TPU:0, one launch (start us, length us, event | category | flops | bytes accessed | tf_op | source)
XLA Modules:
  0.0 493.5 jit_solution(14174354290158100647)
XLA Ops:
  27.4 6.8 %collective-permute-done.4 = bf16[128,384]{1,0:T(8,128)(2,1)S(1)} collective-permute-done((bf16[128,384]{1,0:T(8,128)(2,1)S(1)}, bf16[128,384]{1,0:T(8,128)(2,1)S(1)}, u32[]{:S(2)}, u32[]{:S(2)}) %collective-permute-start.4) | collective-permute-done | bytes 98336 | tf_op jit(solution)/shard_map/ppermute | solution.py:1130
  42.0 8.3 %collective-permute-done.9 = bf16[4,128,384]{2,1,0:T(8,128)(2,1)S(1)} collective-permute-done((bf16[4,128,384]{2,1,0:T(8,128)(2,1)S(1)}, bf16[4,128,384]{2,1,0:T(8,128)(2,1)S(1)}, u32[]{:S(2)}, u32[]{:S(2)}) %collective-permute-start.9) | collective-permute-done | bytes 393248 | tf_op jit(solution)/shard_map/ppermute | solution.py:1130
  53.5 6.5 %collective-permute-done.11 = bf16[120,384]{1,0:T(8,128)(2,1)S(1)} collective-permute-done((bf16[120,384]{1,0:T(8,128)(2,1)S(1)}, bf16[120,384]{1,0:T(8,128)(2,1)S(1)}, u32[]{:S(2)}, u32[]{:S(2)}) %collective-permute-start.11) | collective-permute-done | bytes 92192 | tf_op jit(solution)/shard_map/ppermute | solution.py:1130
  59.9 9.3 %collective-permute-done.12 = bf16[120,384]{1,0:T(8,128)(2,1)S(1)} collective-permute-done((bf16[120,384]{1,0:T(8,128)(2,1)S(1)}, bf16[120,384]{1,0:T(8,128)(2,1)S(1)}, u32[]{:S(2)}, u32[]{:S(2)}) %collective-permute-start.12) | collective-permute-done | bytes 92192 | tf_op jit(solution)/shard_map/ppermute | solution.py:1130
  72.5 5.2 %collective-permute-done.14 = bf16[4,120,384]{2,1,0:T(8,128)(2,1)S(1)} collective-permute-done((bf16[4,120,384]{2,1,0:T(8,128)(2,1)S(1)}, bf16[4,120,384]{2,1,0:T(8,128)(2,1)S(1)}, u32[]{:S(2)}, u32[]{:S(2)}) %collective-permute-start.14) | collective-permute-done | bytes 368672 | tf_op jit(solution)/shard_map/ppermute | solution.py:1130
  89.1 12.0 %attend_fast.1 = (bf16[1024,384]{1,0:T(8,128)(2,1)S(1)}, f32[3,8,1024]{2,1,0:T(8,128)S(1)}) custom-call(s32[1]{0:T(128)S(6)} %copy.104.res, bf16[1024,1152]{1,0:T(8,128)(2,1)S(1)} %convolution_convert_fusion.q_ref.k_ref.v_ref, bf16[1024,1152]{1,0:T(8,128)(2,1)S(1)} %convolution_convert_fusion.q_ref.k_ref.v_ref, ...), custom_call_target="tpu_custom_call" | custom-call | tf_op jit(solution)/shard_map/attend_fast/pallas_call | solution.py:690
  108.5 8.7 %collective-permute-start.18 = (bf16[1024,384]{1,0:T(8,128)(2,1)}, bf16[1024,384]{1,0:T(8,128)(2,1)}, u32[]{:S(2)}, u32[]{:S(2)}) collective-permute-start(bf16[1024,384]{1,0:T(8,128)(2,1)} %fusion.11.refs_0_), channel_id=1, source_target_pairs={{0,2},{1,3},{2,0},{3,1},{4,6},{5,7},{6,4},{7,5},{8,10},{9,11},{10,... | collective-permute-start | bytes 2359304 | tf_op jit(solution)/shard_map/ppermute | solution.py:1130
  121.1 8.6 %collective-permute-done.19.refs_10_ = f32[16,1024]{1,0:T(8,128)S(1)} collective-permute-done((f32[16,1024]{1,0:T(8,128)S(1)}, f32[16,1024]{1,0:T(8,128)S(1)}, u32[]{:S(2)}, u32[]{:S(2)}) %collective-permute-start.19) | collective-permute-done | bytes 65568 | tf_op jit(solution)/shard_map/ppermute | solution.py:1130
  136.2 9.8 %all-to-all-start = ((f32[32,48,384]{2,1,0:T(8,128)}), f32[32,48,384]{2,1,0:T(8,128)}, u32[]{:S(2)}, u32[]{:S(2)}) async-start(f32[32,48,384]{2,1,0:T(8,128)} %pack_owned.1), calls=%async_computation | async-start | bytes 4718592 | tf_op jit(solution)/shard_map/all_to_all | solution.py:1340
  146.0 24.1 %shared_units.1 = (bf16[1024,768]{1,0:T(8,128)(2,1)}, bf16[1024,768]{1,0:T(8,128)(2,1)}, bf16[1024,768]{1,0:T(8,128)(2,1)}, bf16[1024,768]{1,0:T(8,128)(2,1)}, bf16[384,1536]{1,0:T(8,128)(2,1)}) custom-call(bf16[1024,384]{1,0:T(8,128)(2,1)} %fusion.11.refs_0_, bf16[1024,384]{1,0:T(8,128)(2,1)} %collective-permute-done.17.refs_1_, ...), custom_call_target="tpu_custom_call" | custom-call | tf_op jit(solution)/shard_map/shared_units/pallas_call | solution.py:633
  174.9 56.4 %routed_experts.1 = (bf16[1024,384]{1,0:T(8,128)(2,1)}, bf16[1024,384]{1,0:T(8,128)(2,1)}, bf16[1024,384]{1,0:T(8,128)(2,1)}, bf16[1024,384]{1,0:T(8,128)(2,1)},...) custom-call(s32[3]{0:T(128)} %pad_add_fusion.ids, ...), custom_call_target="tpu_custom_call" | custom-call | tf_op jit(solution)/shard_map/routed_experts/pallas_call | solution.py:603
  263.5 7.7 %collective-permute-done.36 = bf16[384,1536]{1,0:T(8,128)(2,1)} collective-permute-done((bf16[384,1536]{1,0:T(8,128)(2,1)}, bf16[384,1536]{1,0:T(8,128)(2,1)}, u32[]{:S(2)}, u32[]{:S(2)}) %collective-permute-start.36) | collective-permute-done | bytes 1179680 | tf_op jit(solution)/shard_map/ppermute | solution.py:1130
  284.9 12.0 %attend_back_fast.1 = (bf16[1024,384]{1,0:T(8,128)(2,1)S(1)}, bf16[1024,384]{1,0:T(8,128)(2,1)S(1)}, bf16[1024,384]{1,0:T(8,128)(2,1)S(1)}) custom-call(s32[1]{0:T(128)S(6)} %copy.104.res, bf16[1024,1152]{1,0:T(8,128)(2,1)S(1)} %convolution_convert_fusion.q_ref.k_ref.v_ref, bf16[1024,1152]{1,0:T(8,128)(2,1)S(1)} %convolution_convert_fusion.q_ref.k_ref.v_ref, ...), custom_call_target="tpu_custom_call" | custom-call | tf_op jit(solution)/shard_map/attend_back_fast/pallas_call | solution.py:772
  302.3 7.2 %collective-permute-done.38 = bf16[384,1536]{1,0:T(8,128)(2,1)} collective-permute-done((bf16[384,1536]{1,0:T(8,128)(2,1)S(1)}, bf16[384,1536]{1,0:T(8,128)(2,1)}, u32[]{:S(2)}, u32[]{:S(2)}) %collective-permute-start.38) | collective-permute-done | bytes 1179680 | tf_op jit(solution)/shard_map/ppermute | solution.py:1130
  317.3 7.5 %first_back.1 = (f32[1024,384]{1,0:T(8,128)}, f32[2,384,384]{2,1,0:T(8,128)S(1)}, bf16[2,384,384]{2,1,0:T(8,128)(2,1)}, f32[32,8,512]{2,1,0:T(8,128)}) custom-call(s32[3]{0:T(128)S(1)} %copy-done.24, bf16[1024,384]{1,0:T(8,128)(2,1)S(1)} %get-tuple-element.248.dq, bf16[1024,384]{1,0:T(8,128)(2,1)S(1)} %get-tuple-element.249.dk, ...), custom_call_target="tpu_custom_call" | custom-call | tf_op jit(solution)/shard_map/first_back/pallas_call | solution.py:1089
  325.8 14.0 %collective-permute-start.46 = (bf16[384,1536]{1,0:T(8,128)(2,1)}, bf16[384,1536]{1,0:T(8,128)(2,1)}, u32[]{:S(2)}, u32[]{:S(2)}) collective-permute-start(bf16[384,1536]{1,0:T(8,128)(2,1)} %add_convert_fusion.2), channel_id=1, source_target_pairs={{0,8},{1,9},{2,10},{3,11},{4,12},{5,13},{6,14},{7,15},{24,16},{25,... | collective-permute-start | bytes 3538952 | tf_op jit(solution)/shard_map/ppermute | solution.py:1130
  346.5 6.9 %all-to-all-start.1 = ((f32[32,8,512]{2,1,0:T(8,128)}), f32[32,8,512]{2,1,0:T(8,128)}, u32[]{:S(2)}, u32[]{:S(2)}) async-start(f32[32,8,512]{2,1,0:T(8,128)} %get-tuple-element.261), calls=%async_computation.1 | async-start | bytes 1048576 | tf_op jit(solution)/shard_map/all_to_all | solution.py:1456
  353.4 11.9 %collective-permute-done.46 = bf16[384,1536]{1,0:T(8,128)(2,1)} collective-permute-done((bf16[384,1536]{1,0:T(8,128)(2,1)}, bf16[384,1536]{1,0:T(8,128)(2,1)}, u32[]{:S(2)}, u32[]{:S(2)}) %collective-permute-start.46) | collective-permute-done | bytes 1179680 | tf_op jit(solution)/shard_map/ppermute | solution.py:1130
  371.4 5.4 %collective-permute-done.49 = bf16[384,384]{1,0:T(8,128)(2,1)S(1)} collective-permute-done((bf16[384,384]{1,0:T(8,128)(2,1)S(1)}, bf16[384,384]{1,0:T(8,128)(2,1)S(1)}, u32[]{:S(2)}, u32[]{:S(2)}) %collective-permute-start.49) | collective-permute-done | bytes 294944 | tf_op jit(solution)/shard_map/ppermute | solution.py:1130
  378.7 5.5 %collective-permute-start.50 = (bf16[384,384]{1,0:T(8,128)(2,1)}, bf16[384,384]{1,0:T(8,128)(2,1)}, u32[]{:S(2)}, u32[]{:S(2)}) collective-permute-start(bf16[384,384]{1,0:T(8,128)(2,1)} %fusion.15), channel_id=1, source_target_pairs={{0,8},{1,9},{2,10},{3,11},{24,16},{25,17},{26,18},{27,19}} | collective-permute-start | bytes 884744 | tf_op jit(solution)/shard_map/ppermute | solution.py:1130
  402.8 10.1 %all-to-all-start.2 = ((bf16[32,56,384]{2,1,0:T(8,128)(2,1)}), bf16[32,56,384]{2,1,0:T(8,128)(2,1)}, u32[]{:S(2)}, u32[]{:S(2)}) async-start(bf16[32,56,384]{2,1,0:T(8,128)(2,1)} %copy-done.12), calls=%async_computation.2 | async-start | bytes 2752512 | tf_op jit(solution)/shard_map/all_to_all | solution.py:1475
  412.9 23.7 %ortho_owned.1 = bf16[32,48,384]{2,1,0:T(8,128)(2,1)} custom-call(s32[3]{0:T(128)S(1)} %copy-done.24, f32[4,384,384]{2,1,0:T(8,128)S(1)} %copy-done.11, f32[32,48,384]{2,1,0:T(8,128)} %all-to-all-done.moment), custom_call_target="tpu_custom_call" | custom-call | tf_op jit(solution)/shard_map/ortho_owned/pallas_call | solution.py:970
  436.6 9.6 %all-to-all-done.2.grads = bf16[32,56,384]{2,1,0:T(8,128)(2,1)} async-done(((bf16[32,56,384]{2,1,0:T(8,128)(2,1)}), bf16[32,56,384]{2,1,0:T(8,128)(2,1)}, u32[]{:S(2)}, u32[]{:S(2)}) %all-to-all-start.2) | async-done | bytes 1376288 | tf_op jit(solution)/shard_map/all_to_all | solution.py:1475
  456.9 22.1 %all-to-all-done.3.orthos = bf16[32,48,384]{2,1,0:T(8,128)(2,1)} async-done(((bf16[32,48,384]{2,1,0:T(8,128)(2,1)}), bf16[32,48,384]{2,1,0:T(8,128)(2,1)}, u32[]{:S(2)}, u32[]{:S(2)}) %all-to-all-start.3) | async-done | bytes 1179680 | tf_op jit(solution)/shard_map/all_to_all | solution.py:1479
  (376 shorter events, 174.9 us)
Async XLA Ops:
  7.2 129.0 %all-gather.3.cloned.1.call-start = ((), (), s32[]{:S(2)}) async-start(), calls=%async_computation.4 | async-start | bytes 6635520 | tf_op jit(solution)/shard_map/all_gather | solution.py:1262
  50.3 18.9 %collective-permute-start.12 = (bf16[120,384]{1,0:T(8,128)(2,1)S(1)}, bf16[120,384]{1,0:T(8,128)(2,1)S(1)}, u32[]{:S(2)}, u32[]{:S(2)}) collective-permute-start(bf16[120,384]{1,0:T(8,128)(2,1)S(1)} %bitcast.282), channel_id=1, source_target_pairs={{0,16},{1,17},{2,18},{3,19},{4,20},{5,21},{6,22},{7,23},{8,24},{9,... | collective-permute-start | bytes 276488 | tf_op jit(solution)/shard_map/ppermute | solution.py:1130
  53.4 25.4 %collective-permute-start.10 = (bf16[4,2,128,384]{3,2,0,1:T(8,128)(2,1)S(1)}, bf16[4,2,128,384]{3,2,0,1:T(8,128)(2,1)S(1)}, u32[]{:S(2)}, u32[]{:S(2)}) collective-permute-start(bf16[4,2,128,384]{3,2,0,1:T(8,128)(2,1)S(1)} %pad_maximum_fusion.1), channel_id=1, source_target_pairs={{0,1},{1,0},{2,3},{3,2},{4,5},{5,4},{6,7},{7,6},{8,9},{9,8},{10,11... | collective-permute-start | bytes 2359304 | tf_op jit(solution)/shard_map/ppermute | solution.py:1130
  84.3 19.7 %collective-permute-start.16 = (bf16[1024,384]{1,0:T(8,128)(2,1)S(1)}, bf16[1024,384]{1,0:T(8,128)(2,1)S(1)}, u32[]{:S(2)}, u32[]{:S(2)}) collective-permute-start(bf16[1024,384]{1,0:T(8,128)(2,1)S(1)} %fusion.7.refs_4_), channel_id=1, source_target_pairs={{0,2},{1,3},{2,0},{3,1},{4,6},{5,7},{6,4},{7,5},{8,10},{9,11},{10,... | collective-permute-start | bytes 2359304 | tf_op jit(solution)/shard_map/ppermute | solution.py:1130
  108.5 21.9 %collective-permute-start.18 = (bf16[1024,384]{1,0:T(8,128)(2,1)}, bf16[1024,384]{1,0:T(8,128)(2,1)}, u32[]{:S(2)}, u32[]{:S(2)}) collective-permute-start(bf16[1024,384]{1,0:T(8,128)(2,1)} %fusion.11.refs_0_), channel_id=1, source_target_pairs={{0,2},{1,3},{2,0},{3,1},{4,6},{5,7},{6,4},{7,5},{8,10},{9,11},{10,... | collective-permute-start | bytes 2359304 | tf_op jit(solution)/shard_map/ppermute | solution.py:1130
  136.2 95.2 %all-to-all-start = ((f32[32,48,384]{2,1,0:T(8,128)}), f32[32,48,384]{2,1,0:T(8,128)}, u32[]{:S(2)}, u32[]{:S(2)}) async-start(f32[32,48,384]{2,1,0:T(8,128)} %pack_owned.1), calls=%async_computation | async-start | bytes 4718592 | tf_op jit(solution)/shard_map/all_to_all | solution.py:1340
  172.3 59.1 %collective-permute-start.25 = (bf16[384,384]{1,0:T(8,128)(2,1)S(1)}, bf16[384,384]{1,0:T(8,128)(2,1)}, u32[]{:S(2)}, u32[]{:S(2)}) collective-permute-start(bf16[384,384]{1,0:T(8,128)(2,1)S(1)} %get-tuple-element.303), channel_id=1, source_target_pairs={{0,1},{1,0},{2,3},{3,2},{4,5},{5,4},{6,7},{7,6},{8,9},{9,8},{10,11... | collective-permute-start | bytes 884744 | tf_op jit(solution)/shard_map/ppermute | solution.py:1130
  172.7 58.7 %collective-permute-start.26 = (bf16[384,384]{1,0:T(8,128)(2,1)S(1)}, bf16[384,384]{1,0:T(8,128)(2,1)}, u32[]{:S(2)}, u32[]{:S(2)}) collective-permute-start(bf16[384,384]{1,0:T(8,128)(2,1)S(1)} %get-tuple-element.302), channel_id=1, source_target_pairs={{0,2},{1,3},{2,0},{3,1},{4,6},{5,7},{6,4},{7,5},{8,10},{9,11},{10,... | collective-permute-start | bytes 884744 | tf_op jit(solution)/shard_map/ppermute | solution.py:1130
  174.3 57.1 %collective-permute-start.27 = (bf16[384,384]{1,0:T(8,128)(2,1)S(1)}, bf16[384,384]{1,0:T(8,128)(2,1)}, u32[]{:S(2)}, u32[]{:S(2)}) collective-permute-start(bf16[384,384]{1,0:T(8,128)(2,1)S(1)} %get-tuple-element.301), channel_id=1, source_target_pairs={{0,3},{1,2},{2,1},{3,0},{4,7},{5,6},{6,5},{7,4},{8,11},{9,10},{10,... | collective-permute-start | bytes 884744 | tf_op jit(solution)/shard_map/ppermute | solution.py:1130
  232.0 31.4 %collective-permute-start.37 = (bf16[384,1536]{1,0:T(8,128)(2,1)}, bf16[384,1536]{1,0:T(8,128)(2,1)}, u32[]{:S(2)}, u32[]{:S(2)}) collective-permute-start(bf16[384,1536]{1,0:T(8,128)(2,1)} %get-tuple-element.213), channel_id=1, source_target_pairs={{0,8},{1,9},{2,10},{3,11},{4,12},{5,13},{6,14},{7,15},{16,24},{17,... | collective-permute-start | bytes 3538952 | tf_op jit(solution)/shard_map/ppermute | solution.py:1130
  242.1 29.1 %collective-permute-start.36 = (bf16[384,1536]{1,0:T(8,128)(2,1)}, bf16[384,1536]{1,0:T(8,128)(2,1)}, u32[]{:S(2)}, u32[]{:S(2)}) collective-permute-start(bf16[384,1536]{1,0:T(8,128)(2,1)} %get-tuple-element.212), channel_id=1, source_target_pairs={{0,4},{1,5},{2,6},{3,7},{4,0},{5,1},{6,2},{7,3},{8,12},{9,13},{10,... | collective-permute-start | bytes 3538952 | tf_op jit(solution)/shard_map/ppermute | solution.py:1130
  246.5 24.7 %collective-permute-start.33 = (bf16[1024,384]{1,0:T(8,128)(2,1)}, bf16[1024,384]{1,0:T(8,128)(2,1)S(1)}, u32[]{:S(2)}, u32[]{:S(2)}) collective-permute-start(bf16[1024,384]{1,0:T(8,128)(2,1)} %add_convert_fusion.7), channel_id=1, source_target_pairs={{0,2},{1,3},{2,0},{3,1},{4,6},{5,7},{6,4},{7,5},{8,10},{9,11},{10,... | collective-permute-start | bytes 2359304 | tf_op jit(solution)/shard_map/ppermute | solution.py:1130
  255.0 43.9 %collective-permute-start.41 = (bf16[384,1536]{1,0:T(8,128)(2,1)}, bf16[384,1536]{1,0:T(8,128)(2,1)}, u32[]{:S(2)}, u32[]{:S(2)}) collective-permute-start(bf16[384,1536]{1,0:T(8,128)(2,1)} %constant_dynamic-update-slice_fusion.2), channel_id=1, source_target_pairs={{0,4},{1,5},{2,6},{3,7},{8,12},{9,13},{10,14},{11,15},{16,20},{17,... | collective-permute-start | bytes 3538952 | tf_op jit(solution)/shard_map/ppermute | solution.py:1130
  260.7 38.2 %collective-permute-start.40 = (bf16[384,1536]{1,0:T(8,128)(2,1)}, bf16[384,1536]{1,0:T(8,128)(2,1)}, u32[]{:S(2)}, u32[]{:S(2)}) collective-permute-start(bf16[384,1536]{1,0:T(8,128)(2,1)} %get-tuple-element.237), channel_id=1, source_target_pairs={{4,0},{5,1},{6,2},{7,3},{12,8},{13,9},{14,10},{15,11},{20,16},{21,... | collective-permute-start | bytes 3538952 | tf_op jit(solution)/shard_map/ppermute | solution.py:1130
  280.5 29.0 %collective-permute-start.38 = (bf16[384,1536]{1,0:T(8,128)(2,1)S(1)}, bf16[384,1536]{1,0:T(8,128)(2,1)}, u32[]{:S(2)}, u32[]{:S(2)}) collective-permute-start(bf16[384,1536]{1,0:T(8,128)(2,1)S(1)} %add_convert_fusion.5), channel_id=1, source_target_pairs={{8,0},{9,1},{10,2},{11,3},{12,4},{13,5},{14,6},{15,7},{24,16},{25,... | collective-permute-start | bytes 3538952 | tf_op jit(solution)/shard_map/ppermute | solution.py:1130
  281.8 27.7 %collective-permute-start.39 = (bf16[384,1536]{1,0:T(8,128)(2,1)S(1)}, bf16[384,1536]{1,0:T(8,128)(2,1)}, u32[]{:S(2)}, u32[]{:S(2)}) collective-permute-start(bf16[384,1536]{1,0:T(8,128)(2,1)S(1)} %add_convert_fusion.4), channel_id=1, source_target_pairs={{8,24},{9,25},{10,26},{11,27},{12,28},{13,29},{14,30},{15,31}} | collective-permute-start | bytes 3538952 | tf_op jit(solution)/shard_map/ppermute | solution.py:1130
  283.5 18.8 %collective-permute-start.42 = (bf16[1024,384]{1,0:T(8,128)(2,1)}, bf16[1024,384]{1,0:T(8,128)(2,1)S(1)}, u32[]{:S(2)}, u32[]{:S(2)}) collective-permute-start(bf16[1024,384]{1,0:T(8,128)(2,1)} %add_convert_fusion.6), channel_id=1, source_target_pairs={{0,2},{1,3},{2,0},{3,1},{4,6},{5,7},{6,4},{7,5},{8,10},{9,11},{10,... | collective-permute-start | bytes 2359304 | tf_op jit(solution)/shard_map/ppermute | solution.py:1130
  325.8 39.5 %collective-permute-start.46 = (bf16[384,1536]{1,0:T(8,128)(2,1)}, bf16[384,1536]{1,0:T(8,128)(2,1)}, u32[]{:S(2)}, u32[]{:S(2)}) collective-permute-start(bf16[384,1536]{1,0:T(8,128)(2,1)} %add_convert_fusion.2), channel_id=1, source_target_pairs={{0,8},{1,9},{2,10},{3,11},{4,12},{5,13},{6,14},{7,15},{24,16},{25,... | collective-permute-start | bytes 3538952 | tf_op jit(solution)/shard_map/ppermute | solution.py:1130
  343.5 53.8 %collective-permute-start.43 = (bf16[384,1536]{1,0:T(8,128)(2,1)S(1)}, bf16[384,1536]{1,0:T(8,128)(2,1)}, u32[]{:S(2)}, u32[]{:S(2)}) collective-permute-start(bf16[384,1536]{1,0:T(8,128)(2,1)S(1)} %add_convert_fusion.3.refs_0_), channel_id=1, source_target_pairs={{16,0},{17,1},{18,2},{19,3},{20,4},{21,5},{22,6},{23,7}} | collective-permute-start | bytes 3538952 | tf_op jit(solution)/shard_map/ppermute | solution.py:1130
  344.8 52.5 %collective-permute-start.48 = (bf16[384,1536]{1,0:T(8,128)(2,1)S(1)}, bf16[384,1536]{1,0:T(8,128)(2,1)}, u32[]{:S(2)}, u32[]{:S(2)}) collective-permute-start(bf16[384,1536]{1,0:T(8,128)(2,1)S(1)} %add_convert_fusion.1.refs_4_), channel_id=1, source_target_pairs={{28,24},{29,25},{30,26},{31,27}} | collective-permute-start | bytes 3538952 | tf_op jit(solution)/shard_map/ppermute | solution.py:1130
  346.5 40.0 %all-to-all-start.1 = ((f32[32,8,512]{2,1,0:T(8,128)}), f32[32,8,512]{2,1,0:T(8,128)}, u32[]{:S(2)}, u32[]{:S(2)}) async-start(f32[32,8,512]{2,1,0:T(8,128)} %get-tuple-element.261), calls=%async_computation.1 | async-start | bytes 1048576 | tf_op jit(solution)/shard_map/all_to_all | solution.py:1456
  369.7 27.6 %collective-permute-start.47 = (bf16[384,1536]{1,0:T(8,128)(2,1)S(1)}, bf16[384,1536]{1,0:T(8,128)(2,1)}, u32[]{:S(2)}, u32[]{:S(2)}) collective-permute-start(bf16[384,1536]{1,0:T(8,128)(2,1)S(1)} %add_convert_fusion.refs_2_), channel_id=1, source_target_pairs={{8,16},{9,17},{10,18},{11,19},{12,20},{13,21},{14,22},{15,23}} | collective-permute-start | bytes 3538952 | tf_op jit(solution)/shard_map/ppermute | solution.py:1130
  402.8 43.4 %all-to-all-start.2 = ((bf16[32,56,384]{2,1,0:T(8,128)(2,1)}), bf16[32,56,384]{2,1,0:T(8,128)(2,1)}, u32[]{:S(2)}, u32[]{:S(2)}) async-start(bf16[32,56,384]{2,1,0:T(8,128)(2,1)} %copy-done.12), calls=%async_computation.2 | async-start | bytes 2752512 | tf_op jit(solution)/shard_map/all_to_all | solution.py:1475
  446.2 32.8 %all-to-all-start.3 = ((bf16[32,48,384]{2,1,0:T(8,128)(2,1)}), bf16[32,48,384]{2,1,0:T(8,128)(2,1)}, u32[]{:S(2)}, u32[]{:S(2)}) async-start(bf16[32,48,384]{2,1,0:T(8,128)(2,1)} %ortho_owned.1), calls=%async_computation.3 | async-start | bytes 2359296 | tf_op jit(solution)/shard_map/all_to_all | solution.py:1479
  (94 other events, 944.7 us)
Sparse Core Ops, SparseCore 0:
  34.6 101.5 all-gather.2
